TPU v7x, 32 devices: a whole 2x2x4 slice. The times are simulated.
32 devices in a mesh: groups: 2 (over y), tensor: 16 (over z, x, core).
Axes of the slice: x: 2, y: 2, z: 4, core: 2. Of those that a mesh axis runs over, the one named last changes fastest.
Arguments:
- inputs: bfloat16 [256, 8192], P('groups', 'tensor'), parts along dimension 0, may hold values from -6 to 6
- gate_weight: bfloat16 [8192, 28672], P(None, 'tensor'), may hold values from -0.09375 to 0.09375
- up_weight: bfloat16 [8192, 28672], P(None, 'tensor'), may hold values from -0.09375 to 0.09375
- down_weight: bfloat16 [28672, 8192], P('tensor'), may hold values from -0.03125 to 0.03125
- cotangent: bfloat16 [4, 256, 8192], P(None, 'groups', 'tensor'), parts along dimension 1, may hold values from -6 to 6
- threshold_levels: int32 [28672], P('tensor'), may hold values from 4 to 16
- membrane_offsets: int32 [256, 28672], P('groups', 'tensor'), parts along dimension 0, may hold values from 0 to 255
Outputs:
- grad_input: float32 [256, 8192], P('groups', 'tensor'), parts along dimension 0
- grad_threshold: float32 [57344], P(('groups', 'tensor')), parts along dimension 0
There are 2 independent parts, one for each index of `groups`. A program takes and returns all parts, laid end to end along the dimension named above; an argument that names none is the same for every part. Nothing has to cross between parts.
All inputs are finite; a program needn't handle non-finite values.
Results may differ from a plain program's by a relative error of at most 0.0031.
Values may be sent and summed in bfloat16 or wider, within the bound.
No kernel may reach another device: no remote copies, remote signals or barrier semaphores. Data moves between devices by JAX's collectives and lax.ppermute only.
A program may use at most 256 MiB of HBM per device.

v0:
```python
import jax
import jax.numpy as jnp
from jax import lax
from jax.sharding import PartitionSpec as P

slope_gain = 4.0


def transposed_product(left, weight):
    return lax.dot_general(
        left, weight, (((1,), (1,)), ((), ())), preferred_element_type=jnp.float32
    )


def body(
    inputs, gate_weight, up_weight, down_weight, cotangent, threshold_levels, membrane_offsets
):
    step_count = cotangent.shape[0]
    piece = lax.all_gather(inputs, "tensor", axis=1, tiled=True)
    gate = jnp.dot(piece, gate_weight, preferred_element_type=jnp.float32)
    up = jnp.dot(piece, up_weight, preferred_element_type=jnp.float32)
    feedback_all = jnp.einsum(
        "tkd,fd->tkf",
        lax.all_gather(cotangent, "tensor", axis=2, tiled=True),
        down_weight,
        preferred_element_type=jnp.float32,
    )
    theta = threshold_levels.astype(jnp.float32) / 8.0
    sig = jax.nn.sigmoid(gate)
    current = gate * sig * up
    dsilu = sig * (1.0 + gate * (1.0 - sig))
    offset_share = membrane_offsets.astype(jnp.float32) / 256.0
    membrane = theta * offset_share
    spikes = []
    for step in range(step_count):
        pre = membrane + current
        spike = jax.nn.sigmoid(slope_gain * (pre - theta))
        spikes.append(spike)
        membrane = pre - theta * spike
    later = jnp.zeros_like(current)
    grad_threshold = jnp.zeros(theta.shape, jnp.float32)
    collected = []
    for step in range(step_count - 1, -1, -1):
        feedback = feedback_all[step]
        spike = spikes[step]
        dspike = theta * (feedback - later)
        slope = slope_gain * spike * (1.0 - spike)
        dpre = dspike * slope + later
        grad_threshold = grad_threshold + jnp.sum(
            feedback * spike - later * spike - dspike * slope, axis=0
        )
        dgate = (dpre * up * dsilu).astype(jnp.bfloat16)
        dup = (dpre * gate * sig).astype(jnp.bfloat16)
        term = transposed_product(dgate, gate_weight) + transposed_product(dup, up_weight)
        collected.append(lax.psum_scatter(term, "tensor", scatter_dimension=1, tiled=True))
        later = dpre
    grad_threshold = grad_threshold + jnp.sum(later * offset_share, axis=0)
    grad_input = collected[0]
    for part_sum in collected[1:]:
        grad_input = grad_input + part_sum
    return (grad_input, grad_threshold)


def solution(mesh):
    placed = (
        P("groups", "tensor"),
        P(None, "tensor"),
        P(None, "tensor"),
        P("tensor", None),
        P(None, "groups", "tensor"),
        P("tensor"),
        P("groups", "tensor"),
    )
    return jax.shard_map(
        body,
        mesh=mesh,
        in_specs=placed,
        out_specs=(P("groups", "tensor"), P(("groups", "tensor"))),
        check_vma=False,
    )
```

profile of v0, /device:TPU:0, one launch (start us, length us, event | category | flops | bytes accessed | tf_op | source)
XLA Modules:
  0.0 368.1 jit_solution(3617723521399008605)
XLA Ops:
  7.2 0.0 all-gather.5.cloned.1.call-start
  7.2 0.7 all-gather.5.cloned.1.call-update
  7.9 0.0 all-gather.3.cloned.1.call-start
  7.9 0.7 all-gather.3.cloned.1.call-update
  8.6 0.0 reduce-scatter.2.cloned.1.call-start
  8.7 0.7 convert_multiply_fusion
  9.4 0.0 copy-start.3
  9.4 44.7 %all-gather.5.cloned.1.call-done = bf16[128,8192]{1,0:T(8,128)(2,1)} async-done(((bf16[128,512]{1,0:T(8,128)(2,1)}), bf16[128,8192]{1,0:T(8,128)(2,1)}) %all-gather.5.cloned.1.call-update) | async-done | bytes 2097168 | tf_op jit(solution)/shard_map/all_gather | solution.py:19
  54.1 0.0 copy-start.2
  54.1 14.8 %fusion.19 = f32[128,1792]{1,0:T(8,128)S(1)} fusion(bf16[128,8192]{1,0:T(8,128)(2,1)} %all-gather.5.cloned.1.call-done, bf16[8192,1792]{1,0:T(8,128)(2,1)} %param.8), kind=kOutput, calls=%fused_computation.54 | convolution fusion | flops 3758096384 | bytes 32374784 | tf_op jit(solution)/shard_map/dot_general | solution.py:20
  68.9 0.0 copy-done.3
  68.9 0.0 copy-done.2
  68.9 15.9 %add_divide_fusion = (f32[128,1792]{1,0:T(8,128)}, f32[128,1792]{1,0:T(8,128)}, f32[128,1792]{1,0:T(8,128)S(1)}) fusion(f32[1792]{0:T(1024)S(1)} %get-tuple-element.14, f32[1792]{0:T(1024)S(1)} %get-tuple-element.13, s32[128,1792]{1,0:T(8,128)S(1)} %copy-done.3, f32[128,1792]{1,0:T(8,128)S(1)} %fusion.19, bf16[128,8192]{1,0:T(8,128)(2,1)S(1)} %copy-done.2, ...), kind=kOutput, calls=%fused_computation.34 | convolution fusion | flops 3766583296 | bytes 36059136 | tf_op jit(solution)/shard_map/dot_general | solution.py:21
  84.8 48.5 %all-gather.3.cloned.1.call-done = bf16[4,128,8192]{2,1,0:T(8,128)(2,1)} async-done(((bf16[4,128,512]{2,1,0:T(8,128)(2,1)}), bf16[4,128,8192]{2,1,0:T(8,128)(2,1)}) %all-gather.3.cloned.1.call-update) | async-done | bytes 8388624 | tf_op jit(solution)/shard_map/all_gather | solution.py:24
  133.3 23.0 %fusion = f32[4,128,1792]{2,1,0:T(8,128)} fusion(bf16[4,128,8192]{2,1,0:T(8,128)(2,1)} %all-gather.3.cloned.1.call-done, bf16[1792,8192]{1,0:T(8,128)(2,1)} %param.10), kind=kOutput, calls=%fused_computation | convolution fusion | flops 15032385536 | bytes 41418752 | tf_op jit(solution)/shard_map/tkd,fd->tkf/dot_general | solution.py:22
  156.3 0.0 copy-done.4
  156.3 0.0 copy-done.5
  156.3 0.0 copy-done.6
  156.3 4.8 %subtract_reduce_fusion.2 = (f32[1792]{0:T(1024)S(1)}, f32[1792]{0:T(1024)S(1)}, f32[1792]{0:T(1024)S(1)}, f32[1792]{0:T(1024)S(1)}, f32[1792]{0:T(1024)S(1)}, /...) fusion(f32[4,128,1792]{2,1,0:T(8,128)} %fusion, ...), kind=kLoop, calls=%fused_computation.16 | loop fusion | flops 16735488 | bytes 10142720 | tf_op jit(solution)/shard_map/reduce_sum | solution.py:49
  161.0 1.0 copy-done
  162.0 14.3 %fusion.11 = f32[128,8192]{1,0:T(8,128)S(1)} fusion(bf16[8192,1792]{1,0:T(8,128)(2,1)} %param.8, f32[128,1792]{1,0:T(8,128)S(1)} %get-tuple-element.7, f32[128,1792]{1,0:T(8,128)S(1)} %get-tuple-element.15, f32[128,1792]{1,0:T(8,128)S(1)} %fusion.19), kind=kOutput, calls=%fused_computation.46 | convolution fusion | flops 3760390144 | bytes 36306944 | tf_op jit(solution)/shard_map/dot_general | solution.py:10
  176.3 15.9 %convolution_add_fusion = f32[128,8192]{1,0:T(8,128)} fusion(f32[128,8192]{1,0:T(8,128)S(1)} %fusion.11, bf16[8192,1792]{1,0:T(8,128)(2,1)} %param.9, f32[128,1792]{1,0:T(8,128)} %copy-done, f32[128,1792]{1,0:T(8,128)S(1)} %fusion.19), kind=kOutput, calls=%fused_computation.2 | convolution fusion | flops 3760521216 | bytes 39583744 | tf_op jit(solution)/shard_map/dot_general | solution.py:10
  192.2 14.4 %fusion.10 = f32[128,8192]{1,0:T(8,128)S(1)} fusion(bf16[8192,1792]{1,0:T(8,128)(2,1)} %param.8, f32[128,1792]{1,0:T(8,128)} %get-tuple-element.8, f32[128,1792]{1,0:T(8,128)S(1)} %get-tuple-element.15, f32[128,1792]{1,0:T(8,128)S(1)} %fusion.19), kind=kOutput, calls=%fused_computation.45 | convolution fusion | flops 3760390144 | bytes 36306944 | tf_op jit(solution)/shard_map/dot_general | solution.py:10
  206.7 16.0 %convolution_add_fusion.1 = f32[128,8192]{1,0:T(8,128)} fusion(f32[128,8192]{1,0:T(8,128)S(1)} %fusion.10, bf16[8192,1792]{1,0:T(8,128)(2,1)} %param.9, f32[128,1792]{1,0:T(8,128)} %get-tuple-element.8, f32[128,1792]{1,0:T(8,128)S(1)} %fusion.19), kind=kOutput, calls=%fused_computation.3 | convolution fusion | flops 3760521216 | bytes 39583744 | tf_op jit(solution)/shard_map/dot_general | solution.py:10
  222.6 14.2 %fusion.9 = f32[128,8192]{1,0:T(8,128)S(1)} fusion(bf16[8192,1792]{1,0:T(8,128)(2,1)} %param.8, f32[128,1792]{1,0:T(8,128)S(1)} %get-tuple-element.9, f32[128,1792]{1,0:T(8,128)S(1)} %get-tuple-element.15, f32[128,1792]{1,0:T(8,128)S(1)} %fusion.19), kind=kOutput, calls=%fused_computation.44 | convolution fusion | flops 3760390144 | bytes 36306944 | tf_op jit(solution)/shard_map/dot_general | solution.py:10
  236.9 16.7 %convolution_add_fusion.2 = f32[128,8192]{1,0:T(8,128)} fusion(f32[128,8192]{1,0:T(8,128)S(1)} %fusion.9, bf16[8192,1792]{1,0:T(8,128)(2,1)} %param.9, f32[128,1792]{1,0:T(8,128)S(1)} %get-tuple-element.9, f32[128,1792]{1,0:T(8,128)S(1)} %fusion.19), kind=kOutput, calls=%fused_computation.4 | convolution fusion | flops 3760521216 | bytes 39583744 | tf_op jit(solution)/shard_map/dot_general | solution.py:10
  253.6 18.2 %fusion.8 = f32[128,8192]{1,0:T(8,128)} fusion(bf16[8192,1792]{1,0:T(8,128)(2,1)} %param.8, f32[128,1792]{1,0:T(8,128)} %get-tuple-element.10, f32[128,1792]{1,0:T(8,128)S(1)} %get-tuple-element.15, f32[128,1792]{1,0:T(8,128)S(1)} %fusion.19), kind=kOutput, calls=%fused_computation.43 | convolution fusion | flops 3760390144 | bytes 36306944 | tf_op jit(solution)/shard_map/dot_general | solution.py:10
  271.7 0.0 copy-done.1
  271.7 19.2 %fusion.4 = f32[128,8192]{1,0:T(8,128)} fusion(f32[128,8192]{1,0:T(8,128)} %convolution_add_fusion, f32[128,8192]{1,0:T(8,128)} %convolution_add_fusion.1, f32[128,8192]{1,0:T(8,128)} %convolution_add_fusion.2, f32[128,8192]{1,0:T(8,128)} %fusion.8, bf16[8192,1792]{1,0:T(8,128)(2,1)} %param.9, f32[128,1792]{1,0:T(8,128)S(1)} %copy-done.1, ...), kind=kOutput, calls=%fused_computation.8 | convolution fusion | flops 3763666944 | bytes 52166656 | tf_op jit(solution)/shard_map/dot_general | solution.py:10
  290.9 0.0 reduce-scatter.2.cloned.1.call-update
  291.0 0.6 add_add_fusion
  291.6 70.0 %reduce-scatter.2.cloned.1.call-done = f32[128,512]{1,0:T(8,128)} async-done(((f32[128,8192]{1,0:T(8,128)}), f32[128,512]{1,0:T(8,128)}) %reduce-scatter.2.cloned.1.call-update) | async-done | bytes 262160 | tf_op jit(solution)/shard_map/reduce_scatter | solution.py:55
  (5 shorter events, 0.0 us)
Async XLA Ops:
  7.2 46.9 %all-gather.5.cloned.1.call-start = ((), (), s32[]{:S(2)}) async-start(), calls=%async_computation.2 | async-start | bytes 2228224 | tf_op jit(solution)/shard_map/all_gather | solution.py:19
  7.9 125.4 %all-gather.3.cloned.1.call-start = ((), (), s32[]{:S(2)}) async-start(), calls=%async_computation.1 | async-start | bytes 8912896 | tf_op jit(solution)/shard_map/all_gather | solution.py:24
  8.6 353.0 %reduce-scatter.2.cloned.1.call-start = ((), (), s32[]{:S(2)}) async-start(), calls=%async_computation.3 | async-start | bytes 4456448 | tf_op jit(solution)/shard_map/reduce_scatter | solution.py:55
  9.4 59.5 %copy-start.3 = (s32[128,1792]{1,0:T(8,128)S(1)}, s32[128,1792]{1,0:T(8,128)}, u32[]{:S(2)}) copy-start(s32[128,1792]{1,0:T(8,128)} %param.13) | copy-start | bytes 2752516
  54.1 14.8 %copy-start.2 = (bf16[128,8192]{1,0:T(8,128)(2,1)S(1)}, bf16[128,8192]{1,0:T(8,128)(2,1)}, u32[]{:S(2)}) copy-start(bf16[128,8192]{1,0:T(8,128)(2,1)} %all-gather.5.cloned.1.call-done) | copy-start | bytes 6291460
  133.3 23.0 %copy-start.4 = (s32[128,1792]{1,0:T(8,128)S(1)}, s32[128,1792]{1,0:T(8,128)}, u32[]{:S(2)}) copy-start(s32[128,1792]{1,0:T(8,128)} %param.13) | copy-start | bytes 2752516
  133.3 23.0 %copy-start.5 = (f32[128,1792]{1,0:T(8,128)S(1)}, f32[128,1792]{1,0:T(8,128)}, u32[]{:S(2)}) copy-start(f32[128,1792]{1,0:T(8,128)} %get-tuple-element.11) | copy-start | bytes 2752516
  133.3 23.0 %copy-start.6 = (f32[128,1792]{1,0:T(8,128)S(1)}, f32[128,1792]{1,0:T(8,128)}, u32[]{:S(2)}) copy-start(f32[128,1792]{1,0:T(8,128)} %get-tuple-element.12) | copy-start | bytes 2752516
  161.0 1.0 copy-start
  253.6 18.2 %copy-start.1 = (f32[128,1792]{1,0:T(8,128)S(1)}, f32[128,1792]{1,0:T(8,128)}, u32[]{:S(2)}) copy-start(f32[128,1792]{1,0:T(8,128)} %get-tuple-element.10) | copy-start | bytes 2752516
Sparse Core Ops, SparseCore 0:
  10.2 43.8 all-gather.4
  56.2 77.0 all-gather.2
  291.1 70.4 reduce-scatter.1
where the time goes:
time: 369 us; the launch traced here: 368 us
  matrix products  183 us (50%)
  waiting for transfers between devices  165 us (45%)
  between operations  13.8 us (4%)
  other arithmetic  6.08 us (2%)
    dot_general x8, matrix products, transposed_product(): lax.dot_general(left, weight, (((1,), (1,)), ((), ())), preferred_element...  129 us
    reduce_scatter x1, waiting for transfers between devices, body(): lax.psum_scatter(term, 'tensor', scatter_dimension=1, tiled=True)  70 us
    all_gather x1, waiting for transfers between devices, body(): lax.all_gather(cotangent, 'tensor', axis=2, tiled=True)  48.5 us
    all_gather x1, waiting for transfers between devices, body(): piece = lax.all_gather(inputs, 'tensor', axis=1, tiled=True)  44.7 us
    dot_general x1, matrix products, body(): jnp.einsum('tkd,fd->tkf', lax.all_gather(cotangent, 'tensor', axis=2, til...  23 us
    dot_general x1, matrix products, body(): up = jnp.dot(piece, up_weight, preferred_element_type=jnp.float32)  15.9 us
    dot_general x1, matrix products, body(): gate = jnp.dot(piece, gate_weight, preferred_element_type=jnp.float32)  14.8 us
  transfers between devices with their start and end apart: 3, of which 3 were waited for; matrix products, arithmetic and copies ran while one was open for 9% of the time, Pallas kernels for 0%

commit v1 on v0

v1 whole, which is shorter than its diff:
```python
import jax
import jax.numpy as jnp
from jax import lax
from jax.experimental import pallas as pl
from jax.experimental.pallas import tpu as pltpu
from jax.sharding import PartitionSpec as P

slope_gain = 4.0
AXIS = "tensor"
NT = (((1,), (1,)), ((), ()))
F32 = jnp.float32
BF16 = jnp.bfloat16
VMEM_LIMIT = 48 << 20


def nt_dot(left, weight):
    return lax.dot_general(left, weight, NT, preferred_element_type=F32)


def dot(left, right):
    return jnp.dot(left, right, preferred_element_type=F32)


def forward_call(tok, pairs, blocks, gate_w, up_w, down_w, sums):
    count = len(pairs)
    rows, width = pairs[0][0].shape
    hidden = gate_w.shape[1]
    first = sums is None
    pieces = [piece for pair in pairs for piece in pair]

    def kernel(blk, *refs):
        data = refs[: 2 * count]
        ga, gb, ua, ub, da, db = refs[2 * count : 2 * count + 6]
        rest = refs[2 * count + 6 :]
        gate, up, feed = rest[-3:]
        at = pl.program_id(0)
        for j in range(count):

            @pl.when(at == j)
            def _(j=j):
                own, other = data[2 * j], data[2 * j + 1]
                fresh = first and j == 0
                xo = own[rows - tok :, :]
                xp = other[rows - tok :, :]
                g = dot(xo, ga[...]) + dot(xp, gb[...])
                u = dot(xo, ua[...]) + dot(xp, ub[...])
                if fresh:
                    gate[...] = g
                    up[...] = u
                elif j == 0:
                    gate[...] = rest[0][...] + g
                    up[...] = rest[1][...] + u
                else:
                    gate[...] += g
                    up[...] += u
                f = nt_dot(own[: rows - tok, :], da[...]) + nt_dot(other[: rows - tok, :], db[...])
                if fresh:
                    feed[...] = f
                elif j == 0:
                    feed[...] = rest[2][...] + f
                else:
                    feed[...] += f

    whole = lambda shape: pl.BlockSpec(shape, lambda j, b: (0, 0))
    spec = lambda k: pl.BlockSpec((width, hidden), lambda j, b: (b[k, j], 0))
    dspec = lambda k: pl.BlockSpec((hidden, width), lambda j, b: (0, b[k, j]))
    sum_shapes = [(tok, hidden), (tok, hidden), (rows - tok, hidden)]
    in_specs = [whole((rows, width)) for _ in pieces]
    in_specs += [spec(0), spec(1), spec(0), spec(1), dspec(0), dspec(1)]
    args = pieces + [gate_w, gate_w, up_w, up_w, down_w, down_w]
    aliases = {}
    if not first:
        aliases = {1 + len(args) + k: k for k in range(3)}
        in_specs += [whole(s) for s in sum_shapes]
        args += list(sums)
    return pl.pallas_call(
        kernel,
        grid_spec=pltpu.PrefetchScalarGridSpec(
            num_scalar_prefetch=1,
            grid=(count,),
            in_specs=in_specs,
            out_specs=[whole(s) for s in sum_shapes],
        ),
        out_shape=[jax.ShapeDtypeStruct(s, F32) for s in sum_shapes],
        input_output_aliases=aliases,
        compiler_params=pltpu.CompilerParams(vmem_limit_bytes=VMEM_LIMIT),
        cost_estimate=pl.CostEstimate(
            flops=2 * count * 2 * width * hidden * (rows + tok),
            transcendentals=0,
            bytes_accessed=2 * count * width * (6 * hidden + 2 * rows),
        ),
        name="forward",
    )(blocks, *args)


def neuron_call(gate, up, feed, levels, offsets):
    tok, hidden = gate.shape
    steps = feed.shape[0] // tok
    part = 256 if hidden % 256 == 0 else hidden
    tile = 16

    def kernel(gate_ref, up_ref, feed_ref, lev_ref, off_ref, dg_ref, du_ref, gt_ref):
        theta = jnp.broadcast_to(lev_ref[...].astype(F32) / 8.0, (tile, part))

        def step_rows(r, acc):
            at = pl.ds(pl.multiple_of(r * tile, tile), tile)
            g = gate_ref[at, :]
            u = up_ref[at, :]
            sig = jax.nn.sigmoid(g)
            gs = g * sig
            current = gs * u
            dsilu = sig * (1.0 + g * (1.0 - sig))
            share = off_ref[at, :].astype(F32) / 256.0
            membrane = theta * share
            spikes = []
            for _ in range(steps):
                pre = membrane + current
                spike = jax.nn.sigmoid(slope_gain * (pre - theta))
                spikes.append(spike)
                membrane = pre - theta * spike
            later = jnp.zeros_like(current)
            usl = u * dsilu
            dgate = jnp.zeros_like(current)
            dup = jnp.zeros_like(current)
            for t in range(steps - 1, -1, -1):
                fb = feed_ref[pl.ds(pl.multiple_of(t * tok + r * tile, tile), tile), :]
                spike = spikes[t]
                diff = fb - later
                slope = slope_gain * spike * (1.0 - spike)
                both = theta * diff * slope
                dpre = both + later
                acc = acc + (diff * spike - both)
                dgate = dgate + (dpre * usl).astype(BF16).astype(F32)
                dup = dup + (dpre * gs).astype(BF16).astype(F32)
                later = dpre
            dg_ref[at, :] = dgate.astype(BF16)
            du_ref[at, :] = dup.astype(BF16)
            return acc + later * share

        acc = lax.fori_loop(0, tok // tile, step_rows, jnp.zeros((tile, part), F32))
        gt_ref[...] = jnp.sum(acc, axis=0, keepdims=True)

    col = lambda rows: pl.BlockSpec((rows, part), lambda s: (0, s))
    return pl.pallas_call(
        kernel,
        grid=(hidden // part,),
        in_specs=[col(tok), col(tok), col(steps * tok), col(1), col(tok)],
        out_specs=[col(tok), col(tok), col(1)],
        out_shape=[
            jax.ShapeDtypeStruct((tok, hidden), BF16),
            jax.ShapeDtypeStruct((tok, hidden), BF16),
            jax.ShapeDtypeStruct((1, hidden), F32),
        ],
        cost_estimate=pl.CostEstimate(
            flops=120 * tok * hidden, transcendentals=10 * tok * hidden, bytes_accessed=32 * tok * hidden
        ),
        name="neuron",
    )(gate, up, feed, levels.reshape(1, hidden), offsets)


def backward_call(dgate, dup, blocks, count, gate_w, up_w, width):
    tok, hidden = dgate.shape

    def kernel(blk, dg, du, ga, gb, ua, ub, own, other):
        own[0] = nt_dot(dg[...], ga[...]) + nt_dot(du[...], ua[...])
        other[0] = nt_dot(dg[...], gb[...]) + nt_dot(du[...], ub[...])

    whole = pl.BlockSpec((tok, hidden), lambda j, b: (0, 0))
    spec = lambda k: pl.BlockSpec((width, hidden), lambda j, b: (b[k, j], 0))
    out = pl.BlockSpec((1, tok, width), lambda j, b: (j, 0, 0))
    return pl.pallas_call(
        kernel,
        grid_spec=pltpu.PrefetchScalarGridSpec(
            num_scalar_prefetch=1,
            grid=(count,),
            in_specs=[whole, whole, spec(0), spec(1), spec(0), spec(1)],
            out_specs=[out, out],
        ),
        out_shape=[jax.ShapeDtypeStruct((count, tok, width), F32)] * 2,
        compiler_params=pltpu.CompilerParams(vmem_limit_bytes=VMEM_LIMIT),
        cost_estimate=pl.CostEstimate(
            flops=count * 8 * width * hidden * tok,
            transcendentals=0,
            bytes_accessed=count * width * (8 * hidden + 8 * tok),
        ),
        name="backward",
    )(blocks, dgate, dup, gate_w, gate_w, up_w, up_w)


def z_map(moves):
    return [(i, moves[i // 4] * 4 + i % 4) for i in range(16) if i // 4 in moves]


CORE = [(i, i ^ 1) for i in range(16)]
PAIR = z_map({0: 1, 1: 0, 2: 3, 3: 2})
MID = z_map({1: 2, 2: 1})
OUT = z_map({1: 0, 2: 3})
CROSS = [(i, i ^ 2) for i in range(16)]


def around(turn, flip):
    return [(i, ((i // 4 + turn) % 4 * 4 + i % 4) ^ (2 * flip)) for i in range(16)]


def send(piece, moves):
    return lax.ppermute(piece, AXIS, moves)


fence = lax.optimization_barrier


def body_line(inputs, gate_w, up_w, down_w, cotangent, levels, offsets):
    steps, tok, width = cotangent.shape
    me = lax.axis_index(AXIS)
    core = me % 2
    chip = me // 2
    z = me // 4
    middle = (z == 1) | (z == 2)

    def blocks_of(chips):
        chips = jnp.stack(chips).astype(jnp.int32)
        return jnp.stack([2 * chips + core, 2 * chips + 1 - core]).astype(jnp.int32)

    far_a = jnp.where(middle, 6, 4)
    far_b = jnp.where(middle, 4, 6)

    own = jnp.concatenate([cotangent.reshape(steps * tok, width), inputs], axis=0)
    x0 = send(own, CROSS)
    p1 = send(own, PAIR)
    p2a = send(own, MID)
    own_c = send(own, CORE)
    sums = forward_call(tok, [(own, own_c)], blocks_of([chip]), gate_w, up_w, down_w, None)
    x0, p1, p2a = fence((x0, p1, p2a))
    x1 = send(p1, CROSS)
    p2b = send(p1, MID)
    p3a = send(p2a, OUT)
    x0_c = send(x0, CORE)
    p1_c = send(p1, CORE)
    sums = forward_call(
        tok, [(x0, x0_c), (p1, p1_c)], blocks_of([chip ^ 1, chip ^ 2]), gate_w, up_w, down_w, sums
    )
    x1, p2b, p3a = fence((x1, p2b, p3a))
    a = jnp.where(middle, p2a, p3a)
    x2 = send(a, CROSS)
    p3b = send(p2b, OUT)
    x1_c = send(x1, CORE)
    a_c = send(a, CORE)
    sums = forward_call(
        tok, [(x1, x1_c), (a, a_c)], blocks_of([chip ^ 3, chip ^ far_a]), gate_w, up_w, down_w, sums
    )
    x2, p3b = fence((x2, p3b))
    b = jnp.where(middle, p2b, p3b)
    x3 = send(b, CROSS)
    x2_c = send(x2, CORE)
    b_c = send(b, CORE)
    sums = forward_call(
        tok, [(x2, x2_c), (b, b_c)], blocks_of([chip ^ 1 ^ far_a, chip ^ far_b]), gate_w, up_w, down_w, sums
    )
    x3_c = send(x3, CORE)
    sums = forward_call(tok, [(x3, x3_c)], blocks_of([chip ^ 1 ^ far_b]), gate_w, up_w, down_w, sums)

    dgate, dup, grad_threshold = neuron_call(*sums, levels, offsets)

    def dest(turn, flip):
        return ((z + turn) % 4 * 2 + chip % 2) ^ flip

    turns = [2, 1, 3]
    other_col = [dest(t, 1) for t in turns + [0]]
    mine1, theirs1 = backward_call(dgate, dup, blocks_of(other_col), 4, gate_w, up_w, width)
    got1 = send(theirs1, CORE)
    own_col = [dest(t, 0) for t in turns]
    mine2, theirs2 = backward_call(dgate, dup, blocks_of(own_col), 3, gate_w, up_w, width)
    got2 = send(theirs2, CORE)
    sum1 = (mine1 + got1).astype(BF16)
    parts = [send(sum1[k], around(t, 1)) for k, t in enumerate(turns + [0])]
    mine3, theirs3 = backward_call(dgate, dup, blocks_of([chip]), 1, gate_w, up_w, width)
    got3 = send(theirs3, CORE)
    sum2 = (mine2 + got2).astype(BF16)
    parts += [send(sum2[k], around(t, 0)) for k, t in enumerate(turns)]
    grad_input = mine3[0] + got3[0]
    for part in parts:
        grad_input = grad_input + part.astype(F32)
    return grad_input, grad_threshold.reshape(-1)


def body_plain(inputs, gate_w, up_w, down_w, cotangent, levels, offsets):
    steps, tok, width = cotangent.shape
    piece = lax.all_gather(inputs, AXIS, axis=1, tiled=True)
    gate = dot(piece, gate_w)
    up = dot(piece, up_w)
    cot = lax.all_gather(cotangent, AXIS, axis=2, tiled=True)
    feed = nt_dot(cot.reshape(steps * tok, -1), down_w)
    dgate, dup, grad_threshold = neuron_call(gate, up, feed, levels, offsets)
    term = nt_dot(dgate, gate_w) + nt_dot(dup, up_w)
    grad_input = lax.psum_scatter(term, AXIS, scatter_dimension=1, tiled=True)
    return grad_input, grad_threshold.reshape(-1)


def solution(mesh):
    placed = (
        P("groups", "tensor"),
        P(None, "tensor"),
        P(None, "tensor"),
        P("tensor", None),
        P(None, "groups", "tensor"),
        P("tensor"),
        P("groups", "tensor"),
    )
    body = body_line if mesh.shape[AXIS] == 16 else body_plain
    return jax.shard_map(
        body,
        mesh=mesh,
        in_specs=placed,
        out_specs=(P("groups", "tensor"), P(("groups", "tensor"))),
        check_vma=False,
    )
```

time: 369 us -> 206 us (0.56)
  matrix products: 183 us -> 0 us
  Pallas kernels: 0 us -> 109 us
  waiting for transfers between devices: 165 us -> 62.6 us
  starting transfers between devices: 0.11 us -> 21.7 us
  between operations: 13.8 us -> 1 us
  local copies, waits for them, and re-layouts: 1.01 us -> 7.24 us
    dot_general x11 -> x0, matrix products: 183 us -> none  [the longest x8 129 us: transposed_product(): lax.dot_general(left, weight, (((1,), (1,)), ((), ())), preferred_element...]
    pallas_call x0 -> x9, Pallas kernels: none -> 109 us  [the longest x5 67.2 us: forward_call(): pl.pallas_call(kernel, grid_spec=pltpu.PrefetchScalarGridSpec(num_scalar_...]
    all_gather x2 -> x0, waiting for transfers between devices: 93.2 us -> none  [the longest x1 48.5 us: body(): lax.all_gather(cotangent, 'tensor', axis=2, tiled=True)]
    reduce_scatter x1 -> x0, waiting for transfers between devices: 70 us -> none  [body(): lax.psum_scatter(term, 'tensor', scatter_dimension=1, tiled=True)]
    ppermute x0 -> x27, waiting for transfers between devices: none -> 62.6 us  [send(): return lax.ppermute(piece, AXIS, moves)]
    ppermute x0 -> x27, starting transfers between devices: none -> 21.7 us  [send(): return lax.ppermute(piece, AXIS, moves)]
    unnamed x14 -> x20, local copies, waits for them, and re-layouts: 1.01 us -> 5.88 us
    reduce_sum x1 -> x0, other arithmetic: 4.77 us -> none  [body(): jnp.sum(feedback * spike - later * spike - dspike * slope, axis=0)]
  transfers between devices with their start and end apart: 3 -> 27, of which waited for: 3 -> 9; matrix products, arithmetic and copies ran while one was open for 9% -> 2% of each run, Pallas kernels for 0% -> 37%
where the time goes in v1:
time: 206 us
  Pallas kernels  109 us (53%)
  waiting for transfers between devices  62.6 us (30%)
  starting transfers between devices  21.7 us (11%)
  local copies, waits for them, and re-layouts  7.24 us (4%)
  other arithmetic  4.79 us (2%)
    pallas_call x5, Pallas kernels, forward_call(): pl.pallas_call(kernel, grid_spec=pltpu.PrefetchScalarGridSpec(num_scalar_...  67.2 us
    ppermute x27, waiting for transfers between devices, send(): return lax.ppermute(piece, AXIS, moves)  62.6 us
    pallas_call x3, Pallas kernels, backward_call(): pl.pallas_call(kernel, grid_spec=pltpu.PrefetchScalarGridSpec(num_scalar_...  32.7 us
    ppermute x27, starting transfers between devices, send(): return lax.ppermute(piece, AXIS, moves)  21.7 us
    pallas_call x1, Pallas kernels, neuron_call(): pl.pallas_call(kernel, grid=(hidden // part,), in_specs=[col(tok), col(to...  8.65 us
    unnamed x20, local copies, waits for them, and re-layouts  5.88 us
  transfers between devices with their start and end apart: 27, of which 9 were waited for; matrix products, arithmetic and copies ran while one was open for 2% of the time, Pallas kernels for 37%

profile of v1, /device:TPU:0, one launch (start us, length us, event | category | flops | bytes accessed | tf_op | source)
XLA Modules:
  0.0 205.9 jit_solution(14228026303452834011)
XLA Ops:
  0.6 1.2 pad_maximum_fusion.refs_0_
  1.8 3.0 %collective-permute-start = (bf16[640,512]{1,0:T(8,128)(2,1)S(1)}, bf16[640,512]{1,0:T(8,128)(2,1)}, u32[]{:S(2)}, u32[]{:S(2)}) collective-permute-start(bf16[640,512]{1,0:T(8,128)(2,1)S(1)} %pad_maximum_fusion.refs_0_), channel_id=1, source_target_pairs={{0,2},{1,3},{2,0},{3,1},{4,6},{5,7},{6,4},{7,5},{8,10},{9,11},{10,... | collective-permute-start | bytes 1966088 | tf_op jit(solution)/shard_map/ppermute | solution.py:206
  4.8 1.6 collective-permute-start.1
  7.5 12.2 %collective-permute-done.refs_0_ = bf16[640,512]{1,0:T(8,128)(2,1)} collective-permute-done((bf16[640,512]{1,0:T(8,128)(2,1)S(1)}, bf16[640,512]{1,0:T(8,128)(2,1)}, u32[]{:S(2)}, u32[]{:S(2)}) %collective-permute-start) | collective-permute-done | bytes 655392 | tf_op jit(solution)/shard_map/ppermute | solution.py:206
  19.6 1.5 collective-permute-done.1.refs_2_
  21.5 1.5 collective-permute-start.4
  23.0 1.3 collective-permute-start.5
  24.5 12.2 %collective-permute-done.3.refs_0_ = bf16[640,512]{1,0:T(8,128)(2,1)} collective-permute-done((bf16[640,512]{1,0:T(8,128)(2,1)}, bf16[640,512]{1,0:T(8,128)(2,1)}, u32[]{:S(2)}, u32[]{:S(2)}) %collective-permute-start.3) | collective-permute-done | bytes 655392 | tf_op jit(solution)/shard_map/ppermute | solution.py:206
  36.7 7.0 %collective-permute-done.5 = bf16[640,512]{1,0:T(8,128)(2,1)S(1)} collective-permute-done((bf16[640,512]{1,0:T(8,128)(2,1)S(1)}, bf16[640,512]{1,0:T(8,128)(2,1)S(1)}, u32[]{:S(2)}, u32[]{:S(2)}) %collective-permute-start.5) | collective-permute-done | bytes 655392 | tf_op jit(solution)/shard_map/ppermute | solution.py:206
  43.8 1.6 collective-permute-start.6
  45.4 1.3 collective-permute-start.7
  47.3 1.3 reshape.365.lev_ref
  48.6 9.1 %collective-permute-done.6.refs_0_ = bf16[640,512]{1,0:T(8,128)(2,1)S(1)} collective-permute-done((bf16[640,512]{1,0:T(8,128)(2,1)S(1)}, bf16[640,512]{1,0:T(8,128)(2,1)S(1)}, u32[]{:S(2)}, u32[]{:S(2)}) %collective-permute-start.6) | collective-permute-done | bytes 655392 | tf_op jit(solution)/shard_map/ppermute | solution.py:206
  57.7 3.4 %collective-permute-done.7 = bf16[640,512]{1,0:T(8,128)(2,1)} collective-permute-done((bf16[640,512]{1,0:T(8,128)(2,1)}, bf16[640,512]{1,0:T(8,128)(2,1)}, u32[]{:S(2)}, u32[]{:S(2)}) %collective-permute-start.7) | collective-permute-done | bytes 655392 | tf_op jit(solution)/shard_map/ppermute | solution.py:206
  61.1 1.2 broadcast_select_fusion.refs_2_
  63.6 1.1 copy-done.6
  64.7 9.7 %forward.5 = (f32[128,1792]{1,0:T(8,128)S(1)}, f32[128,1792]{1,0:T(8,128)S(1)}, f32[512,1792]{1,0:T(8,128)}) custom-call(s32[2,1]{1,0:T(2,128)S(1)} %pad_add_fusion.blk, bf16[640,512]{1,0:T(8,128)(2,1)S(1)} %pad_maximum_fusion.refs_0_, bf16[640,512]{1,0:T(8,128)(2,1)S(1)} %copy-done.6, bf16[8192,1792]{1,0:T(8,128)(2,1)} %gb.5, bf16[8192,1792]{1,0:T(8,128)(2,1)} %gb.5, ...), custom_call_target="tpu_custom_call" | custom-call | flops 2818572288 | bytes 12320768 | tf_op jit(solution)/shard_map/forward/pallas_call | solution.py:76
  74.9 15.3 %forward.6 = (f32[128,1792]{1,0:T(8,128)S(1)}, f32[128,1792]{1,0:T(8,128)S(1)}, f32[512,1792]{1,0:T(8,128)}) custom-call(s32[2,2]{1,0:T(2,128)S(1)} %pad_add_fusion.4.blk, bf16[640,512]{1,0:T(8,128)(2,1)} %collective-permute-done.refs_0_, ...), custom_call_target="tpu_custom_call", output_to_operand_aliasing={{0}: (11, {}), {1}: (12, {}), {2}: (13, {})} | custom-call | flops 5637144576 | bytes 24641536 | tf_op jit(solution)/shard_map/forward/pallas_call | solution.py:76
  90.6 15.5 %forward.7 = (f32[128,1792]{1,0:T(8,128)S(1)}, f32[128,1792]{1,0:T(8,128)S(1)}, f32[512,1792]{1,0:T(8,128)}) custom-call(s32[2,2]{1,0:T(2,128)S(1)} %pad_add_fusion.3.blk, bf16[640,512]{1,0:T(8,128)(2,1)} %collective-permute-done.3.refs_0_, ...), custom_call_target="tpu_custom_call", output_to_operand_aliasing={{0}: (11, {}), {1}: (12, {}), {2}: (13, {})} | custom-call | flops 5637144576 | bytes 24641536 | tf_op jit(solution)/shard_map/forward/pallas_call | solution.py:76
  106.1 15.7 %forward.8 = (f32[128,1792]{1,0:T(8,128)S(1)}, f32[128,1792]{1,0:T(8,128)S(1)}, f32[512,1792]{1,0:T(8,128)}) custom-call(s32[2,2]{1,0:T(2,128)S(1)} %pad_add_fusion.2.blk, bf16[640,512]{1,0:T(8,128)(2,1)S(1)} %copy-done.8, bf16[640,512]{1,0:T(8,128)(2,1)S(1)} %collective-permute-done.10.refs_1_, ...), custom_call_target="tpu_custom_call", output_to_operand_aliasing={{0}: (11, {}), {1}: (12, {}), {2}: (13, {})} | custom-call | flops 5637144576 | bytes 24641536 | tf_op jit(solution)/shard_map/forward/pallas_call | solution.py:76
  121.7 11.1 %forward.9 = (f32[128,1792]{1,0:T(8,128)S(1)}, f32[128,1792]{1,0:T(8,128)S(1)}, f32[512,1792]{1,0:T(8,128)}) custom-call(s32[2,1]{1,0:T(2,128)S(1)} %pad_add_fusion.1.blk, bf16[640,512]{1,0:T(8,128)(2,1)S(1)} %collective-permute-done.8.refs_0_, ...), custom_call_target="tpu_custom_call", output_to_operand_aliasing={{0}: (9, {}), {1}: (10, {}), {2}: (11, {})} | custom-call | flops 2818572288 | bytes 12320768 | tf_op jit(solution)/shard_map/forward/pallas_call | solution.py:76
  134.7 8.6 %neuron.1 = (bf16[128,1792]{1,0:T(8,128)(2,1)}, bf16[128,1792]{1,0:T(8,128)(2,1)}, f32[1,1792]{1,0:T(1,128)}) custom-call(f32[128,1792]{1,0:T(8,128)} %copy-done, f32[128,1792]{1,0:T(8,128)} %copy-done.1, f32[512,1792]{1,0:T(8,128)} %get-tuple-element.56.feed_ref, s32[1,1792]{1,0:T(1,128)} %reshape.365.lev_ref, s32[128,1792]{1,0:T(8,128)} %off_ref.1), custom_call_target="tpu_custom_call" | custom-call | flops 27525120 | bytes 7340032 | tf_op jit(solution)/shard_map/neuron/pallas_call | solution.py:144
  145.3 11.9 %backward.5 = (f32[3,128,512]{2,1,0:T(8,128)S(1)}, f32[3,128,512]{2,1,0:T(8,128)S(1)}) custom-call(s32[2,3]{1,0:T(2,128)S(1)} %pad_add_fusion.6.blk, bf16[128,1792]{1,0:T(8,128)(2,1)S(1)} %copy-done.2, bf16[128,1792]{1,0:T(8,128)(2,1)S(1)} %copy-done.4, bf16[8192,1792]{1,0:T(8,128)(2,1)} %gb.5, bf16[8192,1792]{1,0:T(8,128)(2,1)} %gb.5, ...), custom_call_target="tpu_custom_call" | custom-call | flops 2818572288 | bytes 23592960 | tf_op jit(solution)/shard_map/backward/pallas_call | solution.py:171
  157.5 14.7 %backward.4 = (f32[4,128,512]{2,1,0:T(8,128)S(1)}, f32[4,128,512]{2,1,0:T(8,128)S(1)}) custom-call(s32[2,4]{1,0:T(2,128)S(1)} %pad_add_fusion.5.blk, bf16[128,1792]{1,0:T(8,128)(2,1)S(1)} %copy-done.2, bf16[128,1792]{1,0:T(8,128)(2,1)S(1)} %copy-done.4, bf16[8192,1792]{1,0:T(8,128)(2,1)} %gb.5, bf16[8192,1792]{1,0:T(8,128)(2,1)} %gb.5, ...), custom_call_target="tpu_custom_call" | custom-call | flops 3758096384 | bytes 31457280 | tf_op jit(solution)/shard_map/backward/pallas_call | solution.py:171
  172.6 6.1 %backward.3 = (f32[1,128,512]{2,1,0:T(8,128)S(1)}, f32[1,128,512]{2,1,0:T(8,128)S(1)}) custom-call(s32[2,1]{1,0:T(2,128)S(1)} %pad_add_fusion.blk, bf16[128,1792]{1,0:T(8,128)(2,1)S(1)} %copy-done.3, bf16[128,1792]{1,0:T(8,128)(2,1)S(1)} %copy-done.4, bf16[8192,1792]{1,0:T(8,128)(2,1)} %gb.5, bf16[8192,1792]{1,0:T(8,128)(2,1)} %gb.5, bf16[8192,1792]{1,0:T(8,128)(2,1)} %ub.5, ...), custom_call_target="tpu_custom_call" | custom-call | flops 939524096 | bytes 7864320 | tf_op jit(solution)/shard_map/backward/pallas_call | solution.py:171
  179.4 2.5 %collective-permute-start.25 = (bf16[128,512]{1,0:T(8,128)(2,1)S(1)}, bf16[128,512]{1,0:T(8,128)(2,1)S(1)}, u32[]{:S(2)}, u32[]{:S(2)}) collective-permute-start(bf16[128,512]{1,0:T(8,128)(2,1)S(1)} %get-tuple-element.76), channel_id=1, source_target_pairs={{0,4},{1,5},{2,6},{3,7},{4,8},{5,9},{6,10},{7,11},{8,12},{9,13},{1... | collective-permute-start | bytes 393224 | tf_op jit(solution)/shard_map/ppermute | solution.py:206
  181.8 1.4 collective-permute-start.26
  183.6 2.1 %collective-permute-start.19 = (bf16[128,512]{1,0:T(8,128)(2,1)S(1)}, bf16[128,512]{1,0:T(8,128)(2,1)S(1)}, u32[]{:S(2)}, u32[]{:S(2)}) collective-permute-start(bf16[128,512]{1,0:T(8,128)(2,1)S(1)} %get-tuple-element.70), channel_id=1, source_target_pairs={{0,10},{1,11},{2,8},{3,9},{4,14},{5,15},{6,12},{7,13},{8,2},{9,3},... | collective-permute-start | bytes 393224 | tf_op jit(solution)/shard_map/ppermute | solution.py:206
  185.6 5.7 %collective-permute-done.24 = bf16[128,512]{1,0:T(8,128)(2,1)S(1)} collective-permute-done((bf16[128,512]{1,0:T(8,128)(2,1)S(1)}, bf16[128,512]{1,0:T(8,128)(2,1)S(1)}, u32[]{:S(2)}, u32[]{:S(2)}) %collective-permute-start.24) | collective-permute-done | bytes 131104 | tf_op jit(solution)/shard_map/ppermute | solution.py:206
  191.3 1.5 collective-permute-start.22
  193.5 9.5 %collective-permute-done.19 = bf16[128,512]{1,0:T(8,128)(2,1)S(1)} collective-permute-done((bf16[128,512]{1,0:T(8,128)(2,1)S(1)}, bf16[128,512]{1,0:T(8,128)(2,1)S(1)}, u32[]{:S(2)}, u32[]{:S(2)}) %collective-permute-start.19) | collective-permute-done | bytes 131104 | tf_op jit(solution)/shard_map/ppermute | solution.py:206
  202.9 2.1 %collective-permute-done.22 = bf16[128,512]{1,0:T(8,128)(2,1)S(1)} collective-permute-done((bf16[128,512]{1,0:T(8,128)(2,1)S(1)}, bf16[128,512]{1,0:T(8,128)(2,1)S(1)}, u32[]{:S(2)}, u32[]{:S(2)}) %collective-permute-start.22) | collective-permute-done | bytes 131104 | tf_op jit(solution)/shard_map/ppermute | solution.py:206
  (75 shorter events, 11.5 us)
Async XLA Ops:
  1.8 17.8 %collective-permute-start = (bf16[640,512]{1,0:T(8,128)(2,1)S(1)}, bf16[640,512]{1,0:T(8,128)(2,1)}, u32[]{:S(2)}, u32[]{:S(2)}) collective-permute-start(bf16[640,512]{1,0:T(8,128)(2,1)S(1)} %pad_maximum_fusion.refs_0_), channel_id=1, source_target_pairs={{0,2},{1,3},{2,0},{3,1},{4,6},{5,7},{6,4},{7,5},{8,10},{9,11},{10,... | collective-permute-start | bytes 1966088 | tf_op jit(solution)/shard_map/ppermute | solution.py:206
  4.8 16.3 %collective-permute-start.1 = (bf16[640,512]{1,0:T(8,128)(2,1)S(1)}, bf16[640,512]{1,0:T(8,128)(2,1)}, u32[]{:S(2)}, u32[]{:S(2)}) collective-permute-start(bf16[640,512]{1,0:T(8,128)(2,1)S(1)} %pad_maximum_fusion.refs_0_), channel_id=1, source_target_pairs={{0,4},{1,5},{2,6},{3,7},{4,0},{5,1},{6,2},{7,3},{8,12},{9,13},{10,... | collective-permute-start | bytes 1966088 | tf_op jit(solution)/shard_map/ppermute | solution.py:206
  6.4 14.7 %collective-permute-start.2 = (bf16[640,512]{1,0:T(8,128)(2,1)S(1)}, bf16[640,512]{1,0:T(8,128)(2,1)S(1)}, u32[]{:S(2)}, u32[]{:S(2)}) collective-permute-start(bf16[640,512]{1,0:T(8,128)(2,1)S(1)} %pad_maximum_fusion.refs_0_), channel_id=1, source_target_pairs={{4,8},{5,9},{6,10},{7,11},{8,4},{9,5},{10,6},{11,7},{20,24},{21,25... | collective-permute-start | bytes 1966088 | tf_op jit(solution)/shard_map/ppermute | solution.py:206
  7.1 55.2 %collective-permute-start.16 = (bf16[640,512]{1,0:T(8,128)(2,1)S(1)}, bf16[640,512]{1,0:T(8,128)(2,1)S(1)}, u32[]{:S(2)}, u32[]{:S(2)}) collective-permute-start(bf16[640,512]{1,0:T(8,128)(2,1)S(1)} %pad_maximum_fusion.refs_0_), channel_id=1, source_target_pairs={{0,1},{1,0},{2,3},{3,2},{4,5},{5,4},{6,7},{7,6},{8,9},{9,8},{10,11... | collective-permute-start | bytes 1966088 | tf_op jit(solution)/shard_map/ppermute | solution.py:206
  21.1 15.6 %collective-permute-start.3 = (bf16[640,512]{1,0:T(8,128)(2,1)}, bf16[640,512]{1,0:T(8,128)(2,1)}, u32[]{:S(2)}, u32[]{:S(2)}) collective-permute-start(bf16[640,512]{1,0:T(8,128)(2,1)} %collective-permute-done.1.refs_2_), channel_id=1, source_target_pairs={{0,2},{1,3},{2,0},{3,1},{4,6},{5,7},{6,4},{7,5},{8,10},{9,11},{10,... | collective-permute-start | bytes 1966088 | tf_op jit(solution)/shard_map/ppermute | solution.py:206
  21.5 15.2 %collective-permute-start.4 = (bf16[640,512]{1,0:T(8,128)(2,1)}, bf16[640,512]{1,0:T(8,128)(2,1)}, u32[]{:S(2)}, u32[]{:S(2)}) collective-permute-start(bf16[640,512]{1,0:T(8,128)(2,1)} %collective-permute-done.1.refs_2_), channel_id=1, source_target_pairs={{4,8},{5,9},{6,10},{7,11},{8,4},{9,5},{10,6},{11,7},{20,24},{21,25... | collective-permute-start | bytes 1966088 | tf_op jit(solution)/shard_map/ppermute | solution.py:206
  23.0 20.7 %collective-permute-start.5 = (bf16[640,512]{1,0:T(8,128)(2,1)S(1)}, bf16[640,512]{1,0:T(8,128)(2,1)S(1)}, u32[]{:S(2)}, u32[]{:S(2)}) collective-permute-start(bf16[640,512]{1,0:T(8,128)(2,1)S(1)} %collective-permute-done.2), channel_id=1, source_target_pairs={{4,0},{5,1},{6,2},{7,3},{8,12},{9,13},{10,14},{11,15},{20,16},{21,... | collective-permute-start | bytes 1966088 | tf_op jit(solution)/shard_map/ppermute | solution.py:206
  43.8 13.8 %collective-permute-start.6 = (bf16[640,512]{1,0:T(8,128)(2,1)S(1)}, bf16[640,512]{1,0:T(8,128)(2,1)S(1)}, u32[]{:S(2)}, u32[]{:S(2)}) collective-permute-start(bf16[640,512]{1,0:T(8,128)(2,1)S(1)} %broadcast_select_fusion.1.refs_2_), channel_id=1, source_target_pairs={{0,2},{1,3},{2,0},{3,1},{4,6},{5,7},{6,4},{7,5},{8,10},{9,11},{10,... | collective-permute-start | bytes 1966088 | tf_op jit(solution)/shard_map/ppermute | solution.py:206
  45.4 15.7 %collective-permute-start.7 = (bf16[640,512]{1,0:T(8,128)(2,1)}, bf16[640,512]{1,0:T(8,128)(2,1)}, u32[]{:S(2)}, u32[]{:S(2)}) collective-permute-start(bf16[640,512]{1,0:T(8,128)(2,1)} %collective-permute-done.4), channel_id=1, source_target_pairs={{4,0},{5,1},{6,2},{7,3},{8,12},{9,13},{10,14},{11,15},{20,16},{21,... | collective-permute-start | bytes 1966088 | tf_op jit(solution)/shard_map/ppermute | solution.py:206
  46.7 27.7 %collective-permute-start.15 = (bf16[640,512]{1,0:T(8,128)(2,1)}, bf16[640,512]{1,0:T(8,128)(2,1)S(1)}, u32[]{:S(2)}, u32[]{:S(2)}) collective-permute-start(bf16[640,512]{1,0:T(8,128)(2,1)} %collective-permute-done.1.refs_2_), channel_id=1, source_target_pairs={{0,1},{1,0},{2,3},{3,2},{4,5},{5,4},{6,7},{7,6},{8,9},{9,8},{10,11... | collective-permute-start | bytes 1966088 | tf_op jit(solution)/shard_map/ppermute | solution.py:206
  46.8 27.9 %collective-permute-start.14 = (bf16[640,512]{1,0:T(8,128)(2,1)}, bf16[640,512]{1,0:T(8,128)(2,1)S(1)}, u32[]{:S(2)}, u32[]{:S(2)}) collective-permute-start(bf16[640,512]{1,0:T(8,128)(2,1)} %collective-permute-done.refs_0_), channel_id=1, source_target_pairs={{0,1},{1,0},{2,3},{3,2},{4,5},{5,4},{6,7},{7,6},{8,9},{9,8},{10,11... | collective-permute-start | bytes 1966088 | tf_op jit(solution)/shard_map/ppermute | solution.py:206
  57.6 4.6 %copy-start.7 = (bf16[640,512]{1,0:T(8,128)(2,1)}, bf16[640,512]{1,0:T(8,128)(2,1)S(1)}, u32[]{:S(2)}) copy-start(bf16[640,512]{1,0:T(8,128)(2,1)S(1)} %collective-permute-done.6.refs_0_) | copy-start | bytes 1966084
  57.6 32.9 %collective-permute-start.13 = (bf16[640,512]{1,0:T(8,128)(2,1)S(1)}, bf16[640,512]{1,0:T(8,128)(2,1)S(1)}, u32[]{:S(2)}, u32[]{:S(2)}) collective-permute-start(bf16[640,512]{1,0:T(8,128)(2,1)S(1)} %broadcast_select_fusion.1.refs_2_), channel_id=1, source_target_pairs={{0,1},{1,0},{2,3},{3,2},{4,5},{5,4},{6,7},{7,6},{8,9},{9,8},{10,11... | collective-permute-start | bytes 1966088 | tf_op jit(solution)/shard_map/ppermute | solution.py:206
  61.1 29.5 %collective-permute-start.12 = (bf16[640,512]{1,0:T(8,128)(2,1)}, bf16[640,512]{1,0:T(8,128)(2,1)S(1)}, u32[]{:S(2)}, u32[]{:S(2)}) collective-permute-start(bf16[640,512]{1,0:T(8,128)(2,1)} %collective-permute-done.3.refs_0_), channel_id=1, source_target_pairs={{0,1},{1,0},{2,3},{3,2},{4,5},{5,4},{6,7},{7,6},{8,9},{9,8},{10,11... | collective-permute-start | bytes 1966088 | tf_op jit(solution)/shard_map/ppermute | solution.py:206
  63.1 27.2 %collective-permute-start.8 = (bf16[640,512]{1,0:T(8,128)(2,1)S(1)}, bf16[640,512]{1,0:T(8,128)(2,1)S(1)}, u32[]{:S(2)}, u32[]{:S(2)}) collective-permute-start(bf16[640,512]{1,0:T(8,128)(2,1)S(1)} %broadcast_select_fusion.refs_2_), channel_id=1, source_target_pairs={{0,2},{1,3},{2,0},{3,1},{4,6},{5,7},{6,4},{7,5},{8,10},{9,11},{10,... | collective-permute-start | bytes 1966088 | tf_op jit(solution)/shard_map/ppermute | solution.py:206
  63.6 1.1 copy-start.6
  64.7 9.9 %copy-start.8 = (bf16[640,512]{1,0:T(8,128)(2,1)S(1)}, bf16[640,512]{1,0:T(8,128)(2,1)}, u32[]{:S(2)}) copy-start(bf16[640,512]{1,0:T(8,128)(2,1)} %copy-done.7) | copy-start | bytes 1966084
  74.4 31.6 %collective-permute-start.11 = (bf16[640,512]{1,0:T(8,128)(2,1)S(1)}, bf16[640,512]{1,0:T(8,128)(2,1)S(1)}, u32[]{:S(2)}, u32[]{:S(2)}) collective-permute-start(bf16[640,512]{1,0:T(8,128)(2,1)S(1)} %broadcast_select_fusion.refs_2_), channel_id=1, source_target_pairs={{0,1},{1,0},{2,3},{3,2},{4,5},{5,4},{6,7},{7,6},{8,9},{9,8},{10,11... | collective-permute-start | bytes 1966088 | tf_op jit(solution)/shard_map/ppermute | solution.py:206
  74.6 31.4 %collective-permute-start.10 = (bf16[640,512]{1,0:T(8,128)(2,1)S(1)}, bf16[640,512]{1,0:T(8,128)(2,1)S(1)}, u32[]{:S(2)}, u32[]{:S(2)}) collective-permute-start(bf16[640,512]{1,0:T(8,128)(2,1)S(1)} %copy-done.8), channel_id=1, source_target_pairs={{0,1},{1,0},{2,3},{3,2},{4,5},{5,4},{6,7},{7,6},{8,9},{9,8},{10,11... | collective-permute-start | bytes 1966088 | tf_op jit(solution)/shard_map/ppermute | solution.py:206
  90.3 31.5 %collective-permute-start.9 = (bf16[640,512]{1,0:T(8,128)(2,1)S(1)}, bf16[640,512]{1,0:T(8,128)(2,1)S(1)}, u32[]{:S(2)}, u32[]{:S(2)}) collective-permute-start(bf16[640,512]{1,0:T(8,128)(2,1)S(1)} %collective-permute-done.8.refs_0_), channel_id=1, source_target_pairs={{0,1},{1,0},{2,3},{3,2},{4,5},{5,4},{6,7},{7,6},{8,9},{9,8},{10,11... | collective-permute-start | bytes 1966088 | tf_op jit(solution)/shard_map/ppermute | solution.py:206
  157.2 15.3 %copy-start.3 = (bf16[128,1792]{1,0:T(8,128)(2,1)S(1)}, bf16[128,1792]{1,0:T(8,128)(2,1)}, u32[]{:S(2)}) copy-start(bf16[128,1792]{1,0:T(8,128)(2,1)} %get-tuple-element.57.dg) | copy-start | bytes 1376260
  157.2 21.8 %collective-permute-start.23 = (f32[3,128,512]{2,1,0:T(8,128)S(1)}, f32[3,128,512]{2,1,0:T(8,128)S(1)}, u32[]{:S(2)}, u32[]{:S(2)}) collective-permute-start(f32[3,128,512]{2,1,0:T(8,128)S(1)} %get-tuple-element.64), channel_id=1, source_target_pairs={{0,1},{1,0},{2,3},{3,2},{4,5},{5,4},{6,7},{7,6},{8,9},{9,8},{10,11... | collective-permute-start | bytes 2359304 | tf_op jit(solution)/shard_map/ppermute | solution.py:206
  172.2 11.0 %collective-permute-start.18 = (f32[4,128,512]{2,1,0:T(8,128)S(1)}, f32[4,128,512]{2,1,0:T(8,128)S(1)}, u32[]{:S(2)}, u32[]{:S(2)}) collective-permute-start(f32[4,128,512]{2,1,0:T(8,128)S(1)} %get-tuple-element.62), channel_id=1, source_target_pairs={{0,1},{1,0},{2,3},{3,2},{4,5},{5,4},{6,7},{7,6},{8,9},{9,8},{10,11... | collective-permute-start | bytes 3145736 | tf_op jit(solution)/shard_map/ppermute | solution.py:206
  178.7 14.1 %copy-start.9 = (f32[1,1792]{1,0:T(1,128)S(1)}, f32[1,1792]{1,0:T(1,128)}, u32[]{:S(2)}) copy-start(f32[1,1792]{1,0:T(1,128)} %get-tuple-element.65) | copy-start | bytes 21508
  178.7 6.9 %collective-permute-start.17 = (f32[1,128,512]{2,1,0:T(8,128)S(1)}, f32[1,128,512]{2,1,0:T(8,128)S(1)}, u32[]{:S(2)}, u32[]{:S(2)}) collective-permute-start(f32[1,128,512]{2,1,0:T(8,128)S(1)} %get-tuple-element.60), channel_id=1, source_target_pairs={{0,1},{1,0},{2,3},{3,2},{4,5},{5,4},{6,7},{7,6},{8,9},{9,8},{10,11... | collective-permute-start | bytes 786440 | tf_op jit(solution)/shard_map/ppermute | solution.py:206
  179.3 12.0 %collective-permute-start.24 = (bf16[128,512]{1,0:T(8,128)(2,1)S(1)}, bf16[128,512]{1,0:T(8,128)(2,1)S(1)}, u32[]{:S(2)}, u32[]{:S(2)}) collective-permute-start(bf16[128,512]{1,0:T(8,128)(2,1)S(1)} %get-tuple-element.74), channel_id=1, source_target_pairs={{0,8},{1,9},{2,10},{3,11},{4,12},{5,13},{6,14},{7,15},{8,0},{9,1},... | collective-permute-start | bytes 393224 | tf_op jit(solution)/shard_map/ppermute | solution.py:206
  179.4 12.0 %collective-permute-start.25 = (bf16[128,512]{1,0:T(8,128)(2,1)S(1)}, bf16[128,512]{1,0:T(8,128)(2,1)S(1)}, u32[]{:S(2)}, u32[]{:S(2)}) collective-permute-start(bf16[128,512]{1,0:T(8,128)(2,1)S(1)} %get-tuple-element.76), channel_id=1, source_target_pairs={{0,4},{1,5},{2,6},{3,7},{4,8},{5,9},{6,10},{7,11},{8,12},{9,13},{1... | collective-permute-start | bytes 393224 | tf_op jit(solution)/shard_map/ppermute | solution.py:206
  181.8 11.6 %collective-permute-start.26 = (bf16[128,512]{1,0:T(8,128)(2,1)S(1)}, bf16[128,512]{1,0:T(8,128)(2,1)S(1)}, u32[]{:S(2)}, u32[]{:S(2)}) collective-permute-start(bf16[128,512]{1,0:T(8,128)(2,1)S(1)} %get-tuple-element.75), channel_id=1, source_target_pairs={{0,12},{1,13},{2,14},{3,15},{4,0},{5,1},{6,2},{7,3},{8,4},{9,5},{1... | collective-permute-start | bytes 393224 | tf_op jit(solution)/shard_map/ppermute | solution.py:206
  183.6 19.4 %collective-permute-start.19 = (bf16[128,512]{1,0:T(8,128)(2,1)S(1)}, bf16[128,512]{1,0:T(8,128)(2,1)S(1)}, u32[]{:S(2)}, u32[]{:S(2)}) collective-permute-start(bf16[128,512]{1,0:T(8,128)(2,1)S(1)} %get-tuple-element.70), channel_id=1, source_target_pairs={{0,10},{1,11},{2,8},{3,9},{4,14},{5,15},{6,12},{7,13},{8,2},{9,3},... | collective-permute-start | bytes 393224 | tf_op jit(solution)/shard_map/ppermute | solution.py:206
  185.6 17.3 %collective-permute-start.20 = (bf16[128,512]{1,0:T(8,128)(2,1)S(1)}, bf16[128,512]{1,0:T(8,128)(2,1)S(1)}, u32[]{:S(2)}, u32[]{:S(2)}) collective-permute-start(bf16[128,512]{1,0:T(8,128)(2,1)S(1)} %get-tuple-element.73), channel_id=1, source_target_pairs={{0,6},{1,7},{2,4},{3,5},{4,10},{5,11},{6,8},{7,9},{8,14},{9,15},{1... | collective-permute-start | bytes 393224 | tf_op jit(solution)/shard_map/ppermute | solution.py:206
  191.3 11.6 %collective-permute-start.21 = (bf16[128,512]{1,0:T(8,128)(2,1)S(1)}, bf16[128,512]{1,0:T(8,128)(2,1)S(1)}, u32[]{:S(2)}, u32[]{:S(2)}) collective-permute-start(bf16[128,512]{1,0:T(8,128)(2,1)S(1)} %get-tuple-element.72), channel_id=1, source_target_pairs={{0,14},{1,15},{2,12},{3,13},{4,2},{5,3},{6,0},{7,1},{8,6},{9,7},{1... | collective-permute-start | bytes 393224 | tf_op jit(solution)/shard_map/ppermute | solution.py:206
  191.3 13.7 %collective-permute-start.22 = (bf16[128,512]{1,0:T(8,128)(2,1)S(1)}, bf16[128,512]{1,0:T(8,128)(2,1)S(1)}, u32[]{:S(2)}, u32[]{:S(2)}) collective-permute-start(bf16[128,512]{1,0:T(8,128)(2,1)S(1)} %get-tuple-element.71), channel_id=1, source_target_pairs={{0,2},{1,3},{2,0},{3,1},{4,6},{5,7},{6,4},{7,5},{8,10},{9,11},{10,... | collective-permute-start | bytes 393224 | tf_op jit(solution)/shard_map/ppermute | solution.py:206
  (5 other events, 4.8 us)

commit v2 on v0

v2 whole, which is shorter than its diff:
```python
import jax
import jax.numpy as jnp
from jax import lax
from jax.experimental import pallas as pl
from jax.experimental.pallas import tpu as pltpu
from jax.sharding import PartitionSpec as P

slope_gain = 4.0
AXIS = "tensor"
NT = (((1,), (1,)), ((), ()))
F32 = jnp.float32
BF16 = jnp.bfloat16
VMEM_LIMIT = 48 << 20


def nt_dot(left, weight):
    return lax.dot_general(left, weight, NT, preferred_element_type=F32)


def dot(left, right):
    return jnp.dot(left, right, preferred_element_type=F32)


def forward_call(tok, pairs, chips, core, gate_w, up_w, down_w, sums):
    count = len(pairs)
    rows, half = pairs[0][0].shape
    width = 2 * half
    hidden = gate_w.shape[1]
    slots = 2
    pieces = [piece for pair in pairs for piece in pair]
    sum_shapes = [(tok, hidden), (tok, hidden), (rows - tok, hidden)]
    carried = [] if sums is None else list(sums)
    where = jnp.stack([jnp.asarray(c, jnp.int32) for c in chips + [core]])

    def kernel(where_ref, *refs):
        data = refs[: 2 * count]
        weights = refs[2 * count : 2 * count + 3]
        old = refs[2 * count + 3 : 2 * count + 3 + len(carried)]
        new = refs[2 * count + 3 + len(carried) : 2 * count + 6 + len(carried)]
        feats, gbuf, ubuf, dbuf, gate, up, feed, dsem, wsem, ssem = refs[2 * count + 6 + len(carried) :]
        accs = (gate, up, feed)
        mine = pl.multiple_of(where_ref[count] * half, half)
        theirs = pl.multiple_of(half - where_ref[count] * half, half)

        def loads(i, slot):
            at = pl.multiple_of(where_ref[i] * width, width)
            return (
                pltpu.make_async_copy(weights[0].at[pl.ds(at, width), :], gbuf.at[slot], wsem.at[0, slot]),
                pltpu.make_async_copy(weights[1].at[pl.ds(at, width), :], ubuf.at[slot], wsem.at[1, slot]),
                pltpu.make_async_copy(weights[2].at[:, pl.ds(at, width)], dbuf.at[slot], wsem.at[2, slot]),
            )

        def data_loads(j, own, other):
            return (
                pltpu.make_async_copy(own, feats.at[j, :, pl.ds(mine, half)], dsem.at[0, j]),
                pltpu.make_async_copy(other, feats.at[j, :, pl.ds(theirs, half)], dsem.at[1, j]),
            )

        sums_in = [pltpu.make_async_copy(o, v, ssem.at[k]) for k, (o, v) in enumerate(zip(old, accs))]
        sums_out = [pltpu.make_async_copy(v, o, ssem.at[k]) for k, (v, o) in enumerate(zip(accs, new))]
        for copy in data_loads(0, data[0], data[1]):
            copy.start()
        for copy in loads(0, 0):
            copy.start()
        for copy in sums_in:
            copy.start()
        for j in range(1, count):
            for copy in data_loads(j, data[2 * j], data[2 * j + 1]):
                copy.start()
        if not carried:
            for acc in accs:
                acc[...] = jnp.zeros_like(acc)

        def step(i, _):
            slot = lax.rem(i, slots)

            @pl.when(i + 1 < count)
            def _():
                for copy in loads(i + 1, 1 - slot):
                    copy.start()

            for copy in data_loads(i, data[0], data[1]):
                copy.wait()
            arrived = loads(i, slot)
            for k, (acc, buf) in enumerate(zip(accs, (gbuf, ubuf, dbuf))):
                arrived[k].wait()
                if carried:

                    @pl.when(i == 0)
                    def _(k=k):
                        sums_in[k].wait()

                if k < 2:
                    acc[...] += dot(feats[i, rows - tok :, :], buf[slot])
                else:
                    acc[...] += nt_dot(feats[i, : rows - tok, :], buf[slot])

                @pl.when(i == count - 1)
                def _(k=k):
                    sums_out[k].start()

            return 0

        lax.fori_loop(0, count, step, 0)
        for copy in sums_out:
            copy.wait()

    any_spec = pl.BlockSpec(memory_space=pl.ANY)
    args = pieces + [gate_w, up_w, down_w] + carried
    return pl.pallas_call(
        kernel,
        in_specs=[pl.BlockSpec(memory_space=pltpu.SMEM)] + [any_spec] * len(args),
        out_specs=[any_spec] * 3,
        out_shape=[jax.ShapeDtypeStruct(s, F32) for s in sum_shapes],
        scratch_shapes=[
            pltpu.VMEM((count, rows, width), BF16),
            pltpu.VMEM((slots, width, hidden), BF16),
            pltpu.VMEM((slots, width, hidden), BF16),
            pltpu.VMEM((slots, hidden, width), BF16),
        ]
        + [pltpu.VMEM(s, F32) for s in sum_shapes]
        + [
            pltpu.SemaphoreType.DMA((2, count)),
            pltpu.SemaphoreType.DMA((3, slots)),
            pltpu.SemaphoreType.DMA((3,)),
        ],
        input_output_aliases={1 + 2 * count + 3 + k: k for k in range(3)} if carried else {},
        compiler_params=pltpu.CompilerParams(vmem_limit_bytes=VMEM_LIMIT),
        cost_estimate=pl.CostEstimate(
            flops=count * 2 * width * hidden * (rows + tok),
            transcendentals=0,
            bytes_accessed=count * width * (6 * hidden + 2 * rows),
        ),
        name="forward",
    )(where, *args)


def half_sigmoid(x):
    return 0.5 * jnp.tanh(x) + 0.5


def neuron_tile(theta, share, g, u, feeds):
    sig = half_sigmoid(0.5 * g)
    gs = g * sig
    current = gs * u
    usl = u * (sig * (1.0 + g * (1.0 - sig)))
    membrane = theta * share
    spikes = []
    for _ in feeds:
        pre = membrane + current
        spike = half_sigmoid((0.5 * slope_gain) * (pre - theta))
        spikes.append(spike)
        membrane = pre - theta * spike
    later = None
    for feed, spike in zip(feeds[::-1], spikes[::-1]):
        diff = feed if later is None else feed - later
        both = theta * diff * (slope_gain * spike * (1.0 - spike))
        dpre = both if later is None else both + later
        term = diff * spike - both
        dg = (dpre * usl).astype(BF16).astype(F32)
        du = (dpre * gs).astype(BF16).astype(F32)
        if later is None:
            grad, dgate, dup = term, dg, du
        else:
            grad, dgate, dup = grad + term, dgate + dg, dup + du
        later = dpre
    return dgate, dup, grad + later * share


def neuron_rows(gate, up, feed, lev_ref, off_ref, dg_ref, du_ref, gt_ref):
    tok, part = gate.shape
    steps = feed.shape[0] // tok
    tile = 16
    theta = jnp.broadcast_to(lev_ref[...].astype(F32) / 8.0, (tile, part))
    acc = jnp.zeros((tile, part), F32)
    for r in range(0, tok, tile):
        at = slice(r, r + tile)
        feeds = [feed[t * tok + r : t * tok + r + tile, :] for t in range(steps)]
        share = off_ref[at, :].astype(F32) / 256.0
        dgate, dup, grad = neuron_tile(theta, share, gate[at, :], up[at, :], feeds)
        dg_ref[at, :] = dgate.astype(BF16)
        du_ref[at, :] = dup.astype(BF16)
        acc = acc + grad
    gt_ref[...] = jnp.sum(acc, axis=0, keepdims=True)


def hidden_part(hidden):
    return 256 if hidden % 256 == 0 else hidden


def neuron_outs(tok, hidden):
    return [
        jax.ShapeDtypeStruct((tok, hidden), BF16),
        jax.ShapeDtypeStruct((tok, hidden), BF16),
        jax.ShapeDtypeStruct((1, hidden), F32),
    ]


def neuron_call(gate, up, feed, levels, offsets):
    tok, hidden = gate.shape
    part = hidden_part(hidden)
    col = lambda rows: pl.BlockSpec((rows, part), lambda s: (0, s))
    return pl.pallas_call(
        neuron_rows,
        grid=(hidden // part,),
        in_specs=[col(tok), col(tok), col(feed.shape[0]), col(1), col(tok)],
        out_specs=[col(tok), col(tok), col(1)],
        out_shape=neuron_outs(tok, hidden),
        name="neuron",
    )(gate, up, feed, levels.reshape(1, hidden), offsets)


def last_call(pair, blocks, gate_w, up_w, down_w, sums, levels, offsets):
    rows, width = pair[0].shape
    tok, hidden = sums[0].shape
    part = hidden_part(hidden)
    count = hidden // part

    def kernel(blk, own, other, ga, gb, ua, ub, da, db, gi, ui, fi, lev, off, dg, du, gt, gate, up, feed):
        now = lax.rem(pl.program_id(0), 2)
        neuron_rows(gate.at[1 - now], up.at[1 - now], feed.at[1 - now], lev, off, dg, du, gt)
        xo = own[rows - tok :, :]
        xp = other[rows - tok :, :]
        gate[now] = gi[...] + dot(xo, ga[...]) + dot(xp, gb[...])
        up[now] = ui[...] + dot(xo, ua[...]) + dot(xp, ub[...])
        feed[now] = fi[...] + nt_dot(own[: rows - tok, :], da[...]) + nt_dot(other[: rows - tok, :], db[...])

    ahead = lambda s: jnp.minimum(s, count - 1)
    behind = lambda s: jnp.maximum(s - 1, 0)
    whole = pl.BlockSpec((rows, width), lambda s, b: (0, 0))
    spec = lambda k: pl.BlockSpec((width, part), lambda s, b: (b[k, 0], ahead(s)))
    dspec = lambda k: pl.BlockSpec((part, width), lambda s, b: (ahead(s), b[k, 0]))
    col = lambda n: pl.BlockSpec((n, part), lambda s, b: (0, ahead(s)))
    late = lambda n: pl.BlockSpec((n, part), lambda s, b: (0, behind(s)))
    return pl.pallas_call(
        kernel,
        grid_spec=pltpu.PrefetchScalarGridSpec(
            num_scalar_prefetch=1,
            grid=(count + 1,),
            in_specs=[whole, whole, spec(0), spec(1), spec(0), spec(1), dspec(0), dspec(1)]
            + [col(tok), col(tok), col(rows - tok), late(1), late(tok)],
            out_specs=[late(tok), late(tok), late(1)],
            scratch_shapes=[
                pltpu.VMEM((2, tok, part), F32),
                pltpu.VMEM((2, tok, part), F32),
                pltpu.VMEM((2, rows - tok, part), F32),
            ],
        ),
        out_shape=neuron_outs(tok, hidden),
        compiler_params=pltpu.CompilerParams(vmem_limit_bytes=VMEM_LIMIT),
        name="last",
    )(blocks, *pair, gate_w, gate_w, up_w, up_w, down_w, down_w, *sums, levels.reshape(1, hidden), offsets)


def backward_call(dgate, dup, blocks, gate_w, up_w, width):
    tok, hidden = dgate.shape
    count = blocks.shape[0]
    slots = 3

    def kernel(blk, dg, du, gw, uw, out, gbuf, ubuf, sem):
        def loads(i, slot):
            at = pl.multiple_of(blk[i] * width, width)
            return (
                pltpu.make_async_copy(gw.at[pl.ds(at, width), :], gbuf.at[slot], sem.at[0, slot]),
                pltpu.make_async_copy(uw.at[pl.ds(at, width), :], ubuf.at[slot], sem.at[1, slot]),
            )

        for i in range(min(slots - 1, count)):
            for copy in loads(i, i):
                copy.start()

        def step(i, _):
            slot = lax.rem(i, slots)

            @pl.when(i + slots - 1 < count)
            def _():
                for copy in loads(i + slots - 1, lax.rem(i + slots - 1, slots)):
                    copy.start()

            for copy in loads(i, slot):
                copy.wait()
            out[i] = nt_dot(dg[...], gbuf[slot]) + nt_dot(du[...], ubuf[slot])
            return 0

        lax.fori_loop(0, count, step, 0)

    vmem = pl.BlockSpec(memory_space=pltpu.VMEM)
    any_spec = pl.BlockSpec(memory_space=pl.ANY)
    return pl.pallas_call(
        kernel,
        in_specs=[pl.BlockSpec(memory_space=pltpu.SMEM), vmem, vmem, any_spec, any_spec],
        out_specs=vmem,
        out_shape=jax.ShapeDtypeStruct((count, tok, width), F32),
        scratch_shapes=[
            pltpu.VMEM((slots, width, hidden), BF16),
            pltpu.VMEM((slots, width, hidden), BF16),
            pltpu.SemaphoreType.DMA((2, slots)),
        ],
        compiler_params=pltpu.CompilerParams(vmem_limit_bytes=VMEM_LIMIT),
        cost_estimate=pl.CostEstimate(
            flops=count * 4 * width * hidden * tok,
            transcendentals=0,
            bytes_accessed=count * width * (4 * hidden + 4 * tok),
        ),
        name="backward",
    )(blocks, dgate, dup, gate_w, up_w)


def z_map(moves):
    return [(i, moves[i // 4] * 4 + i % 4) for i in range(16) if i // 4 in moves]


CORE = [(i, i ^ 1) for i in range(16)]
PAIR = z_map({0: 1, 1: 0, 2: 3, 3: 2})
MID = z_map({1: 2, 2: 1})
OUT = z_map({1: 0, 2: 3})
CROSS = [(i, i ^ 2) for i in range(16)]


def around(turn, flip):
    return [(i, ((i // 4 + turn) % 4 * 4 + i % 4) ^ (2 * flip)) for i in range(16)]


def send(piece, moves):
    return lax.ppermute(piece, AXIS, moves)


fence = lax.optimization_barrier


def body_line(inputs, gate_w, up_w, down_w, cotangent, levels, offsets):
    steps, tok, width = cotangent.shape
    me = lax.axis_index(AXIS)
    core = me % 2
    chip = me // 2
    z = me // 4
    middle = (z == 1) | (z == 2)

    def blocks_of(chips):
        chips = jnp.stack(chips).astype(jnp.int32)
        return jnp.stack([2 * chips + core, 2 * chips + 1 - core]).astype(jnp.int32)

    far_a = jnp.where(middle, 6, 4)
    far_b = jnp.where(middle, 4, 6)

    own = jnp.concatenate([cotangent.reshape(steps * tok, width), inputs], axis=0)
    def more(pairs, chips, sums):
        return forward_call(tok, pairs, chips, core, gate_w, up_w, down_w, sums)

    p1 = send(own, PAIR)
    p2a = send(own, MID)
    x0 = send(own, CROSS)
    own_c = send(own, CORE)
    sums = more([(own, own_c)], [chip], None)
    x0, p1, p2a, sums = fence((x0, p1, p2a, sums))
    p2b = send(p1, MID)
    p3a = send(p2a, OUT)
    x1 = send(p1, CROSS)
    x0_c = send(x0, CORE)
    p1_c = send(p1, CORE)
    sums = more([(x0, x0_c), (p1, p1_c)], [chip ^ 1, chip ^ 2], sums)
    x1, p2a, p2b, p3a, sums = fence((x1, p2a, p2b, p3a, sums))
    a = jnp.where(middle, p2a, p3a)
    p3b = send(p2b, OUT)
    x2 = send(a, CROSS)
    x1_c = send(x1, CORE)
    a_c = send(a, CORE)
    sums = more([(x1, x1_c), (a, a_c)], [chip ^ 3, chip ^ far_a], sums)
    x2, p2b, p3b, sums = fence((x2, p2b, p3b, sums))
    b = jnp.where(middle, p2b, p3b)
    x3 = send(b, CROSS)
    x2_c = send(x2, CORE)
    b_c = send(b, CORE)
    sums = more([(x2, x2_c), (b, b_c)], [chip ^ 1 ^ far_a, chip ^ far_b], sums)
    x3, sums = fence((x3, sums))
    x3_c = send(x3, CORE)
    dgate, dup, grad_threshold = last_call(
        (x3, x3_c), blocks_of([chip ^ 1 ^ far_b]), gate_w, up_w, down_w, sums, levels, offsets
    )

    turns = [2, 1, 3, 0]

    def partial(dgate, dup, flip):
        chips = jnp.stack([((z + t) % 4 * 2 + chip % 2) ^ flip for t in turns]).astype(jnp.int32)
        out = backward_call(
            dgate, dup, jnp.concatenate([2 * chips + 1 - core, 2 * chips + core]), gate_w, up_w, width
        )
        return out[:4], out[4:]

    theirs, mine = partial(dgate, dup, 1)
    across = (mine + send(theirs, CORE)).astype(BF16)
    dgate, dup, across = fence((dgate, dup, across))
    across = send(across, CROSS)
    theirs, mine = partial(dgate, dup, 0)
    theirs, mine, across = fence((theirs, mine, across))
    column = mine + send(theirs, CORE) + across.astype(F32)
    grad_input = column[3]
    column = column.astype(BF16)
    for k in range(3):
        grad_input = grad_input + send(column[k], around(turns[k], 0)).astype(F32)
    return grad_input, grad_threshold.reshape(-1)


def body_plain(inputs, gate_w, up_w, down_w, cotangent, levels, offsets):
    steps, tok, width = cotangent.shape
    piece = lax.all_gather(inputs, AXIS, axis=1, tiled=True)
    gate = dot(piece, gate_w)
    up = dot(piece, up_w)
    cot = lax.all_gather(cotangent, AXIS, axis=2, tiled=True)
    feed = nt_dot(cot.reshape(steps * tok, -1), down_w)
    dgate, dup, grad_threshold = neuron_call(gate, up, feed, levels, offsets)
    term = nt_dot(dgate, gate_w) + nt_dot(dup, up_w)
    grad_input = lax.psum_scatter(term, AXIS, scatter_dimension=1, tiled=True)
    return grad_input, grad_threshold.reshape(-1)


def solution(mesh):
    placed = (
        P("groups", "tensor"),
        P(None, "tensor"),
        P(None, "tensor"),
        P("tensor", None),
        P(None, "groups", "tensor"),
        P("tensor"),
        P("groups", "tensor"),
    )
    body = body_line if mesh.shape[AXIS] == 16 else body_plain
    return jax.shard_map(
        body,
        mesh=mesh,
        in_specs=placed,
        out_specs=(P("groups", "tensor"), P(("groups", "tensor"))),
        check_vma=False,
    )
```

time: 369 us -> 150 us (0.41)
  matrix products: 183 us -> 0 us
  waiting for transfers between devices: 165 us -> 29.9 us
  Pallas kernels: 0 us -> 90.5 us
  starting transfers between devices: 0.11 us -> 19.6 us
  between operations: 13.8 us -> 0.92 us
    dot_general x11 -> x0, matrix products: 183 us -> none  [the longest x8 129 us: transposed_product(): lax.dot_general(left, weight, (((1,), (1,)), ((), ())), preferred_element...]
    all_gather x2 -> x0, waiting for transfers between devices: 93.2 us -> none  [the longest x1 48.5 us: body(): lax.all_gather(cotangent, 'tensor', axis=2, tiled=True)]
    pallas_call x0 -> x7, Pallas kernels: none -> 90.5 us  [the longest x4 51.9 us: forward_call(): pl.pallas_call(kernel, in_specs=[pl.BlockSpec(memory_space=pltpu.SMEM)] +...]
    reduce_scatter x1 -> x0, waiting for transfers between devices: 70 us -> none  [body(): lax.psum_scatter(term, 'tensor', scatter_dimension=1, tiled=True)]
    ppermute x0 -> x23, waiting for transfers between devices: none -> 29.9 us  [send(): return lax.ppermute(piece, AXIS, moves)]
    ppermute x0 -> x23, starting transfers between devices: none -> 19.6 us  [send(): return lax.ppermute(piece, AXIS, moves)]
    reduce_sum x1 -> x0, other arithmetic: 4.77 us -> none  [body(): jnp.sum(feedback * spike - later * spike - dspike * slope, axis=0)]
  transfers between devices with their start and end apart: 3 -> 23, of which waited for: 3 -> 12; matrix products, arithmetic and copies ran while one was open for 9% -> 1% of each run, Pallas kernels for 0% -> 44%
where the time goes in v2:
time: 150 us; the launch traced here: 149 us
  Pallas kernels  90.5 us (60%)
  waiting for transfers between devices  29.9 us (20%)
  starting transfers between devices  19.6 us (13%)
  other arithmetic  5.98 us (4%)
  local copies, waits for them, and re-layouts  2.2 us (1%)
    pallas_call x4, Pallas kernels, forward_call(): pl.pallas_call(kernel, in_specs=[pl.BlockSpec(memory_space=pltpu.SMEM)] +...  51.9 us
    ppermute x23, waiting for transfers between devices, send(): return lax.ppermute(piece, AXIS, moves)  29.9 us
    pallas_call x2, Pallas kernels, backward_call(): pl.pallas_call(kernel, in_specs=[pl.BlockSpec(memory_space=pltpu.SMEM), v...  26 us
    ppermute x23, starting transfers between devices, send(): return lax.ppermute(piece, AXIS, moves)  19.6 us
    pallas_call x1, Pallas kernels, last_call(): pl.pallas_call(kernel, grid_spec=pltpu.PrefetchScalarGridSpec(num_scalar_...  12.5 us
  transfers between devices with their start and end apart: 23, of which 12 were waited for; matrix products, arithmetic and copies ran while one was open for 1% of the time, Pallas kernels for 44%

profile of v2, /device:TPU:0, one launch (start us, length us, event | category | flops | bytes accessed | tf_op | source)
XLA Modules:
  0.0 149.0 jit_solution(16832745173344583260)
XLA Ops:
  0.6 1.2 pad_maximum_fusion.refs_0_
  2.3 2.6 %collective-permute-start = (bf16[640,512]{1,0:T(8,128)(2,1)S(1)}, bf16[640,512]{1,0:T(8,128)(2,1)}, u32[]{:S(2)}, u32[]{:S(2)}) collective-permute-start(bf16[640,512]{1,0:T(8,128)(2,1)S(1)} %pad_maximum_fusion.refs_0_), channel_id=1, source_target_pairs={{0,2},{1,3},{2,0},{3,1},{4,6},{5,7},{6,4},{7,5},{8,10},{9,11},{10,... | collective-permute-start | bytes 1966088 | tf_op jit(solution)/shard_map/ppermute | solution.py:325
  4.9 1.6 %collective-permute-start.1 = (bf16[640,512]{1,0:T(8,128)(2,1)S(1)}, bf16[640,512]{1,0:T(8,128)(2,1)S(1)}, u32[]{:S(2)}, u32[]{:S(2)}) collective-permute-start(bf16[640,512]{1,0:T(8,128)(2,1)S(1)} %pad_maximum_fusion.refs_0_), channel_id=1, source_target_pairs={{0,4},{1,5},{2,6},{3,7},{4,0},{5,1},{6,2},{7,3},{8,12},{9,13},{10,... | collective-permute-start | bytes 1966088 | tf_op jit(solution)/shard_map/ppermute | solution.py:325
  6.5 1.5 %collective-permute-start.2 = (bf16[640,512]{1,0:T(8,128)(2,1)S(1)}, bf16[640,512]{1,0:T(8,128)(2,1)}, u32[]{:S(2)}, u32[]{:S(2)}) collective-permute-start(bf16[640,512]{1,0:T(8,128)(2,1)S(1)} %pad_maximum_fusion.refs_0_), channel_id=1, source_target_pairs={{4,8},{5,9},{6,10},{7,11},{8,4},{9,5},{10,6},{11,7},{20,24},{21,25... | collective-permute-start | bytes 1966088 | tf_op jit(solution)/shard_map/ppermute | solution.py:325
  8.0 0.8 copy-done.1
  8.9 1.1 copy-done.2
  10.0 8.9 %forward.4 = (f32[128,1792]{1,0:T(8,128)S(1)}, f32[128,1792]{1,0:T(8,128)S(1)}, f32[512,1792]{1,0:T(8,128)}) custom-call(s32[2]{0:T(128)S(1)} %pad_add_fusion.2.where_ref, bf16[640,512]{1,0:T(8,128)(2,1)S(1)} %pad_maximum_fusion.refs_0_, bf16[640,512]{1,0:T(8,128)(2,1)S(1)} %copy-done.2, bf16[8192,1792]{1,0:T(8,128)(2,1)} %gw.3, bf16[8192,1792]{1,0:T(8,128)(2,1)} %uw.3, ...), custom_call_target="tpu_custom_call" | custom-call | flops 2818572288 | bytes 12320768 | tf_op jit(solution)/shard_map/forward/pallas_call | solution.py:110
  18.9 1.4 collective-permute-done.refs_0_
  20.3 1.4 collective-permute-done.1.refs_2_
  22.6 1.5 %collective-permute-start.5 = (bf16[640,512]{1,0:T(8,128)(2,1)S(1)}, bf16[640,512]{1,0:T(8,128)(2,1)}, u32[]{:S(2)}, u32[]{:S(2)}) collective-permute-start(bf16[640,512]{1,0:T(8,128)(2,1)S(1)} %collective-permute-done.1.refs_2_), channel_id=1, source_target_pairs={{4,8},{5,9},{6,10},{7,11},{8,4},{9,5},{10,6},{11,7},{20,24},{21,25... | collective-permute-start | bytes 1966088 | tf_op jit(solution)/shard_map/ppermute | solution.py:325
  24.1 1.3 collective-permute-start.6
  25.5 14.4 %forward.5 = (f32[128,1792]{1,0:T(8,128)S(1)}, f32[128,1792]{1,0:T(8,128)S(1)}, f32[512,1792]{1,0:T(8,128)}) custom-call(s32[3]{0:T(128)S(1)} %add_add_fusion.where_ref, bf16[640,512]{1,0:T(8,128)(2,1)} %collective-permute-done.refs_0_, bf16[640,512]{1,0:T(8,128)(2,1)} %collective-permute-done.7.refs_1_, ...), custom_call_target="tpu_custom_call", output_to_operand_aliasing={{0}: (8, {}), {1}: (9, {}), {2}: (10, {})} | custom-call | flops 5637144576 | bytes 24641536 | tf_op jit(solution)/shard_map/forward/pallas_call | solution.py:110
  39.9 7.1 %collective-permute-done.6 = bf16[640,512]{1,0:T(8,128)(2,1)} collective-permute-done((bf16[640,512]{1,0:T(8,128)(2,1)}, bf16[640,512]{1,0:T(8,128)(2,1)}, u32[]{:S(2)}, u32[]{:S(2)}) %collective-permute-start.6) | collective-permute-done | bytes 655392 | tf_op jit(solution)/shard_map/ppermute | solution.py:325
  47.0 1.2 broadcast_select_fusion.1.refs_2_
  48.7 1.5 %collective-permute-start.9 = (bf16[640,512]{1,0:T(8,128)(2,1)S(1)}, bf16[640,512]{1,0:T(8,128)(2,1)}, u32[]{:S(2)}, u32[]{:S(2)}) collective-permute-start(bf16[640,512]{1,0:T(8,128)(2,1)S(1)} %broadcast_select_fusion.1.refs_2_), channel_id=1, source_target_pairs={{0,2},{1,3},{2,0},{3,1},{4,6},{5,7},{6,4},{7,5},{8,10},{9,11},{10,... | collective-permute-start | bytes 1966088 | tf_op jit(solution)/shard_map/ppermute | solution.py:325
  50.2 1.5 collective-permute-start.10
  51.8 14.2 %forward.6 = (f32[128,1792]{1,0:T(8,128)S(1)}, f32[128,1792]{1,0:T(8,128)S(1)}, f32[512,1792]{1,0:T(8,128)}) custom-call(s32[3]{0:T(128)S(1)} %add_add_fusion.1.where_ref, bf16[640,512]{1,0:T(8,128)(2,1)S(1)} %collective-permute-done.4.refs_0_, ...), custom_call_target="tpu_custom_call", output_to_operand_aliasing={{0}: (8, {}), {1}: (9, {}), {2}: (10, {})} | custom-call | flops 5637144576 | bytes 24641536 | tf_op jit(solution)/shard_map/forward/pallas_call | solution.py:110
  66.1 2.8 %collective-permute-done.10 = bf16[640,512]{1,0:T(8,128)(2,1)} collective-permute-done((bf16[640,512]{1,0:T(8,128)(2,1)}, bf16[640,512]{1,0:T(8,128)(2,1)}, u32[]{:S(2)}, u32[]{:S(2)}) %collective-permute-start.10) | collective-permute-done | bytes 655392 | tf_op jit(solution)/shard_map/ppermute | solution.py:325
  68.9 1.2 broadcast_select_fusion.refs_2_
  71.2 1.2 collective-permute-done.15.refs_3_
  72.5 1.0 collective-permute-done.14.refs_1_
  73.5 14.4 %forward.7 = (f32[128,1792]{1,0:T(8,128)S(1)}, f32[128,1792]{1,0:T(8,128)S(1)}, f32[512,1792]{1,0:T(8,128)}) custom-call(s32[3]{0:T(128)S(1)} %add_add_fusion.2.where_ref, bf16[640,512]{1,0:T(8,128)(2,1)} %collective-permute-done.9.refs_0_, ...), custom_call_target="tpu_custom_call", output_to_operand_aliasing={{0}: (8, {}), {1}: (9, {}), {2}: (10, {})} | custom-call | flops 5637144576 | bytes 24641536 | tf_op jit(solution)/shard_map/forward/pallas_call | solution.py:110
  88.3 1.9 %collective-permute-done.16.other = bf16[640,512]{1,0:T(8,128)(2,1)S(1)} collective-permute-done((bf16[640,512]{1,0:T(8,128)(2,1)}, bf16[640,512]{1,0:T(8,128)(2,1)S(1)}, u32[]{:S(2)}, u32[]{:S(2)}) %collective-permute-start.16) | collective-permute-done | bytes 655392 | tf_op jit(solution)/shard_map/ppermute | solution.py:325
  90.2 12.5 %last.1 = (bf16[128,1792]{1,0:T(8,128)(2,1)S(1)}, bf16[128,1792]{1,0:T(8,128)(2,1)S(1)}, f32[1,1792]{1,0:T(1,128)S(1)}) custom-call(s32[2,1]{1,0:T(2,128)S(1)} %pad_add_fusion.blk, bf16[640,512]{1,0:T(8,128)(2,1)} %collective-permute-done.13.own, bf16[640,512]{1,0:T(8,128)(2,1)S(1)} %collective-permute-done.16.other, bf16[8192,1792]{1,0:T(8,128)(2,1)} %gw.3, ...), custom_call_target="tpu_custom_call" | custom-call | tf_op jit(solution)/shard_map/last/pallas_call | solution.py:235
  102.7 13.0 %backward.2 = f32[8,128,512]{2,1,0:T(8,128)S(1)} custom-call(s32[8]{0:T(128)S(1)} %pad_add_fusion.3.blk, bf16[128,1792]{1,0:T(8,128)(2,1)S(1)} %get-tuple-element.83.dg, bf16[128,1792]{1,0:T(8,128)(2,1)S(1)} %get-tuple-element.84.du, bf16[8192,1792]{1,0:T(8,128)(2,1)} %gw.3, bf16[8192,1792]{1,0:T(8,128)(2,1)} %uw.3), custom_call_target="tpu_custom_call" | custom-call | flops 3758096384 | bytes 31457280 | tf_op jit(solution)/shard_map/backward/pallas_call | solution.py:289
  116.1 2.4 %collective-permute-done.17 = f32[4,128,512]{2,1,0:T(8,128)S(1)} collective-permute-done((f32[4,128,512]{2,1,0:T(8,128)S(1)}, f32[4,128,512]{2,1,0:T(8,128)S(1)}, u32[]{:S(2)}, u32[]{:S(2)}) %collective-permute-start.17) | collective-permute-done | bytes 1048608 | tf_op jit(solution)/shard_map/ppermute | solution.py:325
  119.4 13.0 %backward.3 = f32[8,128,512]{2,1,0:T(8,128)S(1)} custom-call(s32[8]{0:T(128)S(1)} %pad_add_fusion.1.blk, bf16[128,1792]{1,0:T(8,128)(2,1)S(1)} %get-tuple-element.83.dg, bf16[128,1792]{1,0:T(8,128)(2,1)S(1)} %get-tuple-element.84.du, bf16[8192,1792]{1,0:T(8,128)(2,1)} %gw.3, bf16[8192,1792]{1,0:T(8,128)(2,1)} %uw.3), custom_call_target="tpu_custom_call" | custom-call | flops 3758096384 | bytes 31457280 | tf_op jit(solution)/shard_map/backward/pallas_call | solution.py:289
  132.9 2.7 %collective-permute-done.19 = f32[4,128,512]{2,1,0:T(8,128)S(1)} collective-permute-done((f32[4,128,512]{2,1,0:T(8,128)S(1)}, f32[4,128,512]{2,1,0:T(8,128)S(1)}, u32[]{:S(2)}, u32[]{:S(2)}) %collective-permute-start.19) | collective-permute-done | bytes 1048608 | tf_op jit(solution)/shard_map/ppermute | solution.py:325
  136.2 1.5 %collective-permute-start.21 = (bf16[128,512]{1,0:T(8,128)(2,1)S(1)}, bf16[128,512]{1,0:T(8,128)(2,1)S(1)}, u32[]{:S(2)}, u32[]{:S(2)}) collective-permute-start(bf16[128,512]{1,0:T(8,128)(2,1)S(1)} %get-tuple-element.100), channel_id=1, source_target_pairs={{0,4},{1,5},{2,6},{3,7},{4,8},{5,9},{6,10},{7,11},{8,12},{9,13},{1... | collective-permute-start | bytes 393224 | tf_op jit(solution)/shard_map/ppermute | solution.py:325
  137.7 2.3 %collective-permute-start.22 = (bf16[128,512]{1,0:T(8,128)(2,1)S(1)}, bf16[128,512]{1,0:T(8,128)(2,1)S(1)}, u32[]{:S(2)}, u32[]{:S(2)}) collective-permute-start(bf16[128,512]{1,0:T(8,128)(2,1)S(1)} %get-tuple-element.99), channel_id=1, source_target_pairs={{0,12},{1,13},{2,14},{3,15},{4,0},{5,1},{6,2},{7,3},{8,4},{9,5},{1... | collective-permute-start | bytes 393224 | tf_op jit(solution)/shard_map/ppermute | solution.py:325
  140.7 7.4 %collective-permute-done.20 = bf16[128,512]{1,0:T(8,128)(2,1)S(1)} collective-permute-done((bf16[128,512]{1,0:T(8,128)(2,1)S(1)}, bf16[128,512]{1,0:T(8,128)(2,1)S(1)}, u32[]{:S(2)}, u32[]{:S(2)}) %collective-permute-start.20) | collective-permute-done | bytes 131104 | tf_op jit(solution)/shard_map/ppermute | solution.py:325
  148.3 0.8 fusion.3
  (50 shorter events, 6.9 us)
Async XLA Ops:
  1.8 6.2 %collective-permute-start.3 = (bf16[640,512]{1,0:T(8,128)(2,1)S(1)}, bf16[640,512]{1,0:T(8,128)(2,1)S(1)}, u32[]{:S(2)}, u32[]{:S(2)}) collective-permute-start(bf16[640,512]{1,0:T(8,128)(2,1)S(1)} %pad_maximum_fusion.refs_0_), channel_id=1, source_target_pairs={{0,1},{1,0},{2,3},{3,2},{4,5},{5,4},{6,7},{7,6},{8,9},{9,8},{10,11... | collective-permute-start | bytes 1966088 | tf_op jit(solution)/shard_map/ppermute | solution.py:325
  2.3 18.0 %collective-permute-start = (bf16[640,512]{1,0:T(8,128)(2,1)S(1)}, bf16[640,512]{1,0:T(8,128)(2,1)}, u32[]{:S(2)}, u32[]{:S(2)}) collective-permute-start(bf16[640,512]{1,0:T(8,128)(2,1)S(1)} %pad_maximum_fusion.refs_0_), channel_id=1, source_target_pairs={{0,2},{1,3},{2,0},{3,1},{4,6},{5,7},{6,4},{7,5},{8,10},{9,11},{10,... | collective-permute-start | bytes 1966088 | tf_op jit(solution)/shard_map/ppermute | solution.py:325
  4.9 16.8 %collective-permute-start.1 = (bf16[640,512]{1,0:T(8,128)(2,1)S(1)}, bf16[640,512]{1,0:T(8,128)(2,1)S(1)}, u32[]{:S(2)}, u32[]{:S(2)}) collective-permute-start(bf16[640,512]{1,0:T(8,128)(2,1)S(1)} %pad_maximum_fusion.refs_0_), channel_id=1, source_target_pairs={{0,4},{1,5},{2,6},{3,7},{4,0},{5,1},{6,2},{7,3},{8,12},{9,13},{10,... | collective-permute-start | bytes 1966088 | tf_op jit(solution)/shard_map/ppermute | solution.py:325
  6.5 15.2 %collective-permute-start.2 = (bf16[640,512]{1,0:T(8,128)(2,1)S(1)}, bf16[640,512]{1,0:T(8,128)(2,1)}, u32[]{:S(2)}, u32[]{:S(2)}) collective-permute-start(bf16[640,512]{1,0:T(8,128)(2,1)S(1)} %pad_maximum_fusion.refs_0_), channel_id=1, source_target_pairs={{4,8},{5,9},{6,10},{7,11},{8,4},{9,5},{10,6},{11,7},{20,24},{21,25... | collective-permute-start | bytes 1966088 | tf_op jit(solution)/shard_map/ppermute | solution.py:325
  8.0 0.8 copy-start.1
  8.9 1.1 copy-start.2
  21.7 3.8 %collective-permute-start.7 = (bf16[640,512]{1,0:T(8,128)(2,1)}, bf16[640,512]{1,0:T(8,128)(2,1)}, u32[]{:S(2)}, u32[]{:S(2)}) collective-permute-start(bf16[640,512]{1,0:T(8,128)(2,1)} %collective-permute-done.refs_0_), channel_id=1, source_target_pairs={{0,1},{1,0},{2,3},{3,2},{4,5},{5,4},{6,7},{7,6},{8,9},{9,8},{10,11... | collective-permute-start | bytes 1966088 | tf_op jit(solution)/shard_map/ppermute | solution.py:325
  21.7 3.8 %collective-permute-start.8 = (bf16[640,512]{1,0:T(8,128)(2,1)S(1)}, bf16[640,512]{1,0:T(8,128)(2,1)}, u32[]{:S(2)}, u32[]{:S(2)}) collective-permute-start(bf16[640,512]{1,0:T(8,128)(2,1)S(1)} %collective-permute-done.1.refs_2_), channel_id=1, source_target_pairs={{0,1},{1,0},{2,3},{3,2},{4,5},{5,4},{6,7},{7,6},{8,9},{9,8},{10,11... | collective-permute-start | bytes 1966088 | tf_op jit(solution)/shard_map/ppermute | solution.py:325
  22.2 17.7 %collective-permute-start.4 = (bf16[640,512]{1,0:T(8,128)(2,1)S(1)}, bf16[640,512]{1,0:T(8,128)(2,1)S(1)}, u32[]{:S(2)}, u32[]{:S(2)}) collective-permute-start(bf16[640,512]{1,0:T(8,128)(2,1)S(1)} %collective-permute-done.1.refs_2_), channel_id=1, source_target_pairs={{0,2},{1,3},{2,0},{3,1},{4,6},{5,7},{6,4},{7,5},{8,10},{9,11},{10,... | collective-permute-start | bytes 1966088 | tf_op jit(solution)/shard_map/ppermute | solution.py:325
  22.6 17.3 %collective-permute-start.5 = (bf16[640,512]{1,0:T(8,128)(2,1)S(1)}, bf16[640,512]{1,0:T(8,128)(2,1)}, u32[]{:S(2)}, u32[]{:S(2)}) collective-permute-start(bf16[640,512]{1,0:T(8,128)(2,1)S(1)} %collective-permute-done.1.refs_2_), channel_id=1, source_target_pairs={{4,8},{5,9},{6,10},{7,11},{8,4},{9,5},{10,6},{11,7},{20,24},{21,25... | collective-permute-start | bytes 1966088 | tf_op jit(solution)/shard_map/ppermute | solution.py:325
  24.1 22.9 %collective-permute-start.6 = (bf16[640,512]{1,0:T(8,128)(2,1)}, bf16[640,512]{1,0:T(8,128)(2,1)}, u32[]{:S(2)}, u32[]{:S(2)}) collective-permute-start(bf16[640,512]{1,0:T(8,128)(2,1)} %collective-permute-done.2), channel_id=1, source_target_pairs={{4,0},{5,1},{6,2},{7,3},{8,12},{9,13},{10,14},{11,15},{20,16},{21,... | collective-permute-start | bytes 1966088 | tf_op jit(solution)/shard_map/ppermute | solution.py:325
  48.2 3.6 %collective-permute-start.12 = (bf16[640,512]{1,0:T(8,128)(2,1)S(1)}, bf16[640,512]{1,0:T(8,128)(2,1)}, u32[]{:S(2)}, u32[]{:S(2)}) collective-permute-start(bf16[640,512]{1,0:T(8,128)(2,1)S(1)} %broadcast_select_fusion.1.refs_2_), channel_id=1, source_target_pairs={{0,1},{1,0},{2,3},{3,2},{4,5},{5,4},{6,7},{7,6},{8,9},{9,8},{10,11... | collective-permute-start | bytes 1966088 | tf_op jit(solution)/shard_map/ppermute | solution.py:325
  48.2 3.6 %collective-permute-start.11 = (bf16[640,512]{1,0:T(8,128)(2,1)S(1)}, bf16[640,512]{1,0:T(8,128)(2,1)}, u32[]{:S(2)}, u32[]{:S(2)}) collective-permute-start(bf16[640,512]{1,0:T(8,128)(2,1)S(1)} %collective-permute-done.4.refs_0_), channel_id=1, source_target_pairs={{0,1},{1,0},{2,3},{3,2},{4,5},{5,4},{6,7},{7,6},{8,9},{9,8},{10,11... | collective-permute-start | bytes 1966088 | tf_op jit(solution)/shard_map/ppermute | solution.py:325
  48.7 17.3 %collective-permute-start.9 = (bf16[640,512]{1,0:T(8,128)(2,1)S(1)}, bf16[640,512]{1,0:T(8,128)(2,1)}, u32[]{:S(2)}, u32[]{:S(2)}) collective-permute-start(bf16[640,512]{1,0:T(8,128)(2,1)S(1)} %broadcast_select_fusion.1.refs_2_), channel_id=1, source_target_pairs={{0,2},{1,3},{2,0},{3,1},{4,6},{5,7},{6,4},{7,5},{8,10},{9,11},{10,... | collective-permute-start | bytes 1966088 | tf_op jit(solution)/shard_map/ppermute | solution.py:325
  50.2 18.6 %collective-permute-start.10 = (bf16[640,512]{1,0:T(8,128)(2,1)}, bf16[640,512]{1,0:T(8,128)(2,1)}, u32[]{:S(2)}, u32[]{:S(2)}) collective-permute-start(bf16[640,512]{1,0:T(8,128)(2,1)} %collective-permute-done.5), channel_id=1, source_target_pairs={{4,0},{5,1},{6,2},{7,3},{8,12},{9,13},{10,14},{11,15},{20,16},{21,... | collective-permute-start | bytes 1966088 | tf_op jit(solution)/shard_map/ppermute | solution.py:325
  70.0 2.4 %collective-permute-start.15 = (bf16[640,512]{1,0:T(8,128)(2,1)S(1)}, bf16[640,512]{1,0:T(8,128)(2,1)}, u32[]{:S(2)}, u32[]{:S(2)}) collective-permute-start(bf16[640,512]{1,0:T(8,128)(2,1)S(1)} %broadcast_select_fusion.refs_2_), channel_id=1, source_target_pairs={{0,1},{1,0},{2,3},{3,2},{4,5},{5,4},{6,7},{7,6},{8,9},{9,8},{10,11... | collective-permute-start | bytes 1966088 | tf_op jit(solution)/shard_map/ppermute | solution.py:325
  70.1 3.4 %collective-permute-start.14 = (bf16[640,512]{1,0:T(8,128)(2,1)}, bf16[640,512]{1,0:T(8,128)(2,1)}, u32[]{:S(2)}, u32[]{:S(2)}) collective-permute-start(bf16[640,512]{1,0:T(8,128)(2,1)} %collective-permute-done.9.refs_0_), channel_id=1, source_target_pairs={{0,1},{1,0},{2,3},{3,2},{4,5},{5,4},{6,7},{7,6},{8,9},{9,8},{10,11... | collective-permute-start | bytes 1966088 | tf_op jit(solution)/shard_map/ppermute | solution.py:325
  70.6 17.3 %collective-permute-start.13 = (bf16[640,512]{1,0:T(8,128)(2,1)S(1)}, bf16[640,512]{1,0:T(8,128)(2,1)}, u32[]{:S(2)}, u32[]{:S(2)}) collective-permute-start(bf16[640,512]{1,0:T(8,128)(2,1)S(1)} %broadcast_select_fusion.refs_2_), channel_id=1, source_target_pairs={{0,2},{1,3},{2,0},{3,1},{4,6},{5,7},{6,4},{7,5},{8,10},{9,11},{10,... | collective-permute-start | bytes 1966088 | tf_op jit(solution)/shard_map/ppermute | solution.py:325
  71.2 16.8 %copy-start.3 = (s32[1792]{0:T(1024)S(1)}, s32[1792]{0:T(1024)}, u32[]{:S(2)}) copy-start(s32[1792]{0:T(1024)} %param.12) | copy-start | bytes 21508
  71.2 19.0 %copy-start = (s32[128,1792]{1,0:T(8,128)S(1)}, s32[128,1792]{1,0:T(8,128)}, u32[]{:S(2)}) copy-start(s32[128,1792]{1,0:T(8,128)} %off.1) | copy-start | bytes 2752516
  87.9 2.4 %collective-permute-start.16 = (bf16[640,512]{1,0:T(8,128)(2,1)}, bf16[640,512]{1,0:T(8,128)(2,1)S(1)}, u32[]{:S(2)}, u32[]{:S(2)}) collective-permute-start(bf16[640,512]{1,0:T(8,128)(2,1)} %collective-permute-done.13.own), channel_id=1, source_target_pairs={{0,1},{1,0},{2,3},{3,2},{4,5},{5,4},{6,7},{7,6},{8,9},{9,8},{10,11... | collective-permute-start | bytes 1966088 | tf_op jit(solution)/shard_map/ppermute | solution.py:325
  115.9 2.7 %collective-permute-start.17 = (f32[4,128,512]{2,1,0:T(8,128)S(1)}, f32[4,128,512]{2,1,0:T(8,128)S(1)}, u32[]{:S(2)}, u32[]{:S(2)}) collective-permute-start(f32[4,128,512]{2,1,0:T(8,128)S(1)} %slice.33), channel_id=1, source_target_pairs={{0,1},{1,0},{2,3},{3,2},{4,5},{5,4},{6,7},{7,6},{8,9},{9,8},{10,11... | collective-permute-start | bytes 3145736 | tf_op jit(solution)/shard_map/ppermute | solution.py:325
  118.9 14.0 %collective-permute-start.18 = (bf16[4,128,512]{2,1,0:T(8,128)(2,1)S(1)}, bf16[4,128,512]{2,1,0:T(8,128)(2,1)S(1)}, u32[]{:S(2)}, u32[]{:S(2)}) collective-permute-start(bf16[4,128,512]{2,1,0:T(8,128)(2,1)S(1)} %fusion), channel_id=1, source_target_pairs={{0,2},{1,3},{2,0},{3,1},{4,6},{5,7},{6,4},{7,5},{8,10},{9,11},{10,... | collective-permute-start | bytes 1572872 | tf_op jit(solution)/shard_map/ppermute | solution.py:325
  132.9 2.7 %collective-permute-start.19 = (f32[4,128,512]{2,1,0:T(8,128)S(1)}, f32[4,128,512]{2,1,0:T(8,128)S(1)}, u32[]{:S(2)}, u32[]{:S(2)}) collective-permute-start(f32[4,128,512]{2,1,0:T(8,128)S(1)} %get-tuple-element.87), channel_id=1, source_target_pairs={{0,1},{1,0},{2,3},{3,2},{4,5},{5,4},{6,7},{7,6},{8,9},{9,8},{10,11... | collective-permute-start | bytes 3145736 | tf_op jit(solution)/shard_map/ppermute | solution.py:325
  135.9 12.2 %collective-permute-start.20 = (bf16[128,512]{1,0:T(8,128)(2,1)S(1)}, bf16[128,512]{1,0:T(8,128)(2,1)S(1)}, u32[]{:S(2)}, u32[]{:S(2)}) collective-permute-start(bf16[128,512]{1,0:T(8,128)(2,1)S(1)} %get-tuple-element.98), channel_id=1, source_target_pairs={{0,8},{1,9},{2,10},{3,11},{4,12},{5,13},{6,14},{7,15},{8,0},{9,1},... | collective-permute-start | bytes 393224 | tf_op jit(solution)/shard_map/ppermute | solution.py:325
  136.2 11.9 %collective-permute-start.21 = (bf16[128,512]{1,0:T(8,128)(2,1)S(1)}, bf16[128,512]{1,0:T(8,128)(2,1)S(1)}, u32[]{:S(2)}, u32[]{:S(2)}) collective-permute-start(bf16[128,512]{1,0:T(8,128)(2,1)S(1)} %get-tuple-element.100), channel_id=1, source_target_pairs={{0,4},{1,5},{2,6},{3,7},{4,8},{5,9},{6,10},{7,11},{8,12},{9,13},{1... | collective-permute-start | bytes 393224 | tf_op jit(solution)/shard_map/ppermute | solution.py:325
  137.7 10.6 %collective-permute-start.22 = (bf16[128,512]{1,0:T(8,128)(2,1)S(1)}, bf16[128,512]{1,0:T(8,128)(2,1)S(1)}, u32[]{:S(2)}, u32[]{:S(2)}) collective-permute-start(bf16[128,512]{1,0:T(8,128)(2,1)S(1)} %get-tuple-element.99), channel_id=1, source_target_pairs={{0,12},{1,13},{2,14},{3,15},{4,0},{5,1},{6,2},{7,3},{8,4},{9,5},{1... | collective-permute-start | bytes 393224 | tf_op jit(solution)/shard_map/ppermute | solution.py:325

commit v3 on v2

--- a/solution.py
+++ b/solution.py
@@ -10,7 +10,6 @@
 NT = (((1,), (1,)), ((), ()))
 F32 = jnp.float32
 BF16 = jnp.bfloat16
-VMEM_LIMIT = 48 << 20
 
 
 def nt_dot(left, weight):
@@ -21,7 +20,7 @@
     return jnp.dot(left, right, preferred_element_type=F32)
 
 
-def forward_call(tok, pairs, chips, core, gate_w, up_w, down_w, sums):
+def forward_call(tok, pairs, place, gate_w, up_w, down_w, sums):
     count = len(pairs)
     rows, half = pairs[0][0].shape
     width = 2 * half
@@ -30,24 +29,30 @@
     pieces = [piece for pair in pairs for piece in pair]
     sum_shapes = [(tok, hidden), (tok, hidden), (rows - tok, hidden)]
     carried = [] if sums is None else list(sums)
-    where = jnp.stack([jnp.asarray(c, jnp.int32) for c in chips + [core]])
-
-    def kernel(where_ref, *refs):
+
+    def kernel(*refs):
+        me = lax.axis_index(AXIS)
+        core = lax.rem(me, 2)
+        chips = place(me)
         data = refs[: 2 * count]
         weights = refs[2 * count : 2 * count + 3]
         old = refs[2 * count + 3 : 2 * count + 3 + len(carried)]
         new = refs[2 * count + 3 + len(carried) : 2 * count + 6 + len(carried)]
-        feats, gbuf, ubuf, dbuf, gate, up, feed, dsem, wsem, ssem = refs[2 * count + 6 + len(carried) :]
-        accs = (gate, up, feed)
-        mine = pl.multiple_of(where_ref[count] * half, half)
-        theirs = pl.multiple_of(half - where_ref[count] * half, half)
+        feats, gbuf, ubuf, dbuf, dsem, wsem = refs[2 * count + 6 + len(carried) :]
+        gate, up, feed = new
+        accs = (gate, feed, up)
+        mine = pl.multiple_of(core * half, half)
+        theirs = pl.multiple_of(half - core * half, half)
 
         def loads(i, slot):
-            at = pl.multiple_of(where_ref[i] * width, width)
+            chip = chips[0]
+            for j in range(1, count):
+                chip = jnp.where(i == j, chips[j], chip)
+            at = pl.multiple_of(chip * width, width)
             return (
                 pltpu.make_async_copy(weights[0].at[pl.ds(at, width), :], gbuf.at[slot], wsem.at[0, slot]),
+                pltpu.make_async_copy(weights[2].at[:, pl.ds(at, width)], dbuf.at[slot], wsem.at[2, slot]),
                 pltpu.make_async_copy(weights[1].at[pl.ds(at, width), :], ubuf.at[slot], wsem.at[1, slot]),
-                pltpu.make_async_copy(weights[2].at[:, pl.ds(at, width)], dbuf.at[slot], wsem.at[2, slot]),
             )
 
         def data_loads(j, own, other):
@@ -56,20 +61,15 @@
                 pltpu.make_async_copy(other, feats.at[j, :, pl.ds(theirs, half)], dsem.at[1, j]),
             )
 
-        sums_in = [pltpu.make_async_copy(o, v, ssem.at[k]) for k, (o, v) in enumerate(zip(old, accs))]
-        sums_out = [pltpu.make_async_copy(v, o, ssem.at[k]) for k, (v, o) in enumerate(zip(accs, new))]
         for copy in data_loads(0, data[0], data[1]):
             copy.start()
         for copy in loads(0, 0):
             copy.start()
-        for copy in sums_in:
-            copy.start()
         for j in range(1, count):
             for copy in data_loads(j, data[2 * j], data[2 * j + 1]):
                 copy.start()
-        if not carried:
-            for acc in accs:
-                acc[...] = jnp.zeros_like(acc)
+        for k, acc in enumerate(new):
+            acc[...] = old[k][...] if carried else jnp.zeros_like(acc)
 
         def step(i, _):
             slot = lax.rem(i, slots)
@@ -82,57 +82,42 @@
             for copy in data_loads(i, data[0], data[1]):
                 copy.wait()
             arrived = loads(i, slot)
-            for k, (acc, buf) in enumerate(zip(accs, (gbuf, ubuf, dbuf))):
+            for k, (acc, buf) in enumerate(zip(accs, (gbuf, dbuf, ubuf))):
                 arrived[k].wait()
-                if carried:
-
-                    @pl.when(i == 0)
-                    def _(k=k):
-                        sums_in[k].wait()
-
-                if k < 2:
+                if k != 1:
                     acc[...] += dot(feats[i, rows - tok :, :], buf[slot])
                 else:
                     acc[...] += nt_dot(feats[i, : rows - tok, :], buf[slot])
 
-                @pl.when(i == count - 1)
-                def _(k=k):
-                    sums_out[k].start()
-
             return 0
 
         lax.fori_loop(0, count, step, 0)
-        for copy in sums_out:
-            copy.wait()
 
     any_spec = pl.BlockSpec(memory_space=pl.ANY)
+    vmem = pl.BlockSpec(memory_space=pltpu.VMEM)
     args = pieces + [gate_w, up_w, down_w] + carried
     return pl.pallas_call(
         kernel,
-        in_specs=[pl.BlockSpec(memory_space=pltpu.SMEM)] + [any_spec] * len(args),
-        out_specs=[any_spec] * 3,
+        in_specs=[any_spec] * (2 * count + 3) + [vmem] * len(carried),
+        out_specs=[vmem] * 3,
         out_shape=[jax.ShapeDtypeStruct(s, F32) for s in sum_shapes],
         scratch_shapes=[
             pltpu.VMEM((count, rows, width), BF16),
             pltpu.VMEM((slots, width, hidden), BF16),
             pltpu.VMEM((slots, width, hidden), BF16),
             pltpu.VMEM((slots, hidden, width), BF16),
-        ]
-        + [pltpu.VMEM(s, F32) for s in sum_shapes]
-        + [
             pltpu.SemaphoreType.DMA((2, count)),
             pltpu.SemaphoreType.DMA((3, slots)),
-            pltpu.SemaphoreType.DMA((3,)),
         ],
-        input_output_aliases={1 + 2 * count + 3 + k: k for k in range(3)} if carried else {},
-        compiler_params=pltpu.CompilerParams(vmem_limit_bytes=VMEM_LIMIT),
+        input_output_aliases={2 * count + 3 + k: k for k in range(3)} if carried else {},
+        compiler_params=pltpu.CompilerParams(vmem_limit_bytes=36 << 20),
         cost_estimate=pl.CostEstimate(
             flops=count * 2 * width * hidden * (rows + tok),
             transcendentals=0,
             bytes_accessed=count * width * (6 * hidden + 2 * rows),
         ),
         name="forward",
-    )(where, *args)
+    )(*args)
 
 
 def half_sigmoid(x):
@@ -221,16 +206,16 @@
         neuron_rows(gate.at[1 - now], up.at[1 - now], feed.at[1 - now], lev, off, dg, du, gt)
         xo = own[rows - tok :, :]
         xp = other[rows - tok :, :]
-        gate[now] = gi[...] + dot(xo, ga[...]) + dot(xp, gb[...])
-        up[now] = ui[...] + dot(xo, ua[...]) + dot(xp, ub[...])
-        feed[now] = fi[...] + nt_dot(own[: rows - tok, :], da[...]) + nt_dot(other[: rows - tok, :], db[...])
+        at = pl.ds(pl.multiple_of(jnp.minimum(pl.program_id(0), count - 1) * part, part), part)
+        gate[now] = gi[:, at] + dot(xo, ga[...]) + dot(xp, gb[...])
+        up[now] = ui[:, at] + dot(xo, ua[...]) + dot(xp, ub[...])
+        feed[now] = fi[:, at] + nt_dot(own[: rows - tok, :], da[...]) + nt_dot(other[: rows - tok, :], db[...])
 
     ahead = lambda s: jnp.minimum(s, count - 1)
     behind = lambda s: jnp.maximum(s - 1, 0)
     whole = pl.BlockSpec((rows, width), lambda s, b: (0, 0))
     spec = lambda k: pl.BlockSpec((width, part), lambda s, b: (b[k, 0], ahead(s)))
     dspec = lambda k: pl.BlockSpec((part, width), lambda s, b: (ahead(s), b[k, 0]))
-    col = lambda n: pl.BlockSpec((n, part), lambda s, b: (0, ahead(s)))
     late = lambda n: pl.BlockSpec((n, part), lambda s, b: (0, behind(s)))
     return pl.pallas_call(
         kernel,
@@ -238,7 +223,8 @@
             num_scalar_prefetch=1,
             grid=(count + 1,),
             in_specs=[whole, whole, spec(0), spec(1), spec(0), spec(1), dspec(0), dspec(1)]
-            + [col(tok), col(tok), col(rows - tok), late(1), late(tok)],
+            + [pl.BlockSpec(memory_space=pltpu.VMEM)] * 3
+            + [late(1), late(tok)],
             out_specs=[late(tok), late(tok), late(1)],
             scratch_shapes=[
                 pltpu.VMEM((2, tok, part), F32),
@@ -247,19 +233,20 @@
             ],
         ),
         out_shape=neuron_outs(tok, hidden),
-        compiler_params=pltpu.CompilerParams(vmem_limit_bytes=VMEM_LIMIT),
+        compiler_params=pltpu.CompilerParams(vmem_limit_bytes=28 << 20),
         name="last",
     )(blocks, *pair, gate_w, gate_w, up_w, up_w, down_w, down_w, *sums, levels.reshape(1, hidden), offsets)
 
 
-def backward_call(dgate, dup, blocks, gate_w, up_w, width):
+def backward_call(dgate, dup, count, place, gate_w, up_w, width):
     tok, hidden = dgate.shape
-    count = blocks.shape[0]
     slots = 3
 
-    def kernel(blk, dg, du, gw, uw, out, gbuf, ubuf, sem):
+    def kernel(dg, du, gw, uw, out, gbuf, ubuf, sem):
+        me = lax.axis_index(AXIS)
+
         def loads(i, slot):
-            at = pl.multiple_of(blk[i] * width, width)
+            at = pl.multiple_of(place(me, i) * width, width)
             return (
                 pltpu.make_async_copy(gw.at[pl.ds(at, width), :], gbuf.at[slot], sem.at[0, slot]),
                 pltpu.make_async_copy(uw.at[pl.ds(at, width), :], ubuf.at[slot], sem.at[1, slot]),
@@ -288,7 +275,7 @@
     any_spec = pl.BlockSpec(memory_space=pl.ANY)
     return pl.pallas_call(
         kernel,
-        in_specs=[pl.BlockSpec(memory_space=pltpu.SMEM), vmem, vmem, any_spec, any_spec],
+        in_specs=[vmem, vmem, any_spec, any_spec],
         out_specs=vmem,
         out_shape=jax.ShapeDtypeStruct((count, tok, width), F32),
         scratch_shapes=[
@@ -296,14 +283,14 @@
             pltpu.VMEM((slots, width, hidden), BF16),
             pltpu.SemaphoreType.DMA((2, slots)),
         ],
-        compiler_params=pltpu.CompilerParams(vmem_limit_bytes=VMEM_LIMIT),
+        compiler_params=pltpu.CompilerParams(vmem_limit_bytes=28 << 20),
         cost_estimate=pl.CostEstimate(
             flops=count * 4 * width * hidden * tok,
             transcendentals=0,
             bytes_accessed=count * width * (4 * hidden + 4 * tok),
         ),
         name="backward",
-    )(blocks, dgate, dup, gate_w, up_w)
+    )(dgate, dup, gate_w, up_w)
 
 
 def z_map(moves):
@@ -340,51 +327,62 @@
         chips = jnp.stack(chips).astype(jnp.int32)
         return jnp.stack([2 * chips + core, 2 * chips + 1 - core]).astype(jnp.int32)
 
-    far_a = jnp.where(middle, 6, 4)
-    far_b = jnp.where(middle, 4, 6)
-
     own = jnp.concatenate([cotangent.reshape(steps * tok, width), inputs], axis=0)
-    def more(pairs, chips, sums):
-        return forward_call(tok, pairs, chips, core, gate_w, up_w, down_w, sums)
+    def far(me):
+        inner = lax.rem(me // 4 + 1, 4) >= 2
+        return jnp.where(inner, 6, 4), jnp.where(inner, 4, 6)
+
+    def more(pairs, place, sums):
+        return forward_call(tok, pairs, place, gate_w, up_w, down_w, sums)
 
     p1 = send(own, PAIR)
     p2a = send(own, MID)
     x0 = send(own, CROSS)
     own_c = send(own, CORE)
-    sums = more([(own, own_c)], [chip], None)
-    x0, p1, p2a, sums = fence((x0, p1, p2a, sums))
+    sums = more([(own, own_c)], lambda me: [me // 2], None)
+    p1, p2a, sums = fence((p1, p2a, sums))
     p2b = send(p1, MID)
     p3a = send(p2a, OUT)
+    p1, x0 = fence((p1, x0))
     x1 = send(p1, CROSS)
+    p1_c = send(p1, CORE)
     x0_c = send(x0, CORE)
-    p1_c = send(p1, CORE)
-    sums = more([(x0, x0_c), (p1, p1_c)], [chip ^ 1, chip ^ 2], sums)
-    x1, p2a, p2b, p3a, sums = fence((x1, p2a, p2b, p3a, sums))
+    sums = more([(p1, p1_c), (x0, x0_c)], lambda me: [(me // 2) ^ 2, (me // 2) ^ 1], sums)
+    p2b, p3a, p2a, sums = fence((p2b, p3a, p2a, sums))
+    p3b = send(p2b, OUT)
     a = jnp.where(middle, p2a, p3a)
-    p3b = send(p2b, OUT)
+    a, x1 = fence((a, x1))
     x2 = send(a, CROSS)
+    a_c = send(a, CORE)
     x1_c = send(x1, CORE)
-    a_c = send(a, CORE)
-    sums = more([(x1, x1_c), (a, a_c)], [chip ^ 3, chip ^ far_a], sums)
-    x2, p2b, p3b, sums = fence((x2, p2b, p3b, sums))
+    sums = more([(a, a_c), (x1, x1_c)], lambda me: [(me // 2) ^ far(me)[0], (me // 2) ^ 3], sums)
+    p3b, p2b, sums = fence((p3b, p2b, sums))
     b = jnp.where(middle, p2b, p3b)
+    b, x2 = fence((b, x2))
     x3 = send(b, CROSS)
+    b_c = send(b, CORE)
     x2_c = send(x2, CORE)
-    b_c = send(b, CORE)
-    sums = more([(x2, x2_c), (b, b_c)], [chip ^ 1 ^ far_a, chip ^ far_b], sums)
+    sums = more(
+        [(b, b_c), (x2, x2_c)],
+        lambda me: [(me // 2) ^ far(me)[1], (me // 2) ^ 1 ^ far(me)[0]],
+        sums,
+    )
     x3, sums = fence((x3, sums))
     x3_c = send(x3, CORE)
     dgate, dup, grad_threshold = last_call(
-        (x3, x3_c), blocks_of([chip ^ 1 ^ far_b]), gate_w, up_w, down_w, sums, levels, offsets
+        (x3, x3_c), blocks_of([chip ^ 1 ^ far(me)[1]]), gate_w, up_w, down_w, sums, levels, offsets
     )
 
     turns = [2, 1, 3, 0]
 
     def partial(dgate, dup, flip):
-        chips = jnp.stack([((z + t) % 4 * 2 + chip % 2) ^ flip for t in turns]).astype(jnp.int32)
-        out = backward_call(
-            dgate, dup, jnp.concatenate([2 * chips + 1 - core, 2 * chips + core]), gate_w, up_w, width
-        )
+        def place(me, i):
+            k = lax.rem(i, 4)
+            turn = jnp.where(k == 0, 2, jnp.where(k == 2, 3, jnp.where(k == 3, 0, 1)))
+            to = (lax.rem(me // 4 + turn, 4) * 2 + lax.rem(me // 2, 2)) ^ flip
+            return 2 * to + jnp.where(i < 4, 1 - lax.rem(me, 2), lax.rem(me, 2))
+
+        out = backward_call(dgate, dup, 8, place, gate_w, up_w, width)
         return out[:4], out[4:]
 
     theirs, mine = partial(dgate, dup, 1)

time: 150 us -> 147 us (0.980)
  Pallas kernels: 90.5 us -> 76 us
  local copies, waits for them, and re-layouts: 2.2 us -> 7.97 us
  starting transfers between devices: 19.6 us -> 25.1 us
  waiting for transfers between devices: 29.9 us -> 32 us
  other arithmetic: 5.98 us -> 4.36 us
    pallas_call x6, Pallas kernels: 78 us -> 64.3 us  [the longest x4 39.1 us: forward_call(): pl.pallas_call(kernel, in_specs=[any_spec] * (2 * count + 3) + [vmem] * l...]
    unnamed x8 -> x12, local copies, waits for them, and re-layouts: 1.93 us -> 7.63 us
    ppermute x23, starting transfers between devices: 19.6 us -> 25.1 us  [send(): return lax.ppermute(piece, AXIS, moves)]
    ppermute x23, waiting for transfers between devices: 29.9 us -> 32 us  [send(): return lax.ppermute(piece, AXIS, moves)]
  transfers between devices with their start and end apart: 23 -> 23, of which waited for: 12 -> 11; matrix products, arithmetic and copies ran while one was open for 1% -> 1% of each run, Pallas kernels for 44% -> 35%
where the time goes in v3:
time: 147 us; the launch traced here: 146 us
  Pallas kernels  76 us (52%)
  waiting for transfers between devices  32 us (22%)
  starting transfers between devices  25.1 us (17%)
  local copies, waits for them, and re-layouts  7.97 us (5%)
  other arithmetic  4.36 us (3%)
    pallas_call x4, Pallas kernels, forward_call(): pl.pallas_call(kernel, in_specs=[any_spec] * (2 * count + 3) + [vmem] * l...  39.1 us
    ppermute x23, waiting for transfers between devices, send(): return lax.ppermute(piece, AXIS, moves)  32 us
    pallas_call x2, Pallas kernels, backward_call(): pl.pallas_call(kernel, in_specs=[vmem, vmem, any_spec, any_spec], out_spe...  25.2 us
    ppermute x23, starting transfers between devices, send(): return lax.ppermute(piece, AXIS, moves)  25.1 us
    pallas_call x1, Pallas kernels, last_call(): pl.pallas_call(kernel, grid_spec=pltpu.PrefetchScalarGridSpec(num_scalar_...  11.8 us
    unnamed x12, local copies, waits for them, and re-layouts  7.63 us
  transfers between devices with their start and end apart: 23, of which 11 were waited for; matrix products, arithmetic and copies ran while one was open for 1% of the time, Pallas kernels for 35%

profile of v3, /device:TPU:0, one launch (start us, length us, event | category | flops | bytes accessed | tf_op | source)
XLA Modules:
  0.0 146.4 jit_solution(10461329689214273670)
XLA Ops:
  2.3 2.6 %collective-permute-start = (bf16[640,512]{1,0:T(8,128)(2,1)S(1)}, bf16[640,512]{1,0:T(8,128)(2,1)S(1)}, u32[]{:S(2)}, u32[]{:S(2)}) collective-permute-start(bf16[640,512]{1,0:T(8,128)(2,1)S(1)} %pad_maximum_fusion.refs_0_), channel_id=1, source_target_pairs={{0,4},{1,5},{2,6},{3,7},{4,0},{5,1},{6,2},{7,3},{8,12},{9,13},{10,... | collective-permute-start | bytes 1966088 | tf_op jit(solution)/shard_map/ppermute | solution.py:312
  5.0 1.5 %collective-permute-start.1 = (bf16[640,512]{1,0:T(8,128)(2,1)S(1)}, bf16[640,512]{1,0:T(8,128)(2,1)}, u32[]{:S(2)}, u32[]{:S(2)}) collective-permute-start(bf16[640,512]{1,0:T(8,128)(2,1)S(1)} %pad_maximum_fusion.refs_0_), channel_id=1, source_target_pairs={{4,8},{5,9},{6,10},{7,11},{8,4},{9,5},{10,6},{11,7},{20,24},{21,25... | collective-permute-start | bytes 1966088 | tf_op jit(solution)/shard_map/ppermute | solution.py:312
  6.5 1.5 %collective-permute-start.5 = (bf16[640,512]{1,0:T(8,128)(2,1)S(1)}, bf16[640,512]{1,0:T(8,128)(2,1)S(1)}, u32[]{:S(2)}, u32[]{:S(2)}) collective-permute-start(bf16[640,512]{1,0:T(8,128)(2,1)S(1)} %pad_maximum_fusion.refs_0_), channel_id=1, source_target_pairs={{0,2},{1,3},{2,0},{3,1},{4,6},{5,7},{6,4},{7,5},{8,10},{9,11},{10,... | collective-permute-start | bytes 1966088 | tf_op jit(solution)/shard_map/ppermute | solution.py:312
  8.0 6.7 %forward.4 = (f32[128,1792]{1,0:T(8,128)S(1)}, f32[128,1792]{1,0:T(8,128)S(1)}, f32[512,1792]{1,0:T(8,128)S(1)}) custom-call(bf16[640,512]{1,0:T(8,128)(2,1)S(1)} %pad_maximum_fusion.refs_0_, bf16[640,512]{1,0:T(8,128)(2,1)S(1)} %collective-permute-done.2.refs_1_, bf16[8192,1792]{1,0:T(8,128)(2,1)} %gw.3, bf16[8192,1792]{1,0:T(8,128)(2,1)} %uw.3, ...), custom_call_target="tpu_custom_call" | custom-call | flops 2818572288 | bytes 12320768 | tf_op jit(solution)/shard_map/forward/pallas_call | solution.py:99
  14.7 1.8 %copy-done = f32[512,1792]{1,0:T(8,128)} copy-done((f32[512,1792]{1,0:T(8,128)}, f32[512,1792]{1,0:T(8,128)S(1)}, u32[]{:S(2)}) %copy-start) | copy-done | bytes 3670040
  16.5 3.8 %collective-permute-done.refs_0_ = bf16[640,512]{1,0:T(8,128)(2,1)S(1)} collective-permute-done((bf16[640,512]{1,0:T(8,128)(2,1)S(1)}, bf16[640,512]{1,0:T(8,128)(2,1)S(1)}, u32[]{:S(2)}, u32[]{:S(2)}) %collective-permute-start) | collective-permute-done | bytes 655392 | tf_op jit(solution)/shard_map/ppermute | solution.py:312
  20.3 3.0 %collective-permute-done.5.refs_2_ = bf16[640,512]{1,0:T(8,128)(2,1)S(1)} collective-permute-done((bf16[640,512]{1,0:T(8,128)(2,1)S(1)}, bf16[640,512]{1,0:T(8,128)(2,1)S(1)}, u32[]{:S(2)}, u32[]{:S(2)}) %collective-permute-start.5) | collective-permute-done | bytes 655392 | tf_op jit(solution)/shard_map/ppermute | solution.py:312
  23.8 1.5 %collective-permute-start.3 = (bf16[640,512]{1,0:T(8,128)(2,1)S(1)}, bf16[640,512]{1,0:T(8,128)(2,1)}, u32[]{:S(2)}, u32[]{:S(2)}) collective-permute-start(bf16[640,512]{1,0:T(8,128)(2,1)S(1)} %collective-permute-done.refs_0_), channel_id=1, source_target_pairs={{4,8},{5,9},{6,10},{7,11},{8,4},{9,5},{10,6},{11,7},{20,24},{21,25... | collective-permute-start | bytes 1966088 | tf_op jit(solution)/shard_map/ppermute | solution.py:312
  25.3 1.3 collective-permute-start.4
  26.6 1.6 %collective-permute-start.9 = (bf16[640,512]{1,0:T(8,128)(2,1)S(1)}, bf16[640,512]{1,0:T(8,128)(2,1)S(1)}, u32[]{:S(2)}, u32[]{:S(2)}) collective-permute-start(bf16[640,512]{1,0:T(8,128)(2,1)S(1)} %collective-permute-done.refs_0_), channel_id=1, source_target_pairs={{0,2},{1,3},{2,0},{3,1},{4,6},{5,7},{6,4},{7,5},{8,10},{9,11},{10,... | collective-permute-start | bytes 1966088 | tf_op jit(solution)/shard_map/ppermute | solution.py:312
  28.2 2.0 %copy-done.1 = f32[512,1792]{1,0:T(8,128)S(1)} copy-done((f32[512,1792]{1,0:T(8,128)S(1)}, f32[512,1792]{1,0:T(8,128)}, u32[]{:S(2)}) %copy-start.1) | copy-done | bytes 3670040
  30.2 11.3 %forward.5 = (f32[128,1792]{1,0:T(8,128)S(1)}, f32[128,1792]{1,0:T(8,128)S(1)}, f32[512,1792]{1,0:T(8,128)S(1)}) custom-call(bf16[640,512]{1,0:T(8,128)(2,1)S(1)} %collective-permute-done.refs_0_, bf16[640,512]{1,0:T(8,128)(2,1)} %collective-permute-done.6.refs_1_, ...), custom_call_target="tpu_custom_call", output_to_operand_aliasing={{0}: (7, {}), {1}: (8, {}), {2}: (9, {})} | custom-call | flops 5637144576 | bytes 24641536 | tf_op jit(solution)/shard_map/forward/pallas_call | solution.py:99
  41.5 4.0 %collective-permute-done.4 = bf16[640,512]{1,0:T(8,128)(2,1)} collective-permute-done((bf16[640,512]{1,0:T(8,128)(2,1)}, bf16[640,512]{1,0:T(8,128)(2,1)}, u32[]{:S(2)}, u32[]{:S(2)}) %collective-permute-start.4) | collective-permute-done | bytes 655392 | tf_op jit(solution)/shard_map/ppermute | solution.py:312
  47.3 1.5 collective-permute-start.8
  48.8 1.6 %collective-permute-start.12 = (bf16[640,512]{1,0:T(8,128)(2,1)S(1)}, bf16[640,512]{1,0:T(8,128)(2,1)S(1)}, u32[]{:S(2)}, u32[]{:S(2)}) collective-permute-start(bf16[640,512]{1,0:T(8,128)(2,1)S(1)} %broadcast_select_fusion.1.refs_0_), channel_id=1, source_target_pairs={{0,2},{1,3},{2,0},{3,1},{4,6},{5,7},{6,4},{7,5},{8,10},{9,11},{10,... | collective-permute-start | bytes 1966088 | tf_op jit(solution)/shard_map/ppermute | solution.py:312
  50.3 10.6 %forward.6 = (f32[128,1792]{1,0:T(8,128)S(1)}, f32[128,1792]{1,0:T(8,128)S(1)}, f32[512,1792]{1,0:T(8,128)S(1)}) custom-call(bf16[640,512]{1,0:T(8,128)(2,1)S(1)} %broadcast_select_fusion.1.refs_0_, bf16[640,512]{1,0:T(8,128)(2,1)S(1)} %collective-permute-done.10.refs_1_, ...), custom_call_target="tpu_custom_call", output_to_operand_aliasing={{0}: (7, {}), {1}: (8, {}), {2}: (9, {})} | custom-call | flops 5637144576 | bytes 24641536 | tf_op jit(solution)/shard_map/forward/pallas_call | solution.py:99
  60.9 5.2 %collective-permute-done.8 = bf16[640,512]{1,0:T(8,128)(2,1)S(1)} collective-permute-done((bf16[640,512]{1,0:T(8,128)(2,1)}, bf16[640,512]{1,0:T(8,128)(2,1)S(1)}, u32[]{:S(2)}, u32[]{:S(2)}) %collective-permute-start.8) | collective-permute-done | bytes 655392 | tf_op jit(solution)/shard_map/ppermute | solution.py:312
  66.8 1.5 %collective-permute-start.13 = (bf16[640,512]{1,0:T(8,128)(2,1)S(1)}, bf16[640,512]{1,0:T(8,128)(2,1)S(1)}, u32[]{:S(2)}, u32[]{:S(2)}) collective-permute-start(bf16[640,512]{1,0:T(8,128)(2,1)S(1)} %broadcast_select_fusion.refs_0_), channel_id=1, source_target_pairs={{0,2},{1,3},{2,0},{3,1},{4,6},{5,7},{6,4},{7,5},{8,10},{9,11},{10,... | collective-permute-start | bytes 1966088 | tf_op jit(solution)/shard_map/ppermute | solution.py:312
  69.3 10.6 %forward.7 = (f32[128,1792]{1,0:T(8,128)S(1)}, f32[128,1792]{1,0:T(8,128)S(1)}, f32[512,1792]{1,0:T(8,128)S(1)}) custom-call(bf16[640,512]{1,0:T(8,128)(2,1)S(1)} %broadcast_select_fusion.refs_0_, bf16[640,512]{1,0:T(8,128)(2,1)S(1)} %collective-permute-done.14.refs_1_, ...), custom_call_target="tpu_custom_call", output_to_operand_aliasing={{0}: (7, {}), {1}: (8, {}), {2}: (9, {})} | custom-call | flops 5637144576 | bytes 24641536 | tf_op jit(solution)/shard_map/forward/pallas_call | solution.py:99
  79.9 1.8 %copy-done.2 = f32[512,1792]{1,0:T(8,128)} copy-done((f32[512,1792]{1,0:T(8,128)}, f32[512,1792]{1,0:T(8,128)S(1)}, u32[]{:S(2)}) %copy-start.2) | copy-done | bytes 3670040
  81.6 1.9 %collective-permute-done.13.own = bf16[640,512]{1,0:T(8,128)(2,1)S(1)} collective-permute-done((bf16[640,512]{1,0:T(8,128)(2,1)S(1)}, bf16[640,512]{1,0:T(8,128)(2,1)S(1)}, u32[]{:S(2)}, u32[]{:S(2)}) %collective-permute-start.13) | collective-permute-done | bytes 655392 | tf_op jit(solution)/shard_map/ppermute | solution.py:312
  83.5 2.2 %collective-permute-done.16.other = bf16[640,512]{1,0:T(8,128)(2,1)} collective-permute-done((bf16[640,512]{1,0:T(8,128)(2,1)S(1)}, bf16[640,512]{1,0:T(8,128)(2,1)}, u32[]{:S(2)}, u32[]{:S(2)}) %collective-permute-start.16) | collective-permute-done | bytes 655392 | tf_op jit(solution)/shard_map/ppermute | solution.py:312
  85.7 2.0 %copy-done.3 = f32[512,1792]{1,0:T(8,128)S(1)} copy-done((f32[512,1792]{1,0:T(8,128)S(1)}, f32[512,1792]{1,0:T(8,128)}, u32[]{:S(2)}) %copy-start.3) | copy-done | bytes 3670040
  87.8 11.8 %last.1 = (bf16[128,1792]{1,0:T(8,128)(2,1)S(1)}, bf16[128,1792]{1,0:T(8,128)(2,1)S(1)}, f32[1,1792]{1,0:T(1,128)S(1)}) custom-call(s32[2,1]{1,0:T(2,128)S(1)} %pad_add_fusion.blk, bf16[640,512]{1,0:T(8,128)(2,1)S(1)} %collective-permute-done.13.own, bf16[640,512]{1,0:T(8,128)(2,1)} %collective-permute-done.16.other, bf16[8192,1792]{1,0:T(8,128)(2,1)} %gw.3, ...), custom_call_target="tpu_custom_call" | custom-call | tf_op jit(solution)/shard_map/last/pallas_call | solution.py:220
  99.5 12.6 %backward.2 = f32[8,128,512]{2,1,0:T(8,128)S(1)} custom-call(bf16[128,1792]{1,0:T(8,128)(2,1)S(1)} %get-tuple-element.89.dg, bf16[128,1792]{1,0:T(8,128)(2,1)S(1)} %get-tuple-element.90.du, bf16[8192,1792]{1,0:T(8,128)(2,1)} %gw.3, bf16[8192,1792]{1,0:T(8,128)(2,1)} %uw.3), custom_call_target="tpu_custom_call" | custom-call | flops 3758096384 | bytes 31457280 | tf_op jit(solution)/shard_map/backward/pallas_call | solution.py:276
  112.4 2.5 %collective-permute-done.17 = f32[4,128,512]{2,1,0:T(8,128)S(1)} collective-permute-done((f32[4,128,512]{2,1,0:T(8,128)S(1)}, f32[4,128,512]{2,1,0:T(8,128)S(1)}, u32[]{:S(2)}, u32[]{:S(2)}) %collective-permute-start.17) | collective-permute-done | bytes 1048608 | tf_op jit(solution)/shard_map/ppermute | solution.py:312
  115.2 1.5 %collective-permute-start.18 = (bf16[4,128,512]{2,1,0:T(8,128)(2,1)S(1)}, bf16[4,128,512]{2,1,0:T(8,128)(2,1)S(1)}, u32[]{:S(2)}, u32[]{:S(2)}) collective-permute-start(bf16[4,128,512]{2,1,0:T(8,128)(2,1)S(1)} %fusion), channel_id=1, source_target_pairs={{0,2},{1,3},{2,0},{3,1},{4,6},{5,7},{6,4},{7,5},{8,10},{9,11},{10,... | collective-permute-start | bytes 1572872 | tf_op jit(solution)/shard_map/ppermute | solution.py:312
  116.8 12.6 %backward.3 = f32[8,128,512]{2,1,0:T(8,128)S(1)} custom-call(bf16[128,1792]{1,0:T(8,128)(2,1)S(1)} %get-tuple-element.89.dg, bf16[128,1792]{1,0:T(8,128)(2,1)S(1)} %get-tuple-element.90.du, bf16[8192,1792]{1,0:T(8,128)(2,1)} %gw.3, bf16[8192,1792]{1,0:T(8,128)(2,1)} %uw.3), custom_call_target="tpu_custom_call" | custom-call | flops 3758096384 | bytes 31457280 | tf_op jit(solution)/shard_map/backward/pallas_call | solution.py:276
  129.7 2.6 %collective-permute-done.19 = f32[4,128,512]{2,1,0:T(8,128)S(1)} collective-permute-done((f32[4,128,512]{2,1,0:T(8,128)S(1)}, f32[4,128,512]{2,1,0:T(8,128)S(1)}, u32[]{:S(2)}, u32[]{:S(2)}) %collective-permute-start.19) | collective-permute-done | bytes 1048608 | tf_op jit(solution)/shard_map/ppermute | solution.py:312
  132.7 2.8 %collective-permute-start.20 = (bf16[128,512]{1,0:T(8,128)(2,1)S(1)}, bf16[128,512]{1,0:T(8,128)(2,1)S(1)}, u32[]{:S(2)}, u32[]{:S(2)}) collective-permute-start(bf16[128,512]{1,0:T(8,128)(2,1)S(1)} %get-tuple-element.100), channel_id=1, source_target_pairs={{0,8},{1,9},{2,10},{3,11},{4,12},{5,13},{6,14},{7,15},{8,0},{9,1},... | collective-permute-start | bytes 393224 | tf_op jit(solution)/shard_map/ppermute | solution.py:312
  135.9 3.4 %collective-permute-start.22 = (bf16[128,512]{1,0:T(8,128)(2,1)S(1)}, bf16[128,512]{1,0:T(8,128)(2,1)S(1)}, u32[]{:S(2)}, u32[]{:S(2)}) collective-permute-start(bf16[128,512]{1,0:T(8,128)(2,1)S(1)} %get-tuple-element.101), channel_id=1, source_target_pairs={{0,12},{1,13},{2,14},{3,15},{4,0},{5,1},{6,2},{7,3},{8,4},{9,5},{1... | collective-permute-start | bytes 393224 | tf_op jit(solution)/shard_map/ppermute | solution.py:312
  139.9 5.7 %collective-permute-done.20 = bf16[128,512]{1,0:T(8,128)(2,1)S(1)} collective-permute-done((bf16[128,512]{1,0:T(8,128)(2,1)S(1)}, bf16[128,512]{1,0:T(8,128)(2,1)S(1)}, u32[]{:S(2)}, u32[]{:S(2)}) %collective-permute-start.20) | collective-permute-done | bytes 131104 | tf_op jit(solution)/shard_map/ppermute | solution.py:312
  (45 shorter events, 8.7 us)
Async XLA Ops:
  1.8 6.2 %collective-permute-start.2 = (bf16[640,512]{1,0:T(8,128)(2,1)S(1)}, bf16[640,512]{1,0:T(8,128)(2,1)S(1)}, u32[]{:S(2)}, u32[]{:S(2)}) collective-permute-start(bf16[640,512]{1,0:T(8,128)(2,1)S(1)} %pad_maximum_fusion.refs_0_), channel_id=1, source_target_pairs={{0,1},{1,0},{2,3},{3,2},{4,5},{5,4},{6,7},{7,6},{8,9},{9,8},{10,11... | collective-permute-start | bytes 1966088 | tf_op jit(solution)/shard_map/ppermute | solution.py:312
  2.3 18.0 %collective-permute-start = (bf16[640,512]{1,0:T(8,128)(2,1)S(1)}, bf16[640,512]{1,0:T(8,128)(2,1)S(1)}, u32[]{:S(2)}, u32[]{:S(2)}) collective-permute-start(bf16[640,512]{1,0:T(8,128)(2,1)S(1)} %pad_maximum_fusion.refs_0_), channel_id=1, source_target_pairs={{0,4},{1,5},{2,6},{3,7},{4,0},{5,1},{6,2},{7,3},{8,12},{9,13},{10,... | collective-permute-start | bytes 1966088 | tf_op jit(solution)/shard_map/ppermute | solution.py:312
  5.0 15.3 %collective-permute-start.1 = (bf16[640,512]{1,0:T(8,128)(2,1)S(1)}, bf16[640,512]{1,0:T(8,128)(2,1)}, u32[]{:S(2)}, u32[]{:S(2)}) collective-permute-start(bf16[640,512]{1,0:T(8,128)(2,1)S(1)} %pad_maximum_fusion.refs_0_), channel_id=1, source_target_pairs={{4,8},{5,9},{6,10},{7,11},{8,4},{9,5},{10,6},{11,7},{20,24},{21,25... | collective-permute-start | bytes 1966088 | tf_op jit(solution)/shard_map/ppermute | solution.py:312
  6.5 16.8 %collective-permute-start.5 = (bf16[640,512]{1,0:T(8,128)(2,1)S(1)}, bf16[640,512]{1,0:T(8,128)(2,1)S(1)}, u32[]{:S(2)}, u32[]{:S(2)}) collective-permute-start(bf16[640,512]{1,0:T(8,128)(2,1)S(1)} %pad_maximum_fusion.refs_0_), channel_id=1, source_target_pairs={{0,2},{1,3},{2,0},{3,1},{4,6},{5,7},{6,4},{7,5},{8,10},{9,11},{10,... | collective-permute-start | bytes 1966088 | tf_op jit(solution)/shard_map/ppermute | solution.py:312
  14.7 1.8 %copy-start = (f32[512,1792]{1,0:T(8,128)}, f32[512,1792]{1,0:T(8,128)S(1)}, u32[]{:S(2)}) copy-start(f32[512,1792]{1,0:T(8,128)S(1)} %get-tuple-element.58.refs_9_) | copy-start | bytes 11010052
  23.3 4.9 %collective-permute-start.6 = (bf16[640,512]{1,0:T(8,128)(2,1)S(1)}, bf16[640,512]{1,0:T(8,128)(2,1)}, u32[]{:S(2)}, u32[]{:S(2)}) collective-permute-start(bf16[640,512]{1,0:T(8,128)(2,1)S(1)} %collective-permute-done.refs_0_), channel_id=1, source_target_pairs={{0,1},{1,0},{2,3},{3,2},{4,5},{5,4},{6,7},{7,6},{8,9},{9,8},{10,11... | collective-permute-start | bytes 1966088 | tf_op jit(solution)/shard_map/ppermute | solution.py:312
  23.3 4.9 %collective-permute-start.7 = (bf16[640,512]{1,0:T(8,128)(2,1)S(1)}, bf16[640,512]{1,0:T(8,128)(2,1)}, u32[]{:S(2)}, u32[]{:S(2)}) collective-permute-start(bf16[640,512]{1,0:T(8,128)(2,1)S(1)} %collective-permute-done.5.refs_2_), channel_id=1, source_target_pairs={{0,1},{1,0},{2,3},{3,2},{4,5},{5,4},{6,7},{7,6},{8,9},{9,8},{10,11... | collective-permute-start | bytes 1966088 | tf_op jit(solution)/shard_map/ppermute | solution.py:312
  23.8 17.7 %collective-permute-start.3 = (bf16[640,512]{1,0:T(8,128)(2,1)S(1)}, bf16[640,512]{1,0:T(8,128)(2,1)}, u32[]{:S(2)}, u32[]{:S(2)}) collective-permute-start(bf16[640,512]{1,0:T(8,128)(2,1)S(1)} %collective-permute-done.refs_0_), channel_id=1, source_target_pairs={{4,8},{5,9},{6,10},{7,11},{8,4},{9,5},{10,6},{11,7},{20,24},{21,25... | collective-permute-start | bytes 1966088 | tf_op jit(solution)/shard_map/ppermute | solution.py:312
  25.3 20.3 %collective-permute-start.4 = (bf16[640,512]{1,0:T(8,128)(2,1)}, bf16[640,512]{1,0:T(8,128)(2,1)}, u32[]{:S(2)}, u32[]{:S(2)}) collective-permute-start(bf16[640,512]{1,0:T(8,128)(2,1)} %collective-permute-done.1), channel_id=1, source_target_pairs={{4,0},{5,1},{6,2},{7,3},{8,12},{9,13},{10,14},{11,15},{20,16},{21,... | collective-permute-start | bytes 1966088 | tf_op jit(solution)/shard_map/ppermute | solution.py:312
  26.6 20.1 %collective-permute-start.9 = (bf16[640,512]{1,0:T(8,128)(2,1)S(1)}, bf16[640,512]{1,0:T(8,128)(2,1)S(1)}, u32[]{:S(2)}, u32[]{:S(2)}) collective-permute-start(bf16[640,512]{1,0:T(8,128)(2,1)S(1)} %collective-permute-done.refs_0_), channel_id=1, source_target_pairs={{0,2},{1,3},{2,0},{3,1},{4,6},{5,7},{6,4},{7,5},{8,10},{9,11},{10,... | collective-permute-start | bytes 1966088 | tf_op jit(solution)/shard_map/ppermute | solution.py:312
  28.2 2.0 %copy-start.1 = (f32[512,1792]{1,0:T(8,128)S(1)}, f32[512,1792]{1,0:T(8,128)}, u32[]{:S(2)}) copy-start(f32[512,1792]{1,0:T(8,128)} %copy-done) | copy-start | bytes 11010052
  46.7 3.6 %collective-permute-start.10 = (bf16[640,512]{1,0:T(8,128)(2,1)S(1)}, bf16[640,512]{1,0:T(8,128)(2,1)S(1)}, u32[]{:S(2)}, u32[]{:S(2)}) collective-permute-start(bf16[640,512]{1,0:T(8,128)(2,1)S(1)} %broadcast_select_fusion.1.refs_0_), channel_id=1, source_target_pairs={{0,1},{1,0},{2,3},{3,2},{4,5},{5,4},{6,7},{7,6},{8,9},{9,8},{10,11... | collective-permute-start | bytes 1966088 | tf_op jit(solution)/shard_map/ppermute | solution.py:312
  46.8 3.5 %collective-permute-start.11 = (bf16[640,512]{1,0:T(8,128)(2,1)S(1)}, bf16[640,512]{1,0:T(8,128)(2,1)S(1)}, u32[]{:S(2)}, u32[]{:S(2)}) collective-permute-start(bf16[640,512]{1,0:T(8,128)(2,1)S(1)} %collective-permute-done.9.refs_2_), channel_id=1, source_target_pairs={{0,1},{1,0},{2,3},{3,2},{4,5},{5,4},{6,7},{7,6},{8,9},{9,8},{10,11... | collective-permute-start | bytes 1966088 | tf_op jit(solution)/shard_map/ppermute | solution.py:312
  47.3 18.8 %collective-permute-start.8 = (bf16[640,512]{1,0:T(8,128)(2,1)}, bf16[640,512]{1,0:T(8,128)(2,1)S(1)}, u32[]{:S(2)}, u32[]{:S(2)}) collective-permute-start(bf16[640,512]{1,0:T(8,128)(2,1)} %collective-permute-done.3), channel_id=1, source_target_pairs={{4,0},{5,1},{6,2},{7,3},{8,12},{9,13},{10,14},{11,15},{20,16},{21,... | collective-permute-start | bytes 1966088 | tf_op jit(solution)/shard_map/ppermute | solution.py:312
  48.8 17.4 %collective-permute-start.12 = (bf16[640,512]{1,0:T(8,128)(2,1)S(1)}, bf16[640,512]{1,0:T(8,128)(2,1)S(1)}, u32[]{:S(2)}, u32[]{:S(2)}) collective-permute-start(bf16[640,512]{1,0:T(8,128)(2,1)S(1)} %broadcast_select_fusion.1.refs_0_), channel_id=1, source_target_pairs={{0,2},{1,3},{2,0},{3,1},{4,6},{5,7},{6,4},{7,5},{8,10},{9,11},{10,... | collective-permute-start | bytes 1966088 | tf_op jit(solution)/shard_map/ppermute | solution.py:312
  66.2 17.3 %copy-start.5 = (s32[1792]{0:T(1024)S(1)}, s32[1792]{0:T(1024)}, u32[]{:S(2)}) copy-start(s32[1792]{0:T(1024)} %param.12) | copy-start | bytes 21508
  66.2 19.5 %copy-start.4 = (s32[128,1792]{1,0:T(8,128)S(1)}, s32[128,1792]{1,0:T(8,128)}, u32[]{:S(2)}) copy-start(s32[128,1792]{1,0:T(8,128)} %off.1) | copy-start | bytes 2752516
  66.2 2.2 %collective-permute-start.14 = (bf16[640,512]{1,0:T(8,128)(2,1)S(1)}, bf16[640,512]{1,0:T(8,128)(2,1)S(1)}, u32[]{:S(2)}, u32[]{:S(2)}) collective-permute-start(bf16[640,512]{1,0:T(8,128)(2,1)S(1)} %broadcast_select_fusion.refs_0_), channel_id=1, source_target_pairs={{0,1},{1,0},{2,3},{3,2},{4,5},{5,4},{6,7},{7,6},{8,9},{9,8},{10,11... | collective-permute-start | bytes 1966088 | tf_op jit(solution)/shard_map/ppermute | solution.py:312
  66.3 3.0 %collective-permute-start.15 = (bf16[640,512]{1,0:T(8,128)(2,1)S(1)}, bf16[640,512]{1,0:T(8,128)(2,1)S(1)}, u32[]{:S(2)}, u32[]{:S(2)}) collective-permute-start(bf16[640,512]{1,0:T(8,128)(2,1)S(1)} %collective-permute-done.12.refs_2_), channel_id=1, source_target_pairs={{0,1},{1,0},{2,3},{3,2},{4,5},{5,4},{6,7},{7,6},{8,9},{9,8},{10,11... | collective-permute-start | bytes 1966088 | tf_op jit(solution)/shard_map/ppermute | solution.py:312
  66.8 16.7 %collective-permute-start.13 = (bf16[640,512]{1,0:T(8,128)(2,1)S(1)}, bf16[640,512]{1,0:T(8,128)(2,1)S(1)}, u32[]{:S(2)}, u32[]{:S(2)}) collective-permute-start(bf16[640,512]{1,0:T(8,128)(2,1)S(1)} %broadcast_select_fusion.refs_0_), channel_id=1, source_target_pairs={{0,2},{1,3},{2,0},{3,1},{4,6},{5,7},{6,4},{7,5},{8,10},{9,11},{10,... | collective-permute-start | bytes 1966088 | tf_op jit(solution)/shard_map/ppermute | solution.py:312
  79.9 1.8 %copy-start.2 = (f32[512,1792]{1,0:T(8,128)}, f32[512,1792]{1,0:T(8,128)S(1)}, u32[]{:S(2)}) copy-start(f32[512,1792]{1,0:T(8,128)S(1)} %get-tuple-element.86.fi) | copy-start | bytes 11010052
  83.5 2.2 %collective-permute-start.16 = (bf16[640,512]{1,0:T(8,128)(2,1)S(1)}, bf16[640,512]{1,0:T(8,128)(2,1)}, u32[]{:S(2)}, u32[]{:S(2)}) collective-permute-start(bf16[640,512]{1,0:T(8,128)(2,1)S(1)} %collective-permute-done.13.own), channel_id=1, source_target_pairs={{0,1},{1,0},{2,3},{3,2},{4,5},{5,4},{6,7},{7,6},{8,9},{9,8},{10,11... | collective-permute-start | bytes 1966088 | tf_op jit(solution)/shard_map/ppermute | solution.py:312
  85.7 2.0 %copy-start.3 = (f32[512,1792]{1,0:T(8,128)S(1)}, f32[512,1792]{1,0:T(8,128)}, u32[]{:S(2)}) copy-start(f32[512,1792]{1,0:T(8,128)} %copy-done.2) | copy-start | bytes 11010052
  112.2 2.7 %collective-permute-start.17 = (f32[4,128,512]{2,1,0:T(8,128)S(1)}, f32[4,128,512]{2,1,0:T(8,128)S(1)}, u32[]{:S(2)}, u32[]{:S(2)}) collective-permute-start(f32[4,128,512]{2,1,0:T(8,128)S(1)} %slice.33), channel_id=1, source_target_pairs={{0,1},{1,0},{2,3},{3,2},{4,5},{5,4},{6,7},{7,6},{8,9},{9,8},{10,11... | collective-permute-start | bytes 3145736 | tf_op jit(solution)/shard_map/ppermute | solution.py:312
  115.2 14.4 %collective-permute-start.18 = (bf16[4,128,512]{2,1,0:T(8,128)(2,1)S(1)}, bf16[4,128,512]{2,1,0:T(8,128)(2,1)S(1)}, u32[]{:S(2)}, u32[]{:S(2)}) collective-permute-start(bf16[4,128,512]{2,1,0:T(8,128)(2,1)S(1)} %fusion), channel_id=1, source_target_pairs={{0,2},{1,3},{2,0},{3,1},{4,6},{5,7},{6,4},{7,5},{8,10},{9,11},{10,... | collective-permute-start | bytes 1572872 | tf_op jit(solution)/shard_map/ppermute | solution.py:312
  129.6 2.7 %collective-permute-start.19 = (f32[4,128,512]{2,1,0:T(8,128)S(1)}, f32[4,128,512]{2,1,0:T(8,128)S(1)}, u32[]{:S(2)}, u32[]{:S(2)}) collective-permute-start(f32[4,128,512]{2,1,0:T(8,128)S(1)} %get-tuple-element.93), channel_id=1, source_target_pairs={{0,1},{1,0},{2,3},{3,2},{4,5},{5,4},{6,7},{7,6},{8,9},{9,8},{10,11... | collective-permute-start | bytes 3145736 | tf_op jit(solution)/shard_map/ppermute | solution.py:312
  132.7 13.0 %collective-permute-start.20 = (bf16[128,512]{1,0:T(8,128)(2,1)S(1)}, bf16[128,512]{1,0:T(8,128)(2,1)S(1)}, u32[]{:S(2)}, u32[]{:S(2)}) collective-permute-start(bf16[128,512]{1,0:T(8,128)(2,1)S(1)} %get-tuple-element.100), channel_id=1, source_target_pairs={{0,8},{1,9},{2,10},{3,11},{4,12},{5,13},{6,14},{7,15},{8,0},{9,1},... | collective-permute-start | bytes 393224 | tf_op jit(solution)/shard_map/ppermute | solution.py:312
  135.5 10.1 %collective-permute-start.21 = (bf16[128,512]{1,0:T(8,128)(2,1)S(1)}, bf16[128,512]{1,0:T(8,128)(2,1)S(1)}, u32[]{:S(2)}, u32[]{:S(2)}) collective-permute-start(bf16[128,512]{1,0:T(8,128)(2,1)S(1)} %get-tuple-element.102), channel_id=1, source_target_pairs={{0,4},{1,5},{2,6},{3,7},{4,8},{5,9},{6,10},{7,11},{8,12},{9,13},{1... | collective-permute-start | bytes 393224 | tf_op jit(solution)/shard_map/ppermute | solution.py:312
  135.9 9.7 %collective-permute-start.22 = (bf16[128,512]{1,0:T(8,128)(2,1)S(1)}, bf16[128,512]{1,0:T(8,128)(2,1)S(1)}, u32[]{:S(2)}, u32[]{:S(2)}) collective-permute-start(bf16[128,512]{1,0:T(8,128)(2,1)S(1)} %get-tuple-element.101), channel_id=1, source_target_pairs={{0,12},{1,13},{2,14},{3,15},{4,0},{5,1},{6,2},{7,3},{8,4},{9,5},{1... | collective-permute-start | bytes 393224 | tf_op jit(solution)/shard_map/ppermute | solution.py:312

commit v4 on v3

--- a/solution.py
+++ b/solution.py
@@ -195,47 +195,84 @@
     )(gate, up, feed, levels.reshape(1, hidden), offsets)
 
 
-def last_call(pair, blocks, gate_w, up_w, down_w, sums, levels, offsets):
-    rows, width = pair[0].shape
+def last_call(pair, place, gate_w, up_w, down_w, sums, levels, offsets):
+    rows, half = pair[0].shape
+    width = 2 * half
     tok, hidden = sums[0].shape
     part = hidden_part(hidden)
     count = hidden // part
-
-    def kernel(blk, own, other, ga, gb, ua, ub, da, db, gi, ui, fi, lev, off, dg, du, gt, gate, up, feed):
-        now = lax.rem(pl.program_id(0), 2)
-        neuron_rows(gate.at[1 - now], up.at[1 - now], feed.at[1 - now], lev, off, dg, du, gt)
-        xo = own[rows - tok :, :]
-        xp = other[rows - tok :, :]
-        at = pl.ds(pl.multiple_of(jnp.minimum(pl.program_id(0), count - 1) * part, part), part)
-        gate[now] = gi[:, at] + dot(xo, ga[...]) + dot(xp, gb[...])
-        up[now] = ui[:, at] + dot(xo, ua[...]) + dot(xp, ub[...])
-        feed[now] = fi[:, at] + nt_dot(own[: rows - tok, :], da[...]) + nt_dot(other[: rows - tok, :], db[...])
-
-    ahead = lambda s: jnp.minimum(s, count - 1)
-    behind = lambda s: jnp.maximum(s - 1, 0)
-    whole = pl.BlockSpec((rows, width), lambda s, b: (0, 0))
-    spec = lambda k: pl.BlockSpec((width, part), lambda s, b: (b[k, 0], ahead(s)))
-    dspec = lambda k: pl.BlockSpec((part, width), lambda s, b: (ahead(s), b[k, 0]))
-    late = lambda n: pl.BlockSpec((n, part), lambda s, b: (0, behind(s)))
+    ahead = 2
+
+    def kernel(
+        own, other, gw, uw, dw, gi, ui, fi, lev, off, dg, du, gt,
+        feats, gbuf, ubuf, dbuf, gate, up, feed, dsem, wsem,
+    ):
+        me = lax.axis_index(AXIS)
+        core = lax.rem(me, 2)
+        at = pl.multiple_of(place(me) * width, width)
+        mine = pl.multiple_of(core * half, half)
+        theirs = pl.multiple_of(half - core * half, half)
+        data = (
+            pltpu.make_async_copy(own, feats.at[:, pl.ds(mine, half)], dsem.at[0]),
+            pltpu.make_async_copy(other, feats.at[:, pl.ds(theirs, half)], dsem.at[1]),
+        )
+
+        def loads(s):
+            cols = pl.ds(pl.multiple_of(s * part, part), part)
+            return (
+                pltpu.make_async_copy(gw.at[pl.ds(at, width), cols], gbuf.at[s], wsem.at[0, s]),
+                pltpu.make_async_copy(uw.at[pl.ds(at, width), cols], ubuf.at[s], wsem.at[1, s]),
+                pltpu.make_async_copy(dw.at[cols, pl.ds(at, width)], dbuf.at[s], wsem.at[2, s]),
+            )
+
+        for copy in data:
+            copy.start()
+        for s in range(min(ahead, count)):
+            for copy in loads(s):
+                copy.start()
+        for copy in data:
+            copy.wait()
+
+        def step(s, _):
+            @pl.when(s + ahead < count)
+            def _():
+                for copy in loads(s + ahead):
+                    copy.start()
+
+            cols = pl.ds(pl.multiple_of(s * part, part), part)
+            for copy in loads(s):
+                copy.wait()
+            gate[...] = gi[:, cols] + dot(feats[rows - tok :, :], gbuf[s])
+            up[...] = ui[:, cols] + dot(feats[rows - tok :, :], ubuf[s])
+            feed[...] = fi[:, cols] + nt_dot(feats[: rows - tok, :], dbuf[s])
+            neuron_rows(
+                gate, up, feed, lev.at[:, cols], off.at[:, cols], dg.at[:, cols], du.at[:, cols], gt.at[:, cols]
+            )
+            return 0
+
+        lax.fori_loop(0, count, step, 0)
+
+    any_spec = pl.BlockSpec(memory_space=pl.ANY)
+    vmem = pl.BlockSpec(memory_space=pltpu.VMEM)
     return pl.pallas_call(
         kernel,
-        grid_spec=pltpu.PrefetchScalarGridSpec(
-            num_scalar_prefetch=1,
-            grid=(count + 1,),
-            in_specs=[whole, whole, spec(0), spec(1), spec(0), spec(1), dspec(0), dspec(1)]
-            + [pl.BlockSpec(memory_space=pltpu.VMEM)] * 3
-            + [late(1), late(tok)],
-            out_specs=[late(tok), late(tok), late(1)],
-            scratch_shapes=[
-                pltpu.VMEM((2, tok, part), F32),
-                pltpu.VMEM((2, tok, part), F32),
-                pltpu.VMEM((2, rows - tok, part), F32),
-            ],
-        ),
+        in_specs=[any_spec] * 5 + [vmem] * 5,
+        out_specs=[vmem] * 3,
         out_shape=neuron_outs(tok, hidden),
+        scratch_shapes=[
+            pltpu.VMEM((rows, width), BF16),
+            pltpu.VMEM((count, width, part), BF16),
+            pltpu.VMEM((count, width, part), BF16),
+            pltpu.VMEM((count, part, width), BF16),
+            pltpu.VMEM((tok, part), F32),
+            pltpu.VMEM((tok, part), F32),
+            pltpu.VMEM((rows - tok, part), F32),
+            pltpu.SemaphoreType.DMA((2,)),
+            pltpu.SemaphoreType.DMA((3, count)),
+        ],
         compiler_params=pltpu.CompilerParams(vmem_limit_bytes=28 << 20),
         name="last",
-    )(blocks, *pair, gate_w, gate_w, up_w, up_w, down_w, down_w, *sums, levels.reshape(1, hidden), offsets)
+    )(*pair, gate_w, up_w, down_w, *sums, levels.reshape(1, hidden), offsets)
 
 
 def backward_call(dgate, dup, count, place, gate_w, up_w, width):
@@ -318,14 +355,8 @@
 def body_line(inputs, gate_w, up_w, down_w, cotangent, levels, offsets):
     steps, tok, width = cotangent.shape
     me = lax.axis_index(AXIS)
-    core = me % 2
-    chip = me // 2
     z = me // 4
     middle = (z == 1) | (z == 2)
-
-    def blocks_of(chips):
-        chips = jnp.stack(chips).astype(jnp.int32)
-        return jnp.stack([2 * chips + core, 2 * chips + 1 - core]).astype(jnp.int32)
 
     own = jnp.concatenate([cotangent.reshape(steps * tok, width), inputs], axis=0)
     def far(me):
@@ -370,7 +401,7 @@
     x3, sums = fence((x3, sums))
     x3_c = send(x3, CORE)
     dgate, dup, grad_threshold = last_call(
-        (x3, x3_c), blocks_of([chip ^ 1 ^ far(me)[1]]), gate_w, up_w, down_w, sums, levels, offsets
+        (x3, x3_c), lambda me: (me // 2) ^ 1 ^ far(me)[1], gate_w, up_w, down_w, sums, levels, offsets
     )
 
     turns = [2, 1, 3, 0]

time: 147 us -> 142 us (0.966)
  local copies, waits for them, and re-layouts: 7.97 us -> 4.16 us
  Pallas kernels: 76 us -> 73.1 us
  waiting for transfers between devices: 32 us -> 33.7 us
    unnamed x12 -> x8, local copies, waits for them, and re-layouts: 7.63 us -> 3.82 us
    pallas_call x1, Pallas kernels: 11.8 us -> 8.84 us  [last_call(): pl.pallas_call(kernel, in_specs=[any_spec] * 5 + [vmem] * 5, out_specs=[v...]
    ppermute x23, waiting for transfers between devices: 32 us -> 33.7 us  [send(): return lax.ppermute(piece, AXIS, moves)]
  transfers between devices with their start and end apart: 23 -> 23, of which waited for: 11 -> 11; matrix products, arithmetic and copies ran while one was open for 1% -> 1% of each run, Pallas kernels for 35% -> 37%
where the time goes in v4:
time: 142 us; the launch traced here: 141 us
  Pallas kernels  73.1 us (51%)
  waiting for transfers between devices  33.7 us (24%)
  starting transfers between devices  25.1 us (18%)
  other arithmetic  4.36 us (3%)
  local copies, waits for them, and re-layouts  4.16 us (3%)
    pallas_call x4, Pallas kernels, forward_call(): pl.pallas_call(kernel, in_specs=[any_spec] * (2 * count + 3) + [vmem] * l...  39.1 us
    ppermute x23, waiting for transfers between devices, send(): return lax.ppermute(piece, AXIS, moves)  33.7 us
    pallas_call x2, Pallas kernels, backward_call(): pl.pallas_call(kernel, in_specs=[vmem, vmem, any_spec, any_spec], out_spe...  25.2 us
    ppermute x23, starting transfers between devices, send(): return lax.ppermute(piece, AXIS, moves)  25.1 us
    pallas_call x1, Pallas kernels, last_call(): pl.pallas_call(kernel, in_specs=[any_spec] * 5 + [vmem] * 5, out_specs=[v...  8.84 us
    unnamed x8, local copies, waits for them, and re-layouts  3.82 us
  transfers between devices with their start and end apart: 23, of which 11 were waited for; matrix products, arithmetic and copies ran while one was open for 1% of the time, Pallas kernels for 37%

profile of v4, /device:TPU:0, one launch (start us, length us, event | category | flops | bytes accessed | tf_op | source)
XLA Modules:
  0.0 141.3 jit_solution(4462241114131529225)
XLA Ops:
  0.6 1.2 pad_maximum_fusion.refs_0_
  2.3 2.6 %collective-permute-start = (bf16[640,512]{1,0:T(8,128)(2,1)S(1)}, bf16[640,512]{1,0:T(8,128)(2,1)S(1)}, u32[]{:S(2)}, u32[]{:S(2)}) collective-permute-start(bf16[640,512]{1,0:T(8,128)(2,1)S(1)} %pad_maximum_fusion.refs_0_), channel_id=1, source_target_pairs={{0,4},{1,5},{2,6},{3,7},{4,0},{5,1},{6,2},{7,3},{8,12},{9,13},{10,... | collective-permute-start | bytes 1966088 | tf_op jit(solution)/shard_map/ppermute | solution.py:349
  5.0 1.5 %collective-permute-start.1 = (bf16[640,512]{1,0:T(8,128)(2,1)S(1)}, bf16[640,512]{1,0:T(8,128)(2,1)}, u32[]{:S(2)}, u32[]{:S(2)}) collective-permute-start(bf16[640,512]{1,0:T(8,128)(2,1)S(1)} %pad_maximum_fusion.refs_0_), channel_id=1, source_target_pairs={{4,8},{5,9},{6,10},{7,11},{8,4},{9,5},{10,6},{11,7},{20,24},{21,25... | collective-permute-start | bytes 1966088 | tf_op jit(solution)/shard_map/ppermute | solution.py:349
  6.5 1.5 %collective-permute-start.5 = (bf16[640,512]{1,0:T(8,128)(2,1)S(1)}, bf16[640,512]{1,0:T(8,128)(2,1)S(1)}, u32[]{:S(2)}, u32[]{:S(2)}) collective-permute-start(bf16[640,512]{1,0:T(8,128)(2,1)S(1)} %pad_maximum_fusion.refs_0_), channel_id=1, source_target_pairs={{0,2},{1,3},{2,0},{3,1},{4,6},{5,7},{6,4},{7,5},{8,10},{9,11},{10,... | collective-permute-start | bytes 1966088 | tf_op jit(solution)/shard_map/ppermute | solution.py:349
  8.0 6.7 %forward.4 = (f32[128,1792]{1,0:T(8,128)S(1)}, f32[128,1792]{1,0:T(8,128)S(1)}, f32[512,1792]{1,0:T(8,128)S(1)}) custom-call(bf16[640,512]{1,0:T(8,128)(2,1)S(1)} %pad_maximum_fusion.refs_0_, bf16[640,512]{1,0:T(8,128)(2,1)S(1)} %collective-permute-done.2.refs_1_, bf16[8192,1792]{1,0:T(8,128)(2,1)} %gw.5, bf16[8192,1792]{1,0:T(8,128)(2,1)} %uw.5, ...), custom_call_target="tpu_custom_call" | custom-call | flops 2818572288 | bytes 12320768 | tf_op jit(solution)/shard_map/forward/pallas_call | solution.py:99
  14.7 1.8 %copy-done = f32[512,1792]{1,0:T(8,128)} copy-done((f32[512,1792]{1,0:T(8,128)}, f32[512,1792]{1,0:T(8,128)S(1)}, u32[]{:S(2)}) %copy-start) | copy-done | bytes 3670040
  16.5 3.8 %collective-permute-done.refs_0_ = bf16[640,512]{1,0:T(8,128)(2,1)S(1)} collective-permute-done((bf16[640,512]{1,0:T(8,128)(2,1)S(1)}, bf16[640,512]{1,0:T(8,128)(2,1)S(1)}, u32[]{:S(2)}, u32[]{:S(2)}) %collective-permute-start) | collective-permute-done | bytes 655392 | tf_op jit(solution)/shard_map/ppermute | solution.py:349
  20.3 3.0 %collective-permute-done.5.refs_2_ = bf16[640,512]{1,0:T(8,128)(2,1)S(1)} collective-permute-done((bf16[640,512]{1,0:T(8,128)(2,1)S(1)}, bf16[640,512]{1,0:T(8,128)(2,1)S(1)}, u32[]{:S(2)}, u32[]{:S(2)}) %collective-permute-start.5) | collective-permute-done | bytes 655392 | tf_op jit(solution)/shard_map/ppermute | solution.py:349
  23.8 1.5 %collective-permute-start.3 = (bf16[640,512]{1,0:T(8,128)(2,1)S(1)}, bf16[640,512]{1,0:T(8,128)(2,1)}, u32[]{:S(2)}, u32[]{:S(2)}) collective-permute-start(bf16[640,512]{1,0:T(8,128)(2,1)S(1)} %collective-permute-done.refs_0_), channel_id=1, source_target_pairs={{4,8},{5,9},{6,10},{7,11},{8,4},{9,5},{10,6},{11,7},{20,24},{21,25... | collective-permute-start | bytes 1966088 | tf_op jit(solution)/shard_map/ppermute | solution.py:349
  25.3 1.3 collective-permute-start.4
  26.6 1.6 %collective-permute-start.9 = (bf16[640,512]{1,0:T(8,128)(2,1)S(1)}, bf16[640,512]{1,0:T(8,128)(2,1)S(1)}, u32[]{:S(2)}, u32[]{:S(2)}) collective-permute-start(bf16[640,512]{1,0:T(8,128)(2,1)S(1)} %collective-permute-done.refs_0_), channel_id=1, source_target_pairs={{0,2},{1,3},{2,0},{3,1},{4,6},{5,7},{6,4},{7,5},{8,10},{9,11},{10,... | collective-permute-start | bytes 1966088 | tf_op jit(solution)/shard_map/ppermute | solution.py:349
  28.2 2.0 %copy-done.1 = f32[512,1792]{1,0:T(8,128)S(1)} copy-done((f32[512,1792]{1,0:T(8,128)S(1)}, f32[512,1792]{1,0:T(8,128)}, u32[]{:S(2)}) %copy-start.1) | copy-done | bytes 3670040
  30.2 11.3 %forward.5 = (f32[128,1792]{1,0:T(8,128)S(1)}, f32[128,1792]{1,0:T(8,128)S(1)}, f32[512,1792]{1,0:T(8,128)S(1)}) custom-call(bf16[640,512]{1,0:T(8,128)(2,1)S(1)} %collective-permute-done.refs_0_, bf16[640,512]{1,0:T(8,128)(2,1)} %collective-permute-done.6.refs_1_, ...), custom_call_target="tpu_custom_call", output_to_operand_aliasing={{0}: (7, {}), {1}: (8, {}), {2}: (9, {})} | custom-call | flops 5637144576 | bytes 24641536 | tf_op jit(solution)/shard_map/forward/pallas_call | solution.py:99
  41.5 4.0 %collective-permute-done.4 = bf16[640,512]{1,0:T(8,128)(2,1)} collective-permute-done((bf16[640,512]{1,0:T(8,128)(2,1)}, bf16[640,512]{1,0:T(8,128)(2,1)}, u32[]{:S(2)}, u32[]{:S(2)}) %collective-permute-start.4) | collective-permute-done | bytes 655392 | tf_op jit(solution)/shard_map/ppermute | solution.py:349
  45.5 1.2 broadcast_select_fusion.1.refs_0_
  47.3 1.5 %collective-permute-start.8 = (bf16[640,512]{1,0:T(8,128)(2,1)}, bf16[640,512]{1,0:T(8,128)(2,1)S(1)}, u32[]{:S(2)}, u32[]{:S(2)}) collective-permute-start(bf16[640,512]{1,0:T(8,128)(2,1)} %collective-permute-done.3), channel_id=1, source_target_pairs={{4,0},{5,1},{6,2},{7,3},{8,12},{9,13},{10,14},{11,15},{20,16},{21,... | collective-permute-start | bytes 1966088 | tf_op jit(solution)/shard_map/ppermute | solution.py:349
  48.8 1.6 %collective-permute-start.12 = (bf16[640,512]{1,0:T(8,128)(2,1)S(1)}, bf16[640,512]{1,0:T(8,128)(2,1)S(1)}, u32[]{:S(2)}, u32[]{:S(2)}) collective-permute-start(bf16[640,512]{1,0:T(8,128)(2,1)S(1)} %broadcast_select_fusion.1.refs_0_), channel_id=1, source_target_pairs={{0,2},{1,3},{2,0},{3,1},{4,6},{5,7},{6,4},{7,5},{8,10},{9,11},{10,... | collective-permute-start | bytes 1966088 | tf_op jit(solution)/shard_map/ppermute | solution.py:349
  50.3 10.6 %forward.6 = (f32[128,1792]{1,0:T(8,128)S(1)}, f32[128,1792]{1,0:T(8,128)S(1)}, f32[512,1792]{1,0:T(8,128)S(1)}) custom-call(bf16[640,512]{1,0:T(8,128)(2,1)S(1)} %broadcast_select_fusion.1.refs_0_, bf16[640,512]{1,0:T(8,128)(2,1)S(1)} %collective-permute-done.10.refs_1_, ...), custom_call_target="tpu_custom_call", output_to_operand_aliasing={{0}: (7, {}), {1}: (8, {}), {2}: (9, {})} | custom-call | flops 5637144576 | bytes 24641536 | tf_op jit(solution)/shard_map/forward/pallas_call | solution.py:99
  60.9 5.2 %collective-permute-done.8 = bf16[640,512]{1,0:T(8,128)(2,1)S(1)} collective-permute-done((bf16[640,512]{1,0:T(8,128)(2,1)}, bf16[640,512]{1,0:T(8,128)(2,1)S(1)}, u32[]{:S(2)}, u32[]{:S(2)}) %collective-permute-start.8) | collective-permute-done | bytes 655392 | tf_op jit(solution)/shard_map/ppermute | solution.py:349
  66.8 1.5 %collective-permute-start.13 = (bf16[640,512]{1,0:T(8,128)(2,1)S(1)}, bf16[640,512]{1,0:T(8,128)(2,1)S(1)}, u32[]{:S(2)}, u32[]{:S(2)}) collective-permute-start(bf16[640,512]{1,0:T(8,128)(2,1)S(1)} %broadcast_select_fusion.refs_0_), channel_id=1, source_target_pairs={{0,2},{1,3},{2,0},{3,1},{4,6},{5,7},{6,4},{7,5},{8,10},{9,11},{10,... | collective-permute-start | bytes 1966088 | tf_op jit(solution)/shard_map/ppermute | solution.py:349
  69.3 10.6 %forward.7 = (f32[128,1792]{1,0:T(8,128)S(1)}, f32[128,1792]{1,0:T(8,128)S(1)}, f32[512,1792]{1,0:T(8,128)S(1)}) custom-call(bf16[640,512]{1,0:T(8,128)(2,1)S(1)} %broadcast_select_fusion.refs_0_, bf16[640,512]{1,0:T(8,128)(2,1)S(1)} %collective-permute-done.14.refs_1_, ...), custom_call_target="tpu_custom_call", output_to_operand_aliasing={{0}: (7, {}), {1}: (8, {}), {2}: (9, {})} | custom-call | flops 5637144576 | bytes 24641536 | tf_op jit(solution)/shard_map/forward/pallas_call | solution.py:99
  79.9 3.6 %collective-permute-done.13.own = bf16[640,512]{1,0:T(8,128)(2,1)S(1)} collective-permute-done((bf16[640,512]{1,0:T(8,128)(2,1)S(1)}, bf16[640,512]{1,0:T(8,128)(2,1)S(1)}, u32[]{:S(2)}, u32[]{:S(2)}) %collective-permute-start.13) | collective-permute-done | bytes 655392 | tf_op jit(solution)/shard_map/ppermute | solution.py:349
  83.5 2.1 %collective-permute-done.16.other = bf16[640,512]{1,0:T(8,128)(2,1)S(1)} collective-permute-done((bf16[640,512]{1,0:T(8,128)(2,1)S(1)}, bf16[640,512]{1,0:T(8,128)(2,1)S(1)}, u32[]{:S(2)}, u32[]{:S(2)}) %collective-permute-start.16) | collective-permute-done | bytes 655392 | tf_op jit(solution)/shard_map/ppermute | solution.py:349
  85.6 8.8 %last.1 = (bf16[128,1792]{1,0:T(8,128)(2,1)S(1)}, bf16[128,1792]{1,0:T(8,128)(2,1)S(1)}, f32[1,1792]{1,0:T(1,128)S(1)}) custom-call(bf16[640,512]{1,0:T(8,128)(2,1)S(1)} %collective-permute-done.13.own, bf16[640,512]{1,0:T(8,128)(2,1)S(1)} %collective-permute-done.16.other, bf16[8192,1792]{1,0:T(8,128)(2,1)} %gw.5, bf16[8192,1792]{1,0:T(8,128)(2,1)} %uw.5, ...), custom_call_target="tpu_custom_call" | custom-call | tf_op jit(solution)/shard_map/last/pallas_call | solution.py:257
  94.4 12.6 %backward.2 = f32[8,128,512]{2,1,0:T(8,128)S(1)} custom-call(bf16[128,1792]{1,0:T(8,128)(2,1)S(1)} %get-tuple-element.89.dg, bf16[128,1792]{1,0:T(8,128)(2,1)S(1)} %get-tuple-element.90.du, bf16[8192,1792]{1,0:T(8,128)(2,1)} %gw.5, bf16[8192,1792]{1,0:T(8,128)(2,1)} %uw.5), custom_call_target="tpu_custom_call" | custom-call | flops 3758096384 | bytes 31457280 | tf_op jit(solution)/shard_map/backward/pallas_call | solution.py:313
  107.3 2.5 %collective-permute-done.17 = f32[4,128,512]{2,1,0:T(8,128)S(1)} collective-permute-done((f32[4,128,512]{2,1,0:T(8,128)S(1)}, f32[4,128,512]{2,1,0:T(8,128)S(1)}, u32[]{:S(2)}, u32[]{:S(2)}) %collective-permute-start.17) | collective-permute-done | bytes 1048608 | tf_op jit(solution)/shard_map/ppermute | solution.py:349
  110.1 1.6 %collective-permute-start.18 = (bf16[4,128,512]{2,1,0:T(8,128)(2,1)S(1)}, bf16[4,128,512]{2,1,0:T(8,128)(2,1)S(1)}, u32[]{:S(2)}, u32[]{:S(2)}) collective-permute-start(bf16[4,128,512]{2,1,0:T(8,128)(2,1)S(1)} %fusion), channel_id=1, source_target_pairs={{0,2},{1,3},{2,0},{3,1},{4,6},{5,7},{6,4},{7,5},{8,10},{9,11},{10,... | collective-permute-start | bytes 1572872 | tf_op jit(solution)/shard_map/ppermute | solution.py:349
  111.7 12.6 %backward.3 = f32[8,128,512]{2,1,0:T(8,128)S(1)} custom-call(bf16[128,1792]{1,0:T(8,128)(2,1)S(1)} %get-tuple-element.89.dg, bf16[128,1792]{1,0:T(8,128)(2,1)S(1)} %get-tuple-element.90.du, bf16[8192,1792]{1,0:T(8,128)(2,1)} %gw.5, bf16[8192,1792]{1,0:T(8,128)(2,1)} %uw.5), custom_call_target="tpu_custom_call" | custom-call | flops 3758096384 | bytes 31457280 | tf_op jit(solution)/shard_map/backward/pallas_call | solution.py:313
  124.6 2.6 %collective-permute-done.19 = f32[4,128,512]{2,1,0:T(8,128)S(1)} collective-permute-done((f32[4,128,512]{2,1,0:T(8,128)S(1)}, f32[4,128,512]{2,1,0:T(8,128)S(1)}, u32[]{:S(2)}, u32[]{:S(2)}) %collective-permute-start.19) | collective-permute-done | bytes 1048608 | tf_op jit(solution)/shard_map/ppermute | solution.py:349
  127.6 2.8 %collective-permute-start.20 = (bf16[128,512]{1,0:T(8,128)(2,1)S(1)}, bf16[128,512]{1,0:T(8,128)(2,1)S(1)}, u32[]{:S(2)}, u32[]{:S(2)}) collective-permute-start(bf16[128,512]{1,0:T(8,128)(2,1)S(1)} %get-tuple-element.100), channel_id=1, source_target_pairs={{0,8},{1,9},{2,10},{3,11},{4,12},{5,13},{6,14},{7,15},{8,0},{9,1},... | collective-permute-start | bytes 393224 | tf_op jit(solution)/shard_map/ppermute | solution.py:349
  130.9 3.4 %collective-permute-start.22 = (bf16[128,512]{1,0:T(8,128)(2,1)S(1)}, bf16[128,512]{1,0:T(8,128)(2,1)S(1)}, u32[]{:S(2)}, u32[]{:S(2)}) collective-permute-start(bf16[128,512]{1,0:T(8,128)(2,1)S(1)} %get-tuple-element.101), channel_id=1, source_target_pairs={{0,12},{1,13},{2,14},{3,15},{4,0},{5,1},{6,2},{7,3},{8,4},{9,5},{1... | collective-permute-start | bytes 393224 | tf_op jit(solution)/shard_map/ppermute | solution.py:349
  134.9 5.7 %collective-permute-done.20 = bf16[128,512]{1,0:T(8,128)(2,1)S(1)} collective-permute-done((bf16[128,512]{1,0:T(8,128)(2,1)S(1)}, bf16[128,512]{1,0:T(8,128)(2,1)S(1)}, u32[]{:S(2)}, u32[]{:S(2)}) %collective-permute-start.20) | collective-permute-done | bytes 131104 | tf_op jit(solution)/shard_map/ppermute | solution.py:349
  (40 shorter events, 6.3 us)
Async XLA Ops:
  1.8 6.2 %collective-permute-start.2 = (bf16[640,512]{1,0:T(8,128)(2,1)S(1)}, bf16[640,512]{1,0:T(8,128)(2,1)S(1)}, u32[]{:S(2)}, u32[]{:S(2)}) collective-permute-start(bf16[640,512]{1,0:T(8,128)(2,1)S(1)} %pad_maximum_fusion.refs_0_), channel_id=1, source_target_pairs={{0,1},{1,0},{2,3},{3,2},{4,5},{5,4},{6,7},{7,6},{8,9},{9,8},{10,11... | collective-permute-start | bytes 1966088 | tf_op jit(solution)/shard_map/ppermute | solution.py:349
  2.3 18.0 %collective-permute-start = (bf16[640,512]{1,0:T(8,128)(2,1)S(1)}, bf16[640,512]{1,0:T(8,128)(2,1)S(1)}, u32[]{:S(2)}, u32[]{:S(2)}) collective-permute-start(bf16[640,512]{1,0:T(8,128)(2,1)S(1)} %pad_maximum_fusion.refs_0_), channel_id=1, source_target_pairs={{0,4},{1,5},{2,6},{3,7},{4,0},{5,1},{6,2},{7,3},{8,12},{9,13},{10,... | collective-permute-start | bytes 1966088 | tf_op jit(solution)/shard_map/ppermute | solution.py:349
  5.0 15.3 %collective-permute-start.1 = (bf16[640,512]{1,0:T(8,128)(2,1)S(1)}, bf16[640,512]{1,0:T(8,128)(2,1)}, u32[]{:S(2)}, u32[]{:S(2)}) collective-permute-start(bf16[640,512]{1,0:T(8,128)(2,1)S(1)} %pad_maximum_fusion.refs_0_), channel_id=1, source_target_pairs={{4,8},{5,9},{6,10},{7,11},{8,4},{9,5},{10,6},{11,7},{20,24},{21,25... | collective-permute-start | bytes 1966088 | tf_op jit(solution)/shard_map/ppermute | solution.py:349
  6.5 16.8 %collective-permute-start.5 = (bf16[640,512]{1,0:T(8,128)(2,1)S(1)}, bf16[640,512]{1,0:T(8,128)(2,1)S(1)}, u32[]{:S(2)}, u32[]{:S(2)}) collective-permute-start(bf16[640,512]{1,0:T(8,128)(2,1)S(1)} %pad_maximum_fusion.refs_0_), channel_id=1, source_target_pairs={{0,2},{1,3},{2,0},{3,1},{4,6},{5,7},{6,4},{7,5},{8,10},{9,11},{10,... | collective-permute-start | bytes 1966088 | tf_op jit(solution)/shard_map/ppermute | solution.py:349
  14.7 1.8 %copy-start = (f32[512,1792]{1,0:T(8,128)}, f32[512,1792]{1,0:T(8,128)S(1)}, u32[]{:S(2)}) copy-start(f32[512,1792]{1,0:T(8,128)S(1)} %get-tuple-element.58.refs_9_) | copy-start | bytes 11010052
  23.3 4.9 %collective-permute-start.6 = (bf16[640,512]{1,0:T(8,128)(2,1)S(1)}, bf16[640,512]{1,0:T(8,128)(2,1)}, u32[]{:S(2)}, u32[]{:S(2)}) collective-permute-start(bf16[640,512]{1,0:T(8,128)(2,1)S(1)} %collective-permute-done.refs_0_), channel_id=1, source_target_pairs={{0,1},{1,0},{2,3},{3,2},{4,5},{5,4},{6,7},{7,6},{8,9},{9,8},{10,11... | collective-permute-start | bytes 1966088 | tf_op jit(solution)/shard_map/ppermute | solution.py:349
  23.3 4.9 %collective-permute-start.7 = (bf16[640,512]{1,0:T(8,128)(2,1)S(1)}, bf16[640,512]{1,0:T(8,128)(2,1)}, u32[]{:S(2)}, u32[]{:S(2)}) collective-permute-start(bf16[640,512]{1,0:T(8,128)(2,1)S(1)} %collective-permute-done.5.refs_2_), channel_id=1, source_target_pairs={{0,1},{1,0},{2,3},{3,2},{4,5},{5,4},{6,7},{7,6},{8,9},{9,8},{10,11... | collective-permute-start | bytes 1966088 | tf_op jit(solution)/shard_map/ppermute | solution.py:349
  23.8 17.7 %collective-permute-start.3 = (bf16[640,512]{1,0:T(8,128)(2,1)S(1)}, bf16[640,512]{1,0:T(8,128)(2,1)}, u32[]{:S(2)}, u32[]{:S(2)}) collective-permute-start(bf16[640,512]{1,0:T(8,128)(2,1)S(1)} %collective-permute-done.refs_0_), channel_id=1, source_target_pairs={{4,8},{5,9},{6,10},{7,11},{8,4},{9,5},{10,6},{11,7},{20,24},{21,25... | collective-permute-start | bytes 1966088 | tf_op jit(solution)/shard_map/ppermute | solution.py:349
  25.3 20.2 %collective-permute-start.4 = (bf16[640,512]{1,0:T(8,128)(2,1)}, bf16[640,512]{1,0:T(8,128)(2,1)}, u32[]{:S(2)}, u32[]{:S(2)}) collective-permute-start(bf16[640,512]{1,0:T(8,128)(2,1)} %collective-permute-done.1), channel_id=1, source_target_pairs={{4,0},{5,1},{6,2},{7,3},{8,12},{9,13},{10,14},{11,15},{20,16},{21,... | collective-permute-start | bytes 1966088 | tf_op jit(solution)/shard_map/ppermute | solution.py:349
  26.6 20.1 %collective-permute-start.9 = (bf16[640,512]{1,0:T(8,128)(2,1)S(1)}, bf16[640,512]{1,0:T(8,128)(2,1)S(1)}, u32[]{:S(2)}, u32[]{:S(2)}) collective-permute-start(bf16[640,512]{1,0:T(8,128)(2,1)S(1)} %collective-permute-done.refs_0_), channel_id=1, source_target_pairs={{0,2},{1,3},{2,0},{3,1},{4,6},{5,7},{6,4},{7,5},{8,10},{9,11},{10,... | collective-permute-start | bytes 1966088 | tf_op jit(solution)/shard_map/ppermute | solution.py:349
  28.2 2.0 %copy-start.1 = (f32[512,1792]{1,0:T(8,128)S(1)}, f32[512,1792]{1,0:T(8,128)}, u32[]{:S(2)}) copy-start(f32[512,1792]{1,0:T(8,128)} %copy-done) | copy-start | bytes 11010052
  46.7 3.6 %collective-permute-start.10 = (bf16[640,512]{1,0:T(8,128)(2,1)S(1)}, bf16[640,512]{1,0:T(8,128)(2,1)S(1)}, u32[]{:S(2)}, u32[]{:S(2)}) collective-permute-start(bf16[640,512]{1,0:T(8,128)(2,1)S(1)} %broadcast_select_fusion.1.refs_0_), channel_id=1, source_target_pairs={{0,1},{1,0},{2,3},{3,2},{4,5},{5,4},{6,7},{7,6},{8,9},{9,8},{10,11... | collective-permute-start | bytes 1966088 | tf_op jit(solution)/shard_map/ppermute | solution.py:349
  46.8 3.5 %collective-permute-start.11 = (bf16[640,512]{1,0:T(8,128)(2,1)S(1)}, bf16[640,512]{1,0:T(8,128)(2,1)S(1)}, u32[]{:S(2)}, u32[]{:S(2)}) collective-permute-start(bf16[640,512]{1,0:T(8,128)(2,1)S(1)} %collective-permute-done.9.refs_2_), channel_id=1, source_target_pairs={{0,1},{1,0},{2,3},{3,2},{4,5},{5,4},{6,7},{7,6},{8,9},{9,8},{10,11... | collective-permute-start | bytes 1966088 | tf_op jit(solution)/shard_map/ppermute | solution.py:349
  47.3 18.8 %collective-permute-start.8 = (bf16[640,512]{1,0:T(8,128)(2,1)}, bf16[640,512]{1,0:T(8,128)(2,1)S(1)}, u32[]{:S(2)}, u32[]{:S(2)}) collective-permute-start(bf16[640,512]{1,0:T(8,128)(2,1)} %collective-permute-done.3), channel_id=1, source_target_pairs={{4,0},{5,1},{6,2},{7,3},{8,12},{9,13},{10,14},{11,15},{20,16},{21,... | collective-permute-start | bytes 1966088 | tf_op jit(solution)/shard_map/ppermute | solution.py:349
  48.8 17.4 %collective-permute-start.12 = (bf16[640,512]{1,0:T(8,128)(2,1)S(1)}, bf16[640,512]{1,0:T(8,128)(2,1)S(1)}, u32[]{:S(2)}, u32[]{:S(2)}) collective-permute-start(bf16[640,512]{1,0:T(8,128)(2,1)S(1)} %broadcast_select_fusion.1.refs_0_), channel_id=1, source_target_pairs={{0,2},{1,3},{2,0},{3,1},{4,6},{5,7},{6,4},{7,5},{8,10},{9,11},{10,... | collective-permute-start | bytes 1966088 | tf_op jit(solution)/shard_map/ppermute | solution.py:349
  66.2 17.3 %copy-start.3 = (s32[1792]{0:T(1024)S(1)}, s32[1792]{0:T(1024)}, u32[]{:S(2)}) copy-start(s32[1792]{0:T(1024)} %param.12) | copy-start | bytes 21508
  66.2 19.4 %copy-start.2 = (s32[128,1792]{1,0:T(8,128)S(1)}, s32[128,1792]{1,0:T(8,128)}, u32[]{:S(2)}) copy-start(s32[128,1792]{1,0:T(8,128)} %off.1) | copy-start | bytes 2752516
  66.2 2.2 %collective-permute-start.14 = (bf16[640,512]{1,0:T(8,128)(2,1)S(1)}, bf16[640,512]{1,0:T(8,128)(2,1)S(1)}, u32[]{:S(2)}, u32[]{:S(2)}) collective-permute-start(bf16[640,512]{1,0:T(8,128)(2,1)S(1)} %broadcast_select_fusion.refs_0_), channel_id=1, source_target_pairs={{0,1},{1,0},{2,3},{3,2},{4,5},{5,4},{6,7},{7,6},{8,9},{9,8},{10,11... | collective-permute-start | bytes 1966088 | tf_op jit(solution)/shard_map/ppermute | solution.py:349
  66.3 3.0 %collective-permute-start.15 = (bf16[640,512]{1,0:T(8,128)(2,1)S(1)}, bf16[640,512]{1,0:T(8,128)(2,1)S(1)}, u32[]{:S(2)}, u32[]{:S(2)}) collective-permute-start(bf16[640,512]{1,0:T(8,128)(2,1)S(1)} %collective-permute-done.12.refs_2_), channel_id=1, source_target_pairs={{0,1},{1,0},{2,3},{3,2},{4,5},{5,4},{6,7},{7,6},{8,9},{9,8},{10,11... | collective-permute-start | bytes 1966088 | tf_op jit(solution)/shard_map/ppermute | solution.py:349
  66.8 16.7 %collective-permute-start.13 = (bf16[640,512]{1,0:T(8,128)(2,1)S(1)}, bf16[640,512]{1,0:T(8,128)(2,1)S(1)}, u32[]{:S(2)}, u32[]{:S(2)}) collective-permute-start(bf16[640,512]{1,0:T(8,128)(2,1)S(1)} %broadcast_select_fusion.refs_0_), channel_id=1, source_target_pairs={{0,2},{1,3},{2,0},{3,1},{4,6},{5,7},{6,4},{7,5},{8,10},{9,11},{10,... | collective-permute-start | bytes 1966088 | tf_op jit(solution)/shard_map/ppermute | solution.py:349
  83.5 2.1 %collective-permute-start.16 = (bf16[640,512]{1,0:T(8,128)(2,1)S(1)}, bf16[640,512]{1,0:T(8,128)(2,1)S(1)}, u32[]{:S(2)}, u32[]{:S(2)}) collective-permute-start(bf16[640,512]{1,0:T(8,128)(2,1)S(1)} %collective-permute-done.13.own), channel_id=1, source_target_pairs={{0,1},{1,0},{2,3},{3,2},{4,5},{5,4},{6,7},{7,6},{8,9},{9,8},{10,11... | collective-permute-start | bytes 1966088 | tf_op jit(solution)/shard_map/ppermute | solution.py:349
  107.1 2.7 %collective-permute-start.17 = (f32[4,128,512]{2,1,0:T(8,128)S(1)}, f32[4,128,512]{2,1,0:T(8,128)S(1)}, u32[]{:S(2)}, u32[]{:S(2)}) collective-permute-start(f32[4,128,512]{2,1,0:T(8,128)S(1)} %slice.33), channel_id=1, source_target_pairs={{0,1},{1,0},{2,3},{3,2},{4,5},{5,4},{6,7},{7,6},{8,9},{9,8},{10,11... | collective-permute-start | bytes 3145736 | tf_op jit(solution)/shard_map/ppermute | solution.py:349
  110.1 14.4 %collective-permute-start.18 = (bf16[4,128,512]{2,1,0:T(8,128)(2,1)S(1)}, bf16[4,128,512]{2,1,0:T(8,128)(2,1)S(1)}, u32[]{:S(2)}, u32[]{:S(2)}) collective-permute-start(bf16[4,128,512]{2,1,0:T(8,128)(2,1)S(1)} %fusion), channel_id=1, source_target_pairs={{0,2},{1,3},{2,0},{3,1},{4,6},{5,7},{6,4},{7,5},{8,10},{9,11},{10,... | collective-permute-start | bytes 1572872 | tf_op jit(solution)/shard_map/ppermute | solution.py:349
  124.5 2.7 %collective-permute-start.19 = (f32[4,128,512]{2,1,0:T(8,128)S(1)}, f32[4,128,512]{2,1,0:T(8,128)S(1)}, u32[]{:S(2)}, u32[]{:S(2)}) collective-permute-start(f32[4,128,512]{2,1,0:T(8,128)S(1)} %get-tuple-element.93), channel_id=1, source_target_pairs={{0,1},{1,0},{2,3},{3,2},{4,5},{5,4},{6,7},{7,6},{8,9},{9,8},{10,11... | collective-permute-start | bytes 3145736 | tf_op jit(solution)/shard_map/ppermute | solution.py:349
  127.6 13.0 %collective-permute-start.20 = (bf16[128,512]{1,0:T(8,128)(2,1)S(1)}, bf16[128,512]{1,0:T(8,128)(2,1)S(1)}, u32[]{:S(2)}, u32[]{:S(2)}) collective-permute-start(bf16[128,512]{1,0:T(8,128)(2,1)S(1)} %get-tuple-element.100), channel_id=1, source_target_pairs={{0,8},{1,9},{2,10},{3,11},{4,12},{5,13},{6,14},{7,15},{8,0},{9,1},... | collective-permute-start | bytes 393224 | tf_op jit(solution)/shard_map/ppermute | solution.py:349
  130.4 10.1 %collective-permute-start.21 = (bf16[128,512]{1,0:T(8,128)(2,1)S(1)}, bf16[128,512]{1,0:T(8,128)(2,1)S(1)}, u32[]{:S(2)}, u32[]{:S(2)}) collective-permute-start(bf16[128,512]{1,0:T(8,128)(2,1)S(1)} %get-tuple-element.102), channel_id=1, source_target_pairs={{0,4},{1,5},{2,6},{3,7},{4,8},{5,9},{6,10},{7,11},{8,12},{9,13},{1... | collective-permute-start | bytes 393224 | tf_op jit(solution)/shard_map/ppermute | solution.py:349
  130.9 9.7 %collective-permute-start.22 = (bf16[128,512]{1,0:T(8,128)(2,1)S(1)}, bf16[128,512]{1,0:T(8,128)(2,1)S(1)}, u32[]{:S(2)}, u32[]{:S(2)}) collective-permute-start(bf16[128,512]{1,0:T(8,128)(2,1)S(1)} %get-tuple-element.101), channel_id=1, source_target_pairs={{0,12},{1,13},{2,14},{3,15},{4,0},{5,1},{6,2},{7,3},{8,4},{9,5},{1... | collective-permute-start | bytes 393224 | tf_op jit(solution)/shard_map/ppermute | solution.py:349

commit v5 on v4

--- a/solution.py
+++ b/solution.py
@@ -341,8 +341,8 @@
 CROSS = [(i, i ^ 2) for i in range(16)]
 
 
-def around(turn, flip):
-    return [(i, ((i // 4 + turn) % 4 * 4 + i % 4) ^ (2 * flip)) for i in range(16)]
+def exchanged(turn):
+    return [(i, i ^ (4 * turn)) for i in range(16)]
 
 
 def send(piece, moves):
@@ -404,13 +404,12 @@
         (x3, x3_c), lambda me: (me // 2) ^ 1 ^ far(me)[1], gate_w, up_w, down_w, sums, levels, offsets
     )
 
-    turns = [2, 1, 3, 0]
+    turns = [3, 2, 1, 0]
 
     def partial(dgate, dup, flip):
         def place(me, i):
             k = lax.rem(i, 4)
-            turn = jnp.where(k == 0, 2, jnp.where(k == 2, 3, jnp.where(k == 3, 0, 1)))
-            to = (lax.rem(me // 4 + turn, 4) * 2 + lax.rem(me // 2, 2)) ^ flip
+            to = (((me // 4) ^ (3 - k)) * 2 + lax.rem(me // 2, 2)) ^ flip
             return 2 * to + jnp.where(i < 4, 1 - lax.rem(me, 2), lax.rem(me, 2))
 
         out = backward_call(dgate, dup, 8, place, gate_w, up_w, width)
@@ -426,7 +425,7 @@
     grad_input = column[3]
     column = column.astype(BF16)
     for k in range(3):
-        grad_input = grad_input + send(column[k], around(turns[k], 0)).astype(F32)
+        grad_input = grad_input + send(column[k], exchanged(turns[k])).astype(F32)
     return grad_input, grad_threshold.reshape(-1)
 
 

time: 142 us -> 144 us (1.014)
  waiting for transfers between devices: 33.7 us -> 38 us
  starting transfers between devices: 25.1 us -> 22.9 us
    ppermute x23, waiting for transfers between devices: 33.7 us -> 38 us  [send(): return lax.ppermute(piece, AXIS, moves)]
    ppermute x23, starting transfers between devices: 25.1 us -> 22.9 us  [send(): return lax.ppermute(piece, AXIS, moves)]
  transfers between devices with their start and end apart: 23 -> 23, of which waited for: 11 -> 12; matrix products, arithmetic and copies ran while one was open for 1% -> 1% of each run, Pallas kernels for 37% -> 36%
where the time goes in v5:
time: 144 us; the launch traced here: 143 us
  Pallas kernels  73 us (51%)
  waiting for transfers between devices  38 us (26%)
  starting transfers between devices  22.9 us (16%)
  other arithmetic  4.36 us (3%)
  local copies, waits for them, and re-layouts  4.16 us (3%)
    pallas_call x4, Pallas kernels, forward_call(): pl.pallas_call(kernel, in_specs=[any_spec] * (2 * count + 3) + [vmem] * l...  39.1 us
    ppermute x23, waiting for transfers between devices, send(): return lax.ppermute(piece, AXIS, moves)  38 us
    pallas_call x2, Pallas kernels, backward_call(): pl.pallas_call(kernel, in_specs=[vmem, vmem, any_spec, any_spec], out_spe...  25 us
    ppermute x23, starting transfers between devices, send(): return lax.ppermute(piece, AXIS, moves)  22.9 us
    pallas_call x1, Pallas kernels, last_call(): pl.pallas_call(kernel, in_specs=[any_spec] * 5 + [vmem] * 5, out_specs=[v...  8.84 us
    unnamed x8, local copies, waits for them, and re-layouts  3.82 us
  transfers between devices with their start and end apart: 23, of which 12 were waited for; matrix products, arithmetic and copies ran while one was open for 1% of the time, Pallas kernels for 36%

profile of v5, /device:TPU:0, one launch (start us, length us, event | category | flops | bytes accessed | tf_op | source)
XLA Modules:
  0.0 143.3 jit_solution(3820804563992275964)
XLA Ops:
  0.6 1.2 pad_maximum_fusion.refs_0_
  2.3 2.6 %collective-permute-start = (bf16[640,512]{1,0:T(8,128)(2,1)S(1)}, bf16[640,512]{1,0:T(8,128)(2,1)S(1)}, u32[]{:S(2)}, u32[]{:S(2)}) collective-permute-start(bf16[640,512]{1,0:T(8,128)(2,1)S(1)} %pad_maximum_fusion.refs_0_), channel_id=1, source_target_pairs={{0,4},{1,5},{2,6},{3,7},{4,0},{5,1},{6,2},{7,3},{8,12},{9,13},{10,... | collective-permute-start | bytes 1966088 | tf_op jit(solution)/shard_map/ppermute | solution.py:349
  5.0 1.5 %collective-permute-start.1 = (bf16[640,512]{1,0:T(8,128)(2,1)S(1)}, bf16[640,512]{1,0:T(8,128)(2,1)}, u32[]{:S(2)}, u32[]{:S(2)}) collective-permute-start(bf16[640,512]{1,0:T(8,128)(2,1)S(1)} %pad_maximum_fusion.refs_0_), channel_id=1, source_target_pairs={{4,8},{5,9},{6,10},{7,11},{8,4},{9,5},{10,6},{11,7},{20,24},{21,25... | collective-permute-start | bytes 1966088 | tf_op jit(solution)/shard_map/ppermute | solution.py:349
  6.5 1.5 %collective-permute-start.5 = (bf16[640,512]{1,0:T(8,128)(2,1)S(1)}, bf16[640,512]{1,0:T(8,128)(2,1)S(1)}, u32[]{:S(2)}, u32[]{:S(2)}) collective-permute-start(bf16[640,512]{1,0:T(8,128)(2,1)S(1)} %pad_maximum_fusion.refs_0_), channel_id=1, source_target_pairs={{0,2},{1,3},{2,0},{3,1},{4,6},{5,7},{6,4},{7,5},{8,10},{9,11},{10,... | collective-permute-start | bytes 1966088 | tf_op jit(solution)/shard_map/ppermute | solution.py:349
  8.0 6.7 %forward.4 = (f32[128,1792]{1,0:T(8,128)S(1)}, f32[128,1792]{1,0:T(8,128)S(1)}, f32[512,1792]{1,0:T(8,128)S(1)}) custom-call(bf16[640,512]{1,0:T(8,128)(2,1)S(1)} %pad_maximum_fusion.refs_0_, bf16[640,512]{1,0:T(8,128)(2,1)S(1)} %collective-permute-done.2.refs_1_, bf16[8192,1792]{1,0:T(8,128)(2,1)} %gw.5, bf16[8192,1792]{1,0:T(8,128)(2,1)} %uw.5, ...), custom_call_target="tpu_custom_call" | custom-call | flops 2818572288 | bytes 12320768 | tf_op jit(solution)/shard_map/forward/pallas_call | solution.py:99
  14.7 1.8 %copy-done = f32[512,1792]{1,0:T(8,128)} copy-done((f32[512,1792]{1,0:T(8,128)}, f32[512,1792]{1,0:T(8,128)S(1)}, u32[]{:S(2)}) %copy-start) | copy-done | bytes 3670040
  16.5 3.8 %collective-permute-done.refs_0_ = bf16[640,512]{1,0:T(8,128)(2,1)S(1)} collective-permute-done((bf16[640,512]{1,0:T(8,128)(2,1)S(1)}, bf16[640,512]{1,0:T(8,128)(2,1)S(1)}, u32[]{:S(2)}, u32[]{:S(2)}) %collective-permute-start) | collective-permute-done | bytes 655392 | tf_op jit(solution)/shard_map/ppermute | solution.py:349
  20.3 3.0 %collective-permute-done.5.refs_2_ = bf16[640,512]{1,0:T(8,128)(2,1)S(1)} collective-permute-done((bf16[640,512]{1,0:T(8,128)(2,1)S(1)}, bf16[640,512]{1,0:T(8,128)(2,1)S(1)}, u32[]{:S(2)}, u32[]{:S(2)}) %collective-permute-start.5) | collective-permute-done | bytes 655392 | tf_op jit(solution)/shard_map/ppermute | solution.py:349
  23.8 1.5 %collective-permute-start.3 = (bf16[640,512]{1,0:T(8,128)(2,1)S(1)}, bf16[640,512]{1,0:T(8,128)(2,1)}, u32[]{:S(2)}, u32[]{:S(2)}) collective-permute-start(bf16[640,512]{1,0:T(8,128)(2,1)S(1)} %collective-permute-done.refs_0_), channel_id=1, source_target_pairs={{4,8},{5,9},{6,10},{7,11},{8,4},{9,5},{10,6},{11,7},{20,24},{21,25... | collective-permute-start | bytes 1966088 | tf_op jit(solution)/shard_map/ppermute | solution.py:349
  25.3 1.3 collective-permute-start.4
  26.6 1.6 %collective-permute-start.9 = (bf16[640,512]{1,0:T(8,128)(2,1)S(1)}, bf16[640,512]{1,0:T(8,128)(2,1)S(1)}, u32[]{:S(2)}, u32[]{:S(2)}) collective-permute-start(bf16[640,512]{1,0:T(8,128)(2,1)S(1)} %collective-permute-done.refs_0_), channel_id=1, source_target_pairs={{0,2},{1,3},{2,0},{3,1},{4,6},{5,7},{6,4},{7,5},{8,10},{9,11},{10,... | collective-permute-start | bytes 1966088 | tf_op jit(solution)/shard_map/ppermute | solution.py:349
  28.2 2.0 %copy-done.1 = f32[512,1792]{1,0:T(8,128)S(1)} copy-done((f32[512,1792]{1,0:T(8,128)S(1)}, f32[512,1792]{1,0:T(8,128)}, u32[]{:S(2)}) %copy-start.1) | copy-done | bytes 3670040
  30.2 11.3 %forward.5 = (f32[128,1792]{1,0:T(8,128)S(1)}, f32[128,1792]{1,0:T(8,128)S(1)}, f32[512,1792]{1,0:T(8,128)S(1)}) custom-call(bf16[640,512]{1,0:T(8,128)(2,1)S(1)} %collective-permute-done.refs_0_, bf16[640,512]{1,0:T(8,128)(2,1)} %collective-permute-done.6.refs_1_, ...), custom_call_target="tpu_custom_call", output_to_operand_aliasing={{0}: (7, {}), {1}: (8, {}), {2}: (9, {})} | custom-call | flops 5637144576 | bytes 24641536 | tf_op jit(solution)/shard_map/forward/pallas_call | solution.py:99
  41.5 4.0 %collective-permute-done.4 = bf16[640,512]{1,0:T(8,128)(2,1)} collective-permute-done((bf16[640,512]{1,0:T(8,128)(2,1)}, bf16[640,512]{1,0:T(8,128)(2,1)}, u32[]{:S(2)}, u32[]{:S(2)}) %collective-permute-start.4) | collective-permute-done | bytes 655392 | tf_op jit(solution)/shard_map/ppermute | solution.py:349
  47.3 1.5 %collective-permute-start.8 = (bf16[640,512]{1,0:T(8,128)(2,1)}, bf16[640,512]{1,0:T(8,128)(2,1)S(1)}, u32[]{:S(2)}, u32[]{:S(2)}) collective-permute-start(bf16[640,512]{1,0:T(8,128)(2,1)} %collective-permute-done.3), channel_id=1, source_target_pairs={{4,0},{5,1},{6,2},{7,3},{8,12},{9,13},{10,14},{11,15},{20,16},{21,... | collective-permute-start | bytes 1966088 | tf_op jit(solution)/shard_map/ppermute | solution.py:349
  48.8 1.6 %collective-permute-start.12 = (bf16[640,512]{1,0:T(8,128)(2,1)S(1)}, bf16[640,512]{1,0:T(8,128)(2,1)S(1)}, u32[]{:S(2)}, u32[]{:S(2)}) collective-permute-start(bf16[640,512]{1,0:T(8,128)(2,1)S(1)} %broadcast_select_fusion.1.refs_0_), channel_id=1, source_target_pairs={{0,2},{1,3},{2,0},{3,1},{4,6},{5,7},{6,4},{7,5},{8,10},{9,11},{10,... | collective-permute-start | bytes 1966088 | tf_op jit(solution)/shard_map/ppermute | solution.py:349
  50.3 10.6 %forward.6 = (f32[128,1792]{1,0:T(8,128)S(1)}, f32[128,1792]{1,0:T(8,128)S(1)}, f32[512,1792]{1,0:T(8,128)S(1)}) custom-call(bf16[640,512]{1,0:T(8,128)(2,1)S(1)} %broadcast_select_fusion.1.refs_0_, bf16[640,512]{1,0:T(8,128)(2,1)S(1)} %collective-permute-done.10.refs_1_, ...), custom_call_target="tpu_custom_call", output_to_operand_aliasing={{0}: (7, {}), {1}: (8, {}), {2}: (9, {})} | custom-call | flops 5637144576 | bytes 24641536 | tf_op jit(solution)/shard_map/forward/pallas_call | solution.py:99
  60.9 5.2 %collective-permute-done.8 = bf16[640,512]{1,0:T(8,128)(2,1)S(1)} collective-permute-done((bf16[640,512]{1,0:T(8,128)(2,1)}, bf16[640,512]{1,0:T(8,128)(2,1)S(1)}, u32[]{:S(2)}, u32[]{:S(2)}) %collective-permute-start.8) | collective-permute-done | bytes 655392 | tf_op jit(solution)/shard_map/ppermute | solution.py:349
  66.8 1.5 %collective-permute-start.13 = (bf16[640,512]{1,0:T(8,128)(2,1)S(1)}, bf16[640,512]{1,0:T(8,128)(2,1)S(1)}, u32[]{:S(2)}, u32[]{:S(2)}) collective-permute-start(bf16[640,512]{1,0:T(8,128)(2,1)S(1)} %broadcast_select_fusion.refs_0_), channel_id=1, source_target_pairs={{0,2},{1,3},{2,0},{3,1},{4,6},{5,7},{6,4},{7,5},{8,10},{9,11},{10,... | collective-permute-start | bytes 1966088 | tf_op jit(solution)/shard_map/ppermute | solution.py:349
  69.3 10.6 %forward.7 = (f32[128,1792]{1,0:T(8,128)S(1)}, f32[128,1792]{1,0:T(8,128)S(1)}, f32[512,1792]{1,0:T(8,128)S(1)}) custom-call(bf16[640,512]{1,0:T(8,128)(2,1)S(1)} %broadcast_select_fusion.refs_0_, bf16[640,512]{1,0:T(8,128)(2,1)S(1)} %collective-permute-done.14.refs_1_, ...), custom_call_target="tpu_custom_call", output_to_operand_aliasing={{0}: (7, {}), {1}: (8, {}), {2}: (9, {})} | custom-call | flops 5637144576 | bytes 24641536 | tf_op jit(solution)/shard_map/forward/pallas_call | solution.py:99
  79.9 3.6 %collective-permute-done.13.own = bf16[640,512]{1,0:T(8,128)(2,1)S(1)} collective-permute-done((bf16[640,512]{1,0:T(8,128)(2,1)S(1)}, bf16[640,512]{1,0:T(8,128)(2,1)S(1)}, u32[]{:S(2)}, u32[]{:S(2)}) %collective-permute-start.13) | collective-permute-done | bytes 655392 | tf_op jit(solution)/shard_map/ppermute | solution.py:349
  83.5 2.1 %collective-permute-done.16.other = bf16[640,512]{1,0:T(8,128)(2,1)S(1)} collective-permute-done((bf16[640,512]{1,0:T(8,128)(2,1)S(1)}, bf16[640,512]{1,0:T(8,128)(2,1)S(1)}, u32[]{:S(2)}, u32[]{:S(2)}) %collective-permute-start.16) | collective-permute-done | bytes 655392 | tf_op jit(solution)/shard_map/ppermute | solution.py:349
  85.6 8.8 %last.1 = (bf16[128,1792]{1,0:T(8,128)(2,1)S(1)}, bf16[128,1792]{1,0:T(8,128)(2,1)S(1)}, f32[1,1792]{1,0:T(1,128)S(1)}) custom-call(bf16[640,512]{1,0:T(8,128)(2,1)S(1)} %collective-permute-done.13.own, bf16[640,512]{1,0:T(8,128)(2,1)S(1)} %collective-permute-done.16.other, bf16[8192,1792]{1,0:T(8,128)(2,1)} %gw.5, bf16[8192,1792]{1,0:T(8,128)(2,1)} %uw.5, ...), custom_call_target="tpu_custom_call" | custom-call | tf_op jit(solution)/shard_map/last/pallas_call | solution.py:257
  94.4 12.6 %backward.2 = f32[8,128,512]{2,1,0:T(8,128)S(1)} custom-call(bf16[128,1792]{1,0:T(8,128)(2,1)S(1)} %get-tuple-element.89.dg, bf16[128,1792]{1,0:T(8,128)(2,1)S(1)} %get-tuple-element.90.du, bf16[8192,1792]{1,0:T(8,128)(2,1)} %gw.5, bf16[8192,1792]{1,0:T(8,128)(2,1)} %uw.5), custom_call_target="tpu_custom_call" | custom-call | flops 3758096384 | bytes 31457280 | tf_op jit(solution)/shard_map/backward/pallas_call | solution.py:313
  107.3 2.5 %collective-permute-done.17 = f32[4,128,512]{2,1,0:T(8,128)S(1)} collective-permute-done((f32[4,128,512]{2,1,0:T(8,128)S(1)}, f32[4,128,512]{2,1,0:T(8,128)S(1)}, u32[]{:S(2)}, u32[]{:S(2)}) %collective-permute-start.17) | collective-permute-done | bytes 1048608 | tf_op jit(solution)/shard_map/ppermute | solution.py:349
  110.1 1.6 %collective-permute-start.18 = (bf16[4,128,512]{2,1,0:T(8,128)(2,1)S(1)}, bf16[4,128,512]{2,1,0:T(8,128)(2,1)S(1)}, u32[]{:S(2)}, u32[]{:S(2)}) collective-permute-start(bf16[4,128,512]{2,1,0:T(8,128)(2,1)S(1)} %fusion), channel_id=1, source_target_pairs={{0,2},{1,3},{2,0},{3,1},{4,6},{5,7},{6,4},{7,5},{8,10},{9,11},{10,... | collective-permute-start | bytes 1572872 | tf_op jit(solution)/shard_map/ppermute | solution.py:349
  111.6 12.5 %backward.3 = f32[8,128,512]{2,1,0:T(8,128)S(1)} custom-call(bf16[128,1792]{1,0:T(8,128)(2,1)S(1)} %get-tuple-element.89.dg, bf16[128,1792]{1,0:T(8,128)(2,1)S(1)} %get-tuple-element.90.du, bf16[8192,1792]{1,0:T(8,128)(2,1)} %gw.5, bf16[8192,1792]{1,0:T(8,128)(2,1)} %uw.5), custom_call_target="tpu_custom_call" | custom-call | flops 3758096384 | bytes 31457280 | tf_op jit(solution)/shard_map/backward/pallas_call | solution.py:313
  124.5 2.6 %collective-permute-done.19 = f32[4,128,512]{2,1,0:T(8,128)S(1)} collective-permute-done((f32[4,128,512]{2,1,0:T(8,128)S(1)}, f32[4,128,512]{2,1,0:T(8,128)S(1)}, u32[]{:S(2)}, u32[]{:S(2)}) %collective-permute-start.19) | collective-permute-done | bytes 1048608 | tf_op jit(solution)/shard_map/ppermute | solution.py:349
  127.5 2.7 %collective-permute-start.20 = (bf16[128,512]{1,0:T(8,128)(2,1)S(1)}, bf16[128,512]{1,0:T(8,128)(2,1)S(1)}, u32[]{:S(2)}, u32[]{:S(2)}) collective-permute-start(bf16[128,512]{1,0:T(8,128)(2,1)S(1)} %get-tuple-element.100), channel_id=1, source_target_pairs={{0,12},{1,13},{2,14},{3,15},{4,8},{5,9},{6,10},{7,11},{8,4},{9,5},... | collective-permute-start | bytes 393224 | tf_op jit(solution)/shard_map/ppermute | solution.py:349
  130.6 1.3 collective-permute-start.22
  132.6 3.2 %collective-permute-done.20 = bf16[128,512]{1,0:T(8,128)(2,1)S(1)} collective-permute-done((bf16[128,512]{1,0:T(8,128)(2,1)S(1)}, bf16[128,512]{1,0:T(8,128)(2,1)S(1)}, u32[]{:S(2)}, u32[]{:S(2)}) %collective-permute-start.20) | collective-permute-done | bytes 131104 | tf_op jit(solution)/shard_map/ppermute | solution.py:349
  135.8 6.7 %collective-permute-done.21 = bf16[128,512]{1,0:T(8,128)(2,1)S(1)} collective-permute-done((bf16[128,512]{1,0:T(8,128)(2,1)S(1)}, bf16[128,512]{1,0:T(8,128)(2,1)S(1)}, u32[]{:S(2)}, u32[]{:S(2)}) %collective-permute-start.21) | collective-permute-done | bytes 131104 | tf_op jit(solution)/shard_map/ppermute | solution.py:349
  (40 shorter events, 7.5 us)
Async XLA Ops:
  1.8 6.2 %collective-permute-start.2 = (bf16[640,512]{1,0:T(8,128)(2,1)S(1)}, bf16[640,512]{1,0:T(8,128)(2,1)S(1)}, u32[]{:S(2)}, u32[]{:S(2)}) collective-permute-start(bf16[640,512]{1,0:T(8,128)(2,1)S(1)} %pad_maximum_fusion.refs_0_), channel_id=1, source_target_pairs={{0,1},{1,0},{2,3},{3,2},{4,5},{5,4},{6,7},{7,6},{8,9},{9,8},{10,11... | collective-permute-start | bytes 1966088 | tf_op jit(solution)/shard_map/ppermute | solution.py:349
  2.3 18.0 %collective-permute-start = (bf16[640,512]{1,0:T(8,128)(2,1)S(1)}, bf16[640,512]{1,0:T(8,128)(2,1)S(1)}, u32[]{:S(2)}, u32[]{:S(2)}) collective-permute-start(bf16[640,512]{1,0:T(8,128)(2,1)S(1)} %pad_maximum_fusion.refs_0_), channel_id=1, source_target_pairs={{0,4},{1,5},{2,6},{3,7},{4,0},{5,1},{6,2},{7,3},{8,12},{9,13},{10,... | collective-permute-start | bytes 1966088 | tf_op jit(solution)/shard_map/ppermute | solution.py:349
  5.0 15.3 %collective-permute-start.1 = (bf16[640,512]{1,0:T(8,128)(2,1)S(1)}, bf16[640,512]{1,0:T(8,128)(2,1)}, u32[]{:S(2)}, u32[]{:S(2)}) collective-permute-start(bf16[640,512]{1,0:T(8,128)(2,1)S(1)} %pad_maximum_fusion.refs_0_), channel_id=1, source_target_pairs={{4,8},{5,9},{6,10},{7,11},{8,4},{9,5},{10,6},{11,7},{20,24},{21,25... | collective-permute-start | bytes 1966088 | tf_op jit(solution)/shard_map/ppermute | solution.py:349
  6.5 16.8 %collective-permute-start.5 = (bf16[640,512]{1,0:T(8,128)(2,1)S(1)}, bf16[640,512]{1,0:T(8,128)(2,1)S(1)}, u32[]{:S(2)}, u32[]{:S(2)}) collective-permute-start(bf16[640,512]{1,0:T(8,128)(2,1)S(1)} %pad_maximum_fusion.refs_0_), channel_id=1, source_target_pairs={{0,2},{1,3},{2,0},{3,1},{4,6},{5,7},{6,4},{7,5},{8,10},{9,11},{10,... | collective-permute-start | bytes 1966088 | tf_op jit(solution)/shard_map/ppermute | solution.py:349
  14.7 1.8 %copy-start = (f32[512,1792]{1,0:T(8,128)}, f32[512,1792]{1,0:T(8,128)S(1)}, u32[]{:S(2)}) copy-start(f32[512,1792]{1,0:T(8,128)S(1)} %get-tuple-element.58.refs_9_) | copy-start | bytes 11010052
  23.3 4.9 %collective-permute-start.6 = (bf16[640,512]{1,0:T(8,128)(2,1)S(1)}, bf16[640,512]{1,0:T(8,128)(2,1)}, u32[]{:S(2)}, u32[]{:S(2)}) collective-permute-start(bf16[640,512]{1,0:T(8,128)(2,1)S(1)} %collective-permute-done.refs_0_), channel_id=1, source_target_pairs={{0,1},{1,0},{2,3},{3,2},{4,5},{5,4},{6,7},{7,6},{8,9},{9,8},{10,11... | collective-permute-start | bytes 1966088 | tf_op jit(solution)/shard_map/ppermute | solution.py:349
  23.3 4.9 %collective-permute-start.7 = (bf16[640,512]{1,0:T(8,128)(2,1)S(1)}, bf16[640,512]{1,0:T(8,128)(2,1)}, u32[]{:S(2)}, u32[]{:S(2)}) collective-permute-start(bf16[640,512]{1,0:T(8,128)(2,1)S(1)} %collective-permute-done.5.refs_2_), channel_id=1, source_target_pairs={{0,1},{1,0},{2,3},{3,2},{4,5},{5,4},{6,7},{7,6},{8,9},{9,8},{10,11... | collective-permute-start | bytes 1966088 | tf_op jit(solution)/shard_map/ppermute | solution.py:349
  23.8 17.7 %collective-permute-start.3 = (bf16[640,512]{1,0:T(8,128)(2,1)S(1)}, bf16[640,512]{1,0:T(8,128)(2,1)}, u32[]{:S(2)}, u32[]{:S(2)}) collective-permute-start(bf16[640,512]{1,0:T(8,128)(2,1)S(1)} %collective-permute-done.refs_0_), channel_id=1, source_target_pairs={{4,8},{5,9},{6,10},{7,11},{8,4},{9,5},{10,6},{11,7},{20,24},{21,25... | collective-permute-start | bytes 1966088 | tf_op jit(solution)/shard_map/ppermute | solution.py:349
  25.3 20.2 %collective-permute-start.4 = (bf16[640,512]{1,0:T(8,128)(2,1)}, bf16[640,512]{1,0:T(8,128)(2,1)}, u32[]{:S(2)}, u32[]{:S(2)}) collective-permute-start(bf16[640,512]{1,0:T(8,128)(2,1)} %collective-permute-done.1), channel_id=1, source_target_pairs={{4,0},{5,1},{6,2},{7,3},{8,12},{9,13},{10,14},{11,15},{20,16},{21,... | collective-permute-start | bytes 1966088 | tf_op jit(solution)/shard_map/ppermute | solution.py:349
  26.6 20.1 %collective-permute-start.9 = (bf16[640,512]{1,0:T(8,128)(2,1)S(1)}, bf16[640,512]{1,0:T(8,128)(2,1)S(1)}, u32[]{:S(2)}, u32[]{:S(2)}) collective-permute-start(bf16[640,512]{1,0:T(8,128)(2,1)S(1)} %collective-permute-done.refs_0_), channel_id=1, source_target_pairs={{0,2},{1,3},{2,0},{3,1},{4,6},{5,7},{6,4},{7,5},{8,10},{9,11},{10,... | collective-permute-start | bytes 1966088 | tf_op jit(solution)/shard_map/ppermute | solution.py:349
  28.2 2.0 %copy-start.1 = (f32[512,1792]{1,0:T(8,128)S(1)}, f32[512,1792]{1,0:T(8,128)}, u32[]{:S(2)}) copy-start(f32[512,1792]{1,0:T(8,128)} %copy-done) | copy-start | bytes 11010052
  46.7 3.6 %collective-permute-start.10 = (bf16[640,512]{1,0:T(8,128)(2,1)S(1)}, bf16[640,512]{1,0:T(8,128)(2,1)S(1)}, u32[]{:S(2)}, u32[]{:S(2)}) collective-permute-start(bf16[640,512]{1,0:T(8,128)(2,1)S(1)} %broadcast_select_fusion.1.refs_0_), channel_id=1, source_target_pairs={{0,1},{1,0},{2,3},{3,2},{4,5},{5,4},{6,7},{7,6},{8,9},{9,8},{10,11... | collective-permute-start | bytes 1966088 | tf_op jit(solution)/shard_map/ppermute | solution.py:349
  46.8 3.5 %collective-permute-start.11 = (bf16[640,512]{1,0:T(8,128)(2,1)S(1)}, bf16[640,512]{1,0:T(8,128)(2,1)S(1)}, u32[]{:S(2)}, u32[]{:S(2)}) collective-permute-start(bf16[640,512]{1,0:T(8,128)(2,1)S(1)} %collective-permute-done.9.refs_2_), channel_id=1, source_target_pairs={{0,1},{1,0},{2,3},{3,2},{4,5},{5,4},{6,7},{7,6},{8,9},{9,8},{10,11... | collective-permute-start | bytes 1966088 | tf_op jit(solution)/shard_map/ppermute | solution.py:349
  47.3 18.8 %collective-permute-start.8 = (bf16[640,512]{1,0:T(8,128)(2,1)}, bf16[640,512]{1,0:T(8,128)(2,1)S(1)}, u32[]{:S(2)}, u32[]{:S(2)}) collective-permute-start(bf16[640,512]{1,0:T(8,128)(2,1)} %collective-permute-done.3), channel_id=1, source_target_pairs={{4,0},{5,1},{6,2},{7,3},{8,12},{9,13},{10,14},{11,15},{20,16},{21,... | collective-permute-start | bytes 1966088 | tf_op jit(solution)/shard_map/ppermute | solution.py:349
  48.8 17.4 %collective-permute-start.12 = (bf16[640,512]{1,0:T(8,128)(2,1)S(1)}, bf16[640,512]{1,0:T(8,128)(2,1)S(1)}, u32[]{:S(2)}, u32[]{:S(2)}) collective-permute-start(bf16[640,512]{1,0:T(8,128)(2,1)S(1)} %broadcast_select_fusion.1.refs_0_), channel_id=1, source_target_pairs={{0,2},{1,3},{2,0},{3,1},{4,6},{5,7},{6,4},{7,5},{8,10},{9,11},{10,... | collective-permute-start | bytes 1966088 | tf_op jit(solution)/shard_map/ppermute | solution.py:349
  66.2 17.3 %copy-start.3 = (s32[1792]{0:T(1024)S(1)}, s32[1792]{0:T(1024)}, u32[]{:S(2)}) copy-start(s32[1792]{0:T(1024)} %param.12) | copy-start | bytes 21508
  66.2 19.4 %copy-start.2 = (s32[128,1792]{1,0:T(8,128)S(1)}, s32[128,1792]{1,0:T(8,128)}, u32[]{:S(2)}) copy-start(s32[128,1792]{1,0:T(8,128)} %off.1) | copy-start | bytes 2752516
  66.2 2.2 %collective-permute-start.14 = (bf16[640,512]{1,0:T(8,128)(2,1)S(1)}, bf16[640,512]{1,0:T(8,128)(2,1)S(1)}, u32[]{:S(2)}, u32[]{:S(2)}) collective-permute-start(bf16[640,512]{1,0:T(8,128)(2,1)S(1)} %broadcast_select_fusion.refs_0_), channel_id=1, source_target_pairs={{0,1},{1,0},{2,3},{3,2},{4,5},{5,4},{6,7},{7,6},{8,9},{9,8},{10,11... | collective-permute-start | bytes 1966088 | tf_op jit(solution)/shard_map/ppermute | solution.py:349
  66.3 3.0 %collective-permute-start.15 = (bf16[640,512]{1,0:T(8,128)(2,1)S(1)}, bf16[640,512]{1,0:T(8,128)(2,1)S(1)}, u32[]{:S(2)}, u32[]{:S(2)}) collective-permute-start(bf16[640,512]{1,0:T(8,128)(2,1)S(1)} %collective-permute-done.12.refs_2_), channel_id=1, source_target_pairs={{0,1},{1,0},{2,3},{3,2},{4,5},{5,4},{6,7},{7,6},{8,9},{9,8},{10,11... | collective-permute-start | bytes 1966088 | tf_op jit(solution)/shard_map/ppermute | solution.py:349
  66.8 16.7 %collective-permute-start.13 = (bf16[640,512]{1,0:T(8,128)(2,1)S(1)}, bf16[640,512]{1,0:T(8,128)(2,1)S(1)}, u32[]{:S(2)}, u32[]{:S(2)}) collective-permute-start(bf16[640,512]{1,0:T(8,128)(2,1)S(1)} %broadcast_select_fusion.refs_0_), channel_id=1, source_target_pairs={{0,2},{1,3},{2,0},{3,1},{4,6},{5,7},{6,4},{7,5},{8,10},{9,11},{10,... | collective-permute-start | bytes 1966088 | tf_op jit(solution)/shard_map/ppermute | solution.py:349
  83.5 2.1 %collective-permute-start.16 = (bf16[640,512]{1,0:T(8,128)(2,1)S(1)}, bf16[640,512]{1,0:T(8,128)(2,1)S(1)}, u32[]{:S(2)}, u32[]{:S(2)}) collective-permute-start(bf16[640,512]{1,0:T(8,128)(2,1)S(1)} %collective-permute-done.13.own), channel_id=1, source_target_pairs={{0,1},{1,0},{2,3},{3,2},{4,5},{5,4},{6,7},{7,6},{8,9},{9,8},{10,11... | collective-permute-start | bytes 1966088 | tf_op jit(solution)/shard_map/ppermute | solution.py:349
  107.1 2.7 %collective-permute-start.17 = (f32[4,128,512]{2,1,0:T(8,128)S(1)}, f32[4,128,512]{2,1,0:T(8,128)S(1)}, u32[]{:S(2)}, u32[]{:S(2)}) collective-permute-start(f32[4,128,512]{2,1,0:T(8,128)S(1)} %slice.33), channel_id=1, source_target_pairs={{0,1},{1,0},{2,3},{3,2},{4,5},{5,4},{6,7},{7,6},{8,9},{9,8},{10,11... | collective-permute-start | bytes 3145736 | tf_op jit(solution)/shard_map/ppermute | solution.py:349
  110.1 14.3 %collective-permute-start.18 = (bf16[4,128,512]{2,1,0:T(8,128)(2,1)S(1)}, bf16[4,128,512]{2,1,0:T(8,128)(2,1)S(1)}, u32[]{:S(2)}, u32[]{:S(2)}) collective-permute-start(bf16[4,128,512]{2,1,0:T(8,128)(2,1)S(1)} %fusion), channel_id=1, source_target_pairs={{0,2},{1,3},{2,0},{3,1},{4,6},{5,7},{6,4},{7,5},{8,10},{9,11},{10,... | collective-permute-start | bytes 1572872 | tf_op jit(solution)/shard_map/ppermute | solution.py:349
  124.4 2.7 %collective-permute-start.19 = (f32[4,128,512]{2,1,0:T(8,128)S(1)}, f32[4,128,512]{2,1,0:T(8,128)S(1)}, u32[]{:S(2)}, u32[]{:S(2)}) collective-permute-start(f32[4,128,512]{2,1,0:T(8,128)S(1)} %get-tuple-element.93), channel_id=1, source_target_pairs={{0,1},{1,0},{2,3},{3,2},{4,5},{5,4},{6,7},{7,6},{8,9},{9,8},{10,11... | collective-permute-start | bytes 3145736 | tf_op jit(solution)/shard_map/ppermute | solution.py:349
  127.5 8.3 %collective-permute-start.20 = (bf16[128,512]{1,0:T(8,128)(2,1)S(1)}, bf16[128,512]{1,0:T(8,128)(2,1)S(1)}, u32[]{:S(2)}, u32[]{:S(2)}) collective-permute-start(bf16[128,512]{1,0:T(8,128)(2,1)S(1)} %get-tuple-element.100), channel_id=1, source_target_pairs={{0,12},{1,13},{2,14},{3,15},{4,8},{5,9},{6,10},{7,11},{8,4},{9,5},... | collective-permute-start | bytes 393224 | tf_op jit(solution)/shard_map/ppermute | solution.py:349
  130.2 12.4 %collective-permute-start.21 = (bf16[128,512]{1,0:T(8,128)(2,1)S(1)}, bf16[128,512]{1,0:T(8,128)(2,1)S(1)}, u32[]{:S(2)}, u32[]{:S(2)}) collective-permute-start(bf16[128,512]{1,0:T(8,128)(2,1)S(1)} %get-tuple-element.102), channel_id=1, source_target_pairs={{0,8},{1,9},{2,10},{3,11},{4,12},{5,13},{6,14},{7,15},{8,0},{9,1},... | collective-permute-start | bytes 393224 | tf_op jit(solution)/shard_map/ppermute | solution.py:349
  130.6 11.9 %collective-permute-start.22 = (bf16[128,512]{1,0:T(8,128)(2,1)S(1)}, bf16[128,512]{1,0:T(8,128)(2,1)S(1)}, u32[]{:S(2)}, u32[]{:S(2)}) collective-permute-start(bf16[128,512]{1,0:T(8,128)(2,1)S(1)} %get-tuple-element.101), channel_id=1, source_target_pairs={{0,4},{1,5},{2,6},{3,7},{4,0},{5,1},{6,2},{7,3},{8,12},{9,13},{10,... | collective-permute-start | bytes 393224 | tf_op jit(solution)/shard_map/ppermute | solution.py:349
